TPU v7x, 32 devices: a whole 2x2x4 slice. The times are simulated.
32 devices in a mesh: dp: 16 (over z, y, core), query: 2 (over x).
Axes of the slice: x: 2, y: 2, z: 4, core: 2. Of those that a mesh axis runs over, the one named last changes fastest.
Arguments:
- tokens: bfloat16 [2, 32, 128, 1280], P(None, ('dp', 'query')), may hold values from -6 to 6
- out_cotangent: bfloat16 [2, 32, 128, 1280], P(None, ('dp', 'query')), may hold values from -6 to 6
- qkv_weight: bfloat16 [1280, 3840], P('dp'), may hold values from -0.15625 to 0.15625
- out_weight: bfloat16 [1280, 1280], P('dp'), may hold values from -0.625 to 0.625
- up_weight: bfloat16 [1280, 5120], P('dp'), may hold values from -0.15625 to 0.15625
- down_weight: bfloat16 [5120, 1280], P('dp'), may hold values from -0.078125 to 0.078125
- attn_gain: bfloat16 [1280], P('dp'), may hold values from 0.5 to 1.5
- ffn_gain: bfloat16 [1280], P('dp'), may hold values from 0.5 to 1.5
- up_bias: bfloat16 [5120], P('dp'), may hold values from -3 to 3
- cell_weight: bfloat16 [1280, 5120], P('dp'), may hold values from -0.15625 to 0.15625
- gene_weight: bfloat16 [1280, 5120], P('dp'), may hold values from -0.15625 to 0.15625
- decoder_bias: bfloat16 [5120], P('dp'), may hold values from -3 to 3
- readout: bfloat16 [5120], P('dp'), may hold values from -0.15625 to 0.15625
- gene_embed: bfloat16 [2, 32, 384, 1280], P(None, ('dp', 'query')), may hold values from -6 to 6
- query_cell: int32 [2, 32, 384], P(None, ('dp', 'query')), may hold values from 0 to 1
- query_label: int32 [2, 32, 384], P(None, ('dp', 'query')), may hold values 0 or 1
- query_live: int32 [16, 2, 2], P('dp', None, 'query'), may hold values from 1 to 384, 480 in all within a row
Outputs:
- block_out: bfloat16 [2, 32, 128, 1280], P(None, ('dp', 'query'))
- grad_tokens: float32 [2, 32, 128, 1280], P(None, ('dp', 'query'))
- grad_qkv: float32 [1280, 3840], P('dp')
- grad_out: float32 [1280, 1280], P('dp')
- grad_up: float32 [1280, 5120], P('dp')
- grad_down: float32 [5120, 1280], P('dp')
- grad_attn_gain: float32 [1280], P('dp')
- grad_ffn_gain: float32 [1280], P('dp')
- grad_up_bias: float32 [5120], P('dp')
- grad_cell: float32 [1280, 5120], P('dp')
- grad_gene: float32 [1280, 5120], P('dp')
- grad_decoder_bias: float32 [5120], P('dp')
- grad_readout: float32 [5120], P('dp')
Inputs may be any that keep to these rules, and one draw needn't show every extreme that they name: `query_live`: the 2 devices of one dp index together hold 480 live rows in each micro-batch; a device's live rows are its first slots. `query_cell`: index of a cell within the query group of the row's device.
All inputs are finite; a program needn't handle non-finite values. No bound on the sum of `query_label` on one device may be relied on, other than what follows from the above.
Results may differ from a plain program's by a relative error of at most 0.02.
Values may be sent and summed in bfloat16 or wider, within the bound.
No kernel may reach another device: no remote copies, remote signals or barrier semaphores. Data moves between devices by JAX's collectives and lax.ppermute only.
A program may use at most 320 MiB of HBM per device.

v0:
```python
import jax
import jax.numpy as jnp
from jax import lax
from jax.sharding import PartitionSpec as P

D = 1280
HEADS = 20
HEAD = 64


highest = lax.Precision.HIGHEST
epsilon = 1e-05


def row_product(left, right):
    return lax.dot_general(
        left, right, (((0,), (0,)), ((), ())), preferred_element_type=jnp.float32
    )


def times_transpose(left, right):
    return lax.dot_general(
        left, right, (((1,), (1,)), ((), ())), preferred_element_type=jnp.float32
    )


def layer_stats(values):
    average = jnp.mean(values, axis=-1, keepdims=True)
    centred = values - average
    variance = jnp.mean(centred * centred, axis=-1, keepdims=True)
    inverse = lax.rsqrt(variance + epsilon)
    return (centred * inverse, inverse)


def norm_back(grad_scaled, gain, normal, inverse):
    grad_normal = grad_scaled * gain
    along_normal = jnp.mean(grad_normal * normal, axis=-1, keepdims=True)
    average = jnp.mean(grad_normal, axis=-1, keepdims=True)
    grad_values = inverse * (grad_normal - average - normal * along_normal)
    return (grad_values, jnp.sum(grad_scaled * normal, axis=0))


def encode(inputs, weights):
    qkv_weight, out_weight, up_weight, down_weight, attn_gain, ffn_gain, up_bias = weights
    length = inputs.shape[0]
    tokens_wide = inputs.astype(jnp.float32)
    norm_one, scale_one = layer_stats(tokens_wide)
    normed = (norm_one * attn_gain.astype(jnp.float32)).astype(jnp.bfloat16)
    projected = jnp.dot(normed, qkv_weight, preferred_element_type=jnp.float32).astype(jnp.bfloat16)
    projected = projected.reshape(length, 3, HEADS, HEAD)
    queries = projected[:, 0]
    key_heads = projected[:, 1]
    value_heads = projected[:, 2]
    scores = (
        jnp.einsum("qhd,khd->hqk", queries, key_heads, preferred_element_type=jnp.float32) * 0.125
    )
    row_max = jnp.max(scores, axis=-1, keepdims=True)
    shifted = jnp.exp(scores - row_max)
    row_total = jnp.sum(shifted, axis=-1, keepdims=True)
    attn_probs = (shifted / row_total).astype(jnp.bfloat16)
    logsum = row_max + jnp.log(row_total)
    mixed_heads = jnp.einsum(
        "hqk,khd->qhd", attn_probs, value_heads, preferred_element_type=jnp.float32
    )
    mixed_heads = mixed_heads.astype(jnp.bfloat16).reshape(length, D)
    hidden = tokens_wide + jnp.dot(mixed_heads, out_weight, preferred_element_type=jnp.float32)
    norm_two, scale_two = layer_stats(hidden)
    second = (norm_two * ffn_gain.astype(jnp.float32)).astype(jnp.bfloat16)
    up_proj = jnp.dot(second, up_weight, preferred_element_type=jnp.float32) + up_bias.astype(
        jnp.float32
    )
    active = jax.nn.gelu(up_proj, approximate=True).astype(jnp.bfloat16)
    output = hidden + jnp.dot(active, down_weight, preferred_element_type=jnp.float32)
    saved_state = (
        norm_one,
        scale_one,
        normed,
        queries,
        key_heads,
        value_heads,
        logsum,
        mixed_heads,
        norm_two,
        scale_two,
        second,
        up_proj,
        active,
    )
    return (output, saved_state)


def encode_back(grad_output, saved_state, weights):
    qkv_weight, out_weight, up_weight, down_weight, attn_gain, ffn_gain = weights
    (
        norm_one,
        scale_one,
        normed,
        queries,
        key_heads,
        value_heads,
        logsum,
        mixed_heads,
        norm_two,
        scale_two,
        second,
        up_proj,
        active,
    ) = saved_state
    length = grad_output.shape[0]
    grad_branch = grad_output.astype(jnp.bfloat16)
    grad_down = row_product(active, grad_branch)
    grad_active = times_transpose(grad_branch, down_weight)
    gelu_back = jax.vjp(lambda inner_values: jax.nn.gelu(inner_values, approximate=True), up_proj)[
        1
    ]
    grad_up_proj = gelu_back(grad_active)[0].astype(jnp.bfloat16)
    grad_up = row_product(second, grad_up_proj)
    grad_up_bias = jnp.sum(grad_up_proj.astype(jnp.float32), axis=0)
    grad_second = times_transpose(grad_up_proj, up_weight)
    grad_hidden_norm, grad_ffn_gain = norm_back(
        grad_second, ffn_gain.astype(jnp.float32), norm_two, scale_two
    )
    grad_hidden = grad_output + grad_hidden_norm
    grad_attn = grad_hidden.astype(jnp.bfloat16)
    grad_out = row_product(mixed_heads, grad_attn)
    grad_mixed = (
        times_transpose(grad_attn, out_weight).astype(jnp.bfloat16).reshape(length, HEADS, HEAD)
    )
    scores = (
        jnp.einsum("qhd,khd->hqk", queries, key_heads, preferred_element_type=jnp.float32) * 0.125
    )
    attn_probs = jnp.exp(scores - logsum)
    probs_low = attn_probs.astype(jnp.bfloat16)
    grad_values = jnp.einsum(
        "hqk,qhd->khd", probs_low, grad_mixed, preferred_element_type=jnp.float32
    )
    grad_probs = jnp.einsum(
        "qhd,khd->hqk", grad_mixed, value_heads, preferred_element_type=jnp.float32
    )
    along_probs = jnp.sum(grad_probs * attn_probs, axis=-1, keepdims=True)
    grad_scores = (attn_probs * (grad_probs - along_probs) * 0.125).astype(jnp.bfloat16)
    grad_queries = jnp.einsum(
        "hqk,khd->qhd", grad_scores, key_heads, preferred_element_type=jnp.float32
    )
    grad_keys = jnp.einsum("hqk,qhd->khd", grad_scores, queries, preferred_element_type=jnp.float32)
    grad_projected = (
        jnp.stack([grad_queries, grad_keys, grad_values], axis=1)
        .astype(jnp.bfloat16)
        .reshape(length, 3 * D)
    )
    grad_qkv = row_product(normed, grad_projected)
    grad_normed = times_transpose(grad_projected, qkv_weight)
    grad_input_norm, grad_attn_gain = norm_back(
        grad_normed, attn_gain.astype(jnp.float32), norm_one, scale_one
    )
    grad_input = grad_hidden + grad_input_norm
    return (
        (grad_qkv, grad_out, grad_up, grad_down, grad_attn_gain, grad_ffn_gain, grad_up_bias),
        grad_input,
    )


def decode(summary_all, weights, gene_rows, cell_ids, labels, live_count):
    cell_weight, gene_weight, decoder_bias, readout = weights
    group_size = summary_all.shape[0]
    slot_count = gene_rows.shape[0]
    cell_part = jnp.dot(summary_all, cell_weight, preferred_element_type=jnp.float32)
    onehot = (cell_ids[:, None] == jnp.arange(group_size, dtype=jnp.int32)[None, :]).astype(
        jnp.float32
    )
    picked = jnp.dot(onehot, cell_part, precision=highest)
    pre_act = (
        picked
        + jnp.dot(gene_rows, gene_weight, preferred_element_type=jnp.float32)
        + decoder_bias.astype(jnp.float32)
    )
    activity, silu_back = jax.vjp(jax.nn.silu, pre_act)
    read_wide = readout.astype(jnp.float32)
    logits = jnp.sum(activity * read_wide[None, :], axis=-1)
    live_rows = (jnp.arange(slot_count, dtype=jnp.int32) < live_count).astype(jnp.float32)
    grad_logits = live_rows * (jax.nn.sigmoid(logits) - labels.astype(jnp.float32))
    grad_readout = jnp.sum(grad_logits[:, None] * activity, axis=0)
    grad_pre = silu_back(grad_logits[:, None] * read_wide[None, :])[0].astype(jnp.bfloat16)
    grad_pre_wide = grad_pre.astype(jnp.float32)
    grad_decoder_bias = jnp.sum(grad_pre_wide, axis=0)
    grad_gene = row_product(gene_rows, grad_pre)
    grad_cellproj = lax.dot_general(
        onehot, grad_pre_wide, (((0,), (0,)), ((), ())), precision=highest
    )
    grad_cell = lax.dot_general(
        summary_all.astype(jnp.float32), grad_cellproj, (((0,), (0,)), ((), ())), precision=highest
    )
    grad_summary = lax.dot_general(
        grad_cellproj, cell_weight.astype(jnp.float32), (((1,), (1,)), ((), ())), precision=highest
    )
    return ((grad_cell, grad_gene, grad_decoder_bias, grad_readout), grad_summary)


def shards(
    tokens,
    out_cotangent,
    qkv_weight,
    out_weight,
    up_weight,
    down_weight,
    attn_gain,
    ffn_gain,
    up_bias,
    cell_weight,
    gene_weight,
    decoder_bias,
    readout,
    gene_embed,
    query_cell,
    query_label,
    query_live,
):
    micro_count = tokens.shape[0]
    outputs = []
    input_grads = []
    totals = None
    for micro_index in range(micro_count):
        gathered = (
            lax.all_gather(qkv_weight, "dp", axis=0, tiled=True),
            lax.all_gather(out_weight, "dp", axis=0, tiled=True),
            lax.all_gather(up_weight, "dp", axis=0, tiled=True),
            lax.all_gather(down_weight, "dp", axis=0, tiled=True),
            lax.all_gather(attn_gain, "dp", axis=0, tiled=True),
            lax.all_gather(ffn_gain, "dp", axis=0, tiled=True),
            lax.all_gather(up_bias, "dp", axis=0, tiled=True),
            lax.all_gather(cell_weight, "dp", axis=0, tiled=True),
            lax.all_gather(gene_weight, "dp", axis=0, tiled=True),
            lax.all_gather(decoder_bias, "dp", axis=0, tiled=True),
            lax.all_gather(readout, "dp", axis=0, tiled=True),
        )
        output, saved_state = encode(tokens[micro_index, 0], gathered[:7])
        outputs.append(output.astype(jnp.bfloat16))
        summary_all = lax.all_gather(output[0:1].astype(jnp.bfloat16), "query", axis=0, tiled=True)
        decoder_grads, grad_summary = decode(
            summary_all,
            gathered[7:],
            gene_embed[micro_index, 0],
            query_cell[micro_index, 0],
            query_label[micro_index, 0],
            query_live[0, micro_index, 0],
        )
        grad_own = lax.psum_scatter(
            grad_summary.astype(jnp.bfloat16), "query", scatter_dimension=0, tiled=True
        ).astype(jnp.float32)
        grad_output = out_cotangent[micro_index, 0].astype(jnp.float32)
        grad_output = grad_output.at[0:1].add(grad_own)
        back_weights = (
            lax.all_gather(qkv_weight, "dp", axis=0, tiled=True),
            lax.all_gather(out_weight, "dp", axis=0, tiled=True),
            lax.all_gather(up_weight, "dp", axis=0, tiled=True),
            lax.all_gather(down_weight, "dp", axis=0, tiled=True),
            lax.all_gather(attn_gain, "dp", axis=0, tiled=True),
            lax.all_gather(ffn_gain, "dp", axis=0, tiled=True),
        )
        encoder_grads, grad_input = encode_back(grad_output, saved_state, back_weights)
        input_grads.append(grad_input)
        step_grads = encoder_grads + decoder_grads
        if micro_index == 0:
            totals = tuple(step_grads)
        else:
            totals = tuple((earlier + later for earlier, later in zip(totals, step_grads)))
    owned = (
        lax.psum_scatter(
            totals[0].astype(jnp.bfloat16), "dp", scatter_dimension=0, tiled=True
        ).astype(jnp.float32),
        lax.psum_scatter(
            totals[1].astype(jnp.bfloat16), "dp", scatter_dimension=0, tiled=True
        ).astype(jnp.float32),
        lax.psum_scatter(
            totals[2].astype(jnp.bfloat16), "dp", scatter_dimension=0, tiled=True
        ).astype(jnp.float32),
        lax.psum_scatter(
            totals[3].astype(jnp.bfloat16), "dp", scatter_dimension=0, tiled=True
        ).astype(jnp.float32),
        lax.psum_scatter(
            totals[4].astype(jnp.bfloat16), "dp", scatter_dimension=0, tiled=True
        ).astype(jnp.float32),
        lax.psum_scatter(
            totals[5].astype(jnp.bfloat16), "dp", scatter_dimension=0, tiled=True
        ).astype(jnp.float32),
        lax.psum_scatter(
            totals[6].astype(jnp.bfloat16), "dp", scatter_dimension=0, tiled=True
        ).astype(jnp.float32),
        lax.psum_scatter(
            totals[7].astype(jnp.bfloat16), "dp", scatter_dimension=0, tiled=True
        ).astype(jnp.float32),
        lax.psum_scatter(
            totals[8].astype(jnp.bfloat16), "dp", scatter_dimension=0, tiled=True
        ).astype(jnp.float32),
        lax.psum_scatter(
            totals[9].astype(jnp.bfloat16), "dp", scatter_dimension=0, tiled=True
        ).astype(jnp.float32),
        lax.psum_scatter(
            totals[10].astype(jnp.bfloat16), "dp", scatter_dimension=0, tiled=True
        ).astype(jnp.float32),
    )
    totals = (
        lax.psum(owned[0].astype(jnp.bfloat16), "query").astype(jnp.float32),
        lax.psum(owned[1].astype(jnp.bfloat16), "query").astype(jnp.float32),
        lax.psum(owned[2].astype(jnp.bfloat16), "query").astype(jnp.float32),
        lax.psum(owned[3].astype(jnp.bfloat16), "query").astype(jnp.float32),
        lax.psum(owned[4].astype(jnp.bfloat16), "query").astype(jnp.float32),
        lax.psum(owned[5].astype(jnp.bfloat16), "query").astype(jnp.float32),
        lax.psum(owned[6].astype(jnp.bfloat16), "query").astype(jnp.float32),
        lax.psum(owned[7].astype(jnp.bfloat16), "query").astype(jnp.float32),
        lax.psum(owned[8].astype(jnp.bfloat16), "query").astype(jnp.float32),
        lax.psum(owned[9].astype(jnp.bfloat16), "query").astype(jnp.float32),
        lax.psum(owned[10].astype(jnp.bfloat16), "query").astype(jnp.float32),
    )
    block_out = jnp.stack(outputs, axis=0)[:, None]
    grad_tokens = jnp.stack(input_grads, axis=0)[:, None]
    return (
        block_out,
        grad_tokens,
        totals[0],
        totals[1],
        totals[2],
        totals[3],
        totals[4],
        totals[5],
        totals[6],
        totals[7],
        totals[8],
        totals[9],
        totals[10],
    )


def solution(mesh):
    placed = (
        P(None, ("dp", "query"), None, None),
        P(None, ("dp", "query"), None, None),
        P("dp", None),
        P("dp", None),
        P("dp", None),
        P("dp", None),
        P("dp"),
        P("dp"),
        P("dp"),
        P("dp", None),
        P("dp", None),
        P("dp"),
        P("dp"),
        P(None, ("dp", "query"), None, None),
        P(None, ("dp", "query"), None),
        P(None, ("dp", "query"), None),
        P("dp", None, "query"),
    )
    return jax.shard_map(
        shards,
        mesh=mesh,
        in_specs=placed,
        out_specs=(
            P(None, ("dp", "query"), None, None),
            P(None, ("dp", "query"), None, None),
            P("dp", None),
            P("dp", None),
            P("dp", None),
            P("dp", None),
            P("dp"),
            P("dp"),
            P("dp"),
            P("dp", None),
            P("dp", None),
            P("dp"),
            P("dp"),
        ),
        check_vma=False,
    )
```

profile of v0, /device:TPU:0, one launch (start us, length us, event | category | flops | bytes accessed | tf_op | source)
XLA Modules:
  0.0 1549.1 jit_solution(1948422574728645002)
XLA Ops:
  14.5 65.3 %all-reduce.13 = (bf16[1280]{0:T(1024)(128)(2,1)S(1)}, bf16[5120]{0:T(1024)(128)(2,1)S(1)}, bf16[1280]{0:T(1024)(128)(2,1)S(1)}, bf16[5120]{0:T(1024)(128)(2,1)S(1)}, bf16[5120]{0:T(1024)(128)(2,1)S(1)}) all-reduce(bf16[1280]{0:T(1024)(128)(2,1)S(1)} %dynamic-update-slice.6, ...), channel_id=1, replica_groups=mesh['dp'=16,'query'=2] {'dp'}, use_global_device_ids=true, to_apply=%add | all-reduce | flops 17920 | bytes 71680
  81.0 16.6 %all-gather.9.cloned.1.call-done = bf16[1280,3840]{1,0:T(8,128)(2,1)} async-done(((bf16[80,3840]{1,0:T(8,128)(2,1)}), bf16[1280,3840]{1,0:T(8,128)(2,1)}) %all-gather.9.cloned.1.call-update) | async-done | bytes 9830416 | tf_op jit(solution)/shard_map/all_gather | solution.py:224
  97.6 5.3 convolution_convert_fusion
  103.7 5.9 convolution_convert_fusion.1
  112.9 31.2 %all-gather.11.cloned.1.call-done = bf16[1280,1280]{1,0:T(8,128)(2,1)} async-done(((bf16[80,1280]{1,0:T(8,128)(2,1)}), bf16[1280,1280]{1,0:T(8,128)(2,1)}) %all-gather.11.cloned.1.call-update) | async-done | bytes 3276816 | tf_op jit(solution)/shard_map/all_gather | solution.py:225
  151.0 98.3 %all-gather.13.cloned.1.call-done = bf16[1280,5120]{1,0:T(8,128)(2,1)} async-done(((bf16[80,5120]{1,0:T(8,128)(2,1)}), bf16[1280,5120]{1,0:T(8,128)(2,1)}) %all-gather.13.cloned.1.call-update) | async-done | bytes 13107216 | tf_op jit(solution)/shard_map/all_gather | solution.py:226
  249.3 8.2 convolution_add_fusion.1
  257.5 96.1 %all-gather.15.cloned.1.call-done = bf16[5120,1280]{1,0:T(8,128)(2,1)} async-done(((bf16[320,1280]{1,0:T(8,128)(2,1)}), bf16[5120,1280]{1,0:T(8,128)(2,1)}) %all-gather.15.cloned.1.call-update) | async-done | bytes 13107216 | tf_op jit(solution)/shard_map/all_gather | solution.py:227
  353.6 8.0 fusion.27
  361.6 16.8 %all-gather.1 = bf16[2,1,1280]{2,1,0:T(2,128)(2,1)S(1)} all-gather(bf16[1,1,1280]{2,1,0:T(2,128)(2,1)S(1)} %slice_bitcast_fusion.18), channel_id=1, replica_groups=mesh['dp'=16,'query'=2] {'query'}, dimensions={0}, use_global_device_ids=true | all-gather | bytes 7680 | tf_op jit(solution)/shard_map/all_gather | solution.py:238
  383.0 4.4 all-gather
  387.3 70.6 %all-gather.17.cloned.1.call-done = bf16[1280,5120]{1,0:T(8,128)(2,1)} async-done(((bf16[80,5120]{1,0:T(8,128)(2,1)}), bf16[1280,5120]{1,0:T(8,128)(2,1)}) %all-gather.17.cloned.1.call-update) | async-done | bytes 13107216 | tf_op jit(solution)/shard_map/all_gather | solution.py:231
  457.9 6.5 fusion.165
  464.5 97.8 %all-gather.19.cloned.1.call-done = bf16[1280,5120]{1,0:T(8,128)(2,1)} async-done(((bf16[80,5120]{1,0:T(8,128)(2,1)}), bf16[1280,5120]{1,0:T(8,128)(2,1)}) %all-gather.19.cloned.1.call-update) | async-done | bytes 13107216 | tf_op jit(solution)/shard_map/all_gather | solution.py:232
  562.3 10.5 fusion.49
  572.8 6.2 add_add_fusion
  579.1 12.7 fusion.53
  593.6 9.9 multiply_reduce_fusion.3
  604.8 11.1 convert_reduce_fusion.1
  615.9 12.7 fusion.51
  628.6 16.2 %fusion.2 = bf16[1280,5120]{0,1:T(8,128)(2,1)} fusion(f32[5120,1280]{1,0:T(8,128)} %fusion.51, bf16[384,5120]{1,0:T(8,128)(2,1)} %get-tuple-element.137, bf16[2,1,384,1280]{3,2,1,0:T(8,128)(2,1)} %param.34), kind=kOutput, calls=%fused_computation.7 | convolution fusion | flops 5046272000 | bytes 44236800 | tf_op jit(solution)/shard_map/dot_general | solution.py:16
  644.8 17.6 %copy.89 = bf16[1280,5120]{1,0:T(8,128)(2,1)} copy(bf16[1280,5120]{0,1:T(8,128)(2,1)} %fusion.2) | data formatting | bytes 26214400
  670.4 14.1 convolution_convert_fusion.5
  684.5 13.5 convolution_convert_fusion.4
  698.0 8.3 all-reduce.15
  709.0 11.2 convert_reduce_fusion.3
  720.1 10.6 multiply_reduce_fusion.7
  730.8 9.7 convert_reduce_fusion.2
  740.6 10.3 multiply_reduce_fusion.6
  771.7 3.2 convolution_bitcast_fusion.4
  777.3 3.1 convolution_bitcast_fusion.2
  786.2 8.3 fusion.116
  794.5 11.1 add_convert_fusion.4
  806.7 12.7 fusion.185
  819.5 15.7 %add_convert_fusion.3 = bf16[1280,5120]{1,0:T(8,128)(2,1)} fusion(f32[1280,5120]{1,0:T(8,128)} %fusion.185, bf16[128,5120]{1,0:T(8,128)(2,1)} %copy-done.26, f32[128,1280]{1,0:T(8,128)S(1)} %copy-done.6, f32[128]{0:T(128)S(1)} %copy-done.75, f32[128]{0:T(128)S(1)} %copy-done.70, f32[1280]{0:T(1024)S(1)} %convert_element_type.331), kind=kOutput, calls=%fused_computation.5 | convolution fusion | flops 1691484160 | bytes 41293824 | tf_op jit(solution)/shard_map/dot_general | solution.py:16
  836.3 12.8 fusion.146
  849.1 16.3 %add_convert_fusion.2 = bf16[5120,1280]{1,0:T(8,128)(2,1)} fusion(f32[5120,1280]{1,0:T(8,128)} %fusion.146, f32[128,1280]{1,0:T(8,128)S(1)} %copy-done.22, f32[128,5120]{1,0:T(8,128)} %convolution_add_fusion.1), kind=kOutput, calls=%fused_computation.4 | convolution fusion | flops 1696890880 | bytes 42598400 | tf_op jit(solution)/shard_map/dot_general | solution.py:16
  866.1 13.9 fusion.167
  880.0 19.7 %add_convert_fusion.1 = bf16[1280,5120]{1,0:T(8,128)(2,1)} fusion(f32[1280,5120]{1,0:T(8,128)} %fusion.167, f32[2,5120]{1,0:T(2,128)S(1)} %fusion.134, bf16[2,1,1280]{2,1,0:T(2,128)(2,1)S(1)} %copy-done.61), kind=kOutput, calls=%fused_computation.3 | convolution fusion | flops 170393600 | bytes 39367680 | tf_op jit(solution)/shard_map/dot_general | solution.py:190
  903.5 83.4 %reduce-scatter.9.cloned.1.call-done = bf16[80,3840]{1,0:T(8,128)(2,1)} async-done(((bf16[1280,3840]{1,0:T(8,128)(2,1)}), bf16[80,3840]{1,0:T(8,128)(2,1)}) %reduce-scatter.9.cloned.1.call-update) | async-done | bytes 614416 | tf_op jit(solution)/shard_map/reduce_scatter | solution.py:268
  986.9 142.2 %reduce-scatter.13.cloned.1.call-done = bf16[80,5120]{1,0:T(8,128)(2,1)} async-done(((bf16[1280,5120]{1,0:T(8,128)(2,1)}), bf16[80,5120]{1,0:T(8,128)(2,1)}) %reduce-scatter.13.cloned.1.call-update) | async-done | bytes 819216 | tf_op jit(solution)/shard_map/reduce_scatter | solution.py:274
  1129.0 142.2 %reduce-scatter.15.cloned.1.call-done = bf16[320,1280]{1,0:T(8,128)(2,1)} async-done(((bf16[5120,1280]{1,0:T(8,128)(2,1)}), bf16[320,1280]{1,0:T(8,128)(2,1)}) %reduce-scatter.15.cloned.1.call-update) | async-done | bytes 819216 | tf_op jit(solution)/shard_map/reduce_scatter | solution.py:277
  1271.2 141.5 %reduce-scatter.17.cloned.1.call-done = bf16[80,5120]{1,0:T(8,128)(2,1)} async-done(((bf16[1280,5120]{1,0:T(8,128)(2,1)}), bf16[80,5120]{1,0:T(8,128)(2,1)}) %reduce-scatter.17.cloned.1.call-update) | async-done | bytes 819216 | tf_op jit(solution)/shard_map/reduce_scatter | solution.py:289
  1412.7 7.2 fusion.194
  1420.0 8.4 fusion.81
  1428.6 59.6 %all-reduce.12 = (bf16[1280]{0:T(1024)(128)(2,1)S(1)}, bf16[1280]{0:T(1024)(128)(2,1)S(1)}, bf16[5120]{0:T(1024)(128)(2,1)S(1)}, bf16[5120]{0:T(1024)(128)(2,1)S(1)}, bf16[5120]{0:T(1024)(128)(2,1)S(1)}) all-reduce(bf16[1280]{0:T(1024)(128)(2,1)S(1)} %add_convert_fusion.9, ...), channel_id=8, replica_groups=mesh['dp'=16,'query'=2] {'dp'}, use_global_device_ids=true, to_apply=%region_36.37.clone | all-reduce | flops 17920 | bytes 71680
  1488.6 5.0 all-reduce.14
  1500.0 33.9 %all-reduce.19.cloned.1.call-done = (bf16[80,5120]{0,1:T(8,128)(2,1)}, bf16[80,3840]{1,0:T(8,128)(2,1)}, bf16[80,1280]{1,0:T(8,128)(2,1)}, bf16[80,5120]{1,0:T(8...) async-done(((bf16[80,5120]{0,1:T(8,128)(2,1)}, bf16[80,3840]{1,0:T(8,128)(2,1)}, bf16[80,1280]{1,0:T(8,128)(2,1)}, bf16[80,5120]{1,0:T(8,128)(2,1)}, ...) | async-done | bytes 4096016 | tf_op jit(solution)/shard_map/psum | solution.py:311
  (335 shorter events, 85.2 us)
Async XLA Ops:
  7.2 72.5 %copy-start.85 = (s32[1,2,1]{1,2,0:T(1,128)S(1)}, s32[1,2,1]{1,2,0:T(1,128)}, u32[]{:S(2)}) copy-start(s32[1,2,1]{1,2,0:T(1,128)} %param.37) | copy-start | bytes 28
  7.3 73.1 %copy-start.82 = (s32[2,1,384]{2,1,0:T(1,128)S(1)}, s32[2,1,384]{2,1,0:T(1,128)}, u32[]{:S(2)}) copy-start(s32[2,1,384]{2,1,0:T(1,128)} %param.35) | copy-start | bytes 9220
  7.3 73.1 %copy-start.83 = (s32[2,1,384]{2,1,0:T(1,128)S(1)}, s32[2,1,384]{2,1,0:T(1,128)}, u32[]{:S(2)}) copy-start(s32[2,1,384]{2,1,0:T(1,128)} %param.36) | copy-start | bytes 9220
  7.3 73.2 %copy-start.7 = (bf16[2,1,128,1280]{3,2,1,0:T(8,128)(2,1)S(1)}, bf16[2,1,128,1280]{3,2,1,0:T(8,128)(2,1)}, u32[]{:S(2)}) copy-start(bf16[2,1,128,1280]{3,2,1,0:T(8,128)(2,1)} %param.21) | copy-start | bytes 1966084
  7.3 90.3 %all-gather.9.cloned.1.call-start = ((), (), s32[]{:S(2)}) async-start(), calls=%async_computation.6 | async-start | bytes 10444800 | tf_op jit(solution)/shard_map/all_gather | solution.py:224
  8.0 136.1 %all-gather.11.cloned.1.call-start = ((), (), s32[]{:S(2)}) async-start(), calls=%async_computation.7 | async-start | bytes 3481600 | tf_op jit(solution)/shard_map/all_gather | solution.py:225
  8.8 240.5 %all-gather.13.cloned.1.call-start = ((), (), s32[]{:S(2)}) async-start(), calls=%async_computation.8 | async-start | bytes 13926400 | tf_op jit(solution)/shard_map/all_gather | solution.py:226
  9.5 344.1 %all-gather.15.cloned.1.call-start = ((), (), s32[]{:S(2)}) async-start(), calls=%async_computation.9 | async-start | bytes 13926400 | tf_op jit(solution)/shard_map/all_gather | solution.py:227
  10.1 447.9 %all-gather.17.cloned.1.call-start = ((), (), s32[]{:S(2)}) async-start(), calls=%async_computation.10 | async-start | bytes 13926400 | tf_op jit(solution)/shard_map/all_gather | solution.py:231
  10.7 551.6 %all-gather.19.cloned.1.call-start = ((), (), s32[]{:S(2)}) async-start(), calls=%async_computation.11 | async-start | bytes 13926400 | tf_op jit(solution)/shard_map/all_gather | solution.py:232
  11.2 889.9 %reduce-scatter.19.cloned.1.call-start = ((), (), s32[]{:S(2)}) async-start(), calls=%async_computation.17 | async-start | bytes 13926400
  79.8 23.9 %copy-start.43 = (f32[1280]{0:T(1024)}, f32[1280]{0:T(1024)S(1)}, u32[]{:S(2)}) copy-start(f32[1280]{0:T(1024)S(1)} %convert_element_type.325) | copy-start | bytes 15364
  80.6 22.3 %copy-start.76 = (f32[128]{0:T(128)}, f32[128]{0:T(128)S(1)}, u32[]{:S(2)}) copy-start(f32[128]{0:T(128)S(1)} %get-tuple-element.159) | copy-start | bytes 1540
  80.6 23.0 %copy-start.71 = (f32[128]{0:T(128)}, f32[128]{0:T(128)S(1)}, u32[]{:S(2)}) copy-start(f32[128]{0:T(128)S(1)} %get-tuple-element.160) | copy-start | bytes 1540
  81.0 22.0 %copy-start.80 = (f32[128]{0:T(128)}, f32[128]{0:T(128)S(1)}, u32[]{:S(2)}) copy-start(f32[128]{0:T(128)S(1)} %add_rsqrt_fusion.1) | copy-start | bytes 1540
  81.0 22.6 %copy-start.78 = (f32[128]{0:T(128)}, f32[128]{0:T(128)S(1)}, u32[]{:S(2)}) copy-start(f32[128]{0:T(128)S(1)} %add_rsqrt_fusion.3) | copy-start | bytes 1540
  112.9 34.1 %copy-start.38 = (bf16[20,64,128]{2,1,0:T(8,128)(2,1)}, bf16[20,64,128]{2,1,0:T(8,128)(2,1)S(1)}, u32[]{:S(2)}) copy-start(bf16[20,64,128]{2,1,0:T(8,128)(2,1)S(1)} %convolution_convert_fusion.6) | copy-start | bytes 983044
  146.8 605.2 %copy-start.5 = (f32[128,1280]{1,0:T(8,128)}, f32[128,1280]{1,0:T(8,128)S(1)}, u32[]{:S(2)}) copy-start(f32[128,1280]{1,0:T(8,128)S(1)} %get-tuple-element.146) | copy-start | bytes 1966084
  146.8 102.5 %copy-start.69 = (f32[128]{0:T(128)}, f32[128]{0:T(128)S(1)}, u32[]{:S(2)}) copy-start(f32[128]{0:T(128)S(1)} %broadcast_multiply_fusion.8) | copy-start | bytes 1540
  150.7 589.8 %copy-start.9 = (f32[128,1280]{1,0:T(8,128)}, f32[128,1280]{1,0:T(8,128)S(1)}, u32[]{:S(2)}) copy-start(f32[128,1280]{1,0:T(8,128)S(1)} %get-tuple-element.150) | copy-start | bytes 1966084
  151.0 106.5 %copy-start.74 = (f32[128]{0:T(128)}, f32[128]{0:T(128)S(1)}, u32[]{:S(2)}) copy-start(f32[128]{0:T(128)S(1)} %add_rsqrt_fusion) | copy-start | bytes 1540
  353.6 24.9 %copy-start = (bf16[1280,5120]{1,0:T(8,128)(2,1)S(1)}, bf16[1280,5120]{1,0:T(8,128)(2,1)}, u32[]{:S(2)}) copy-start(bf16[1280,5120]{1,0:T(8,128)(2,1)} %all-gather.13.cloned.1.call-done) | copy-start | bytes 39321604
  353.6 26.9 %slice-start.4 = ((s8[13107200]{0:T(1024)(128)(4,1)}), s8[4194304]{0:T(1024)(128)(4,1)S(1)}, s32[]{:S(2)}) async-start(s8[13107200]{0:T(1024)(128)(4,1)} %bitcast.277), calls=%async_computation.23 | async-start | bytes 8388608
  353.6 26.9 %slice-start.5 = ((s8[13107200]{0:T(1024)(128)(4,1)}), s8[4194304]{0:T(1024)(128)(4,1)S(1)}, s32[]{:S(2)}) async-start(s8[13107200]{0:T(1024)(128)(4,1)} %bitcast.277), calls=%async_computation.24 | async-start | bytes 8388608
  353.6 26.9 %slice-start.6 = ((s8[13107200]{0:T(1024)(128)(4,1)}), s8[4194304]{0:T(1024)(128)(4,1)S(1)}, s32[]{:S(2)}) async-start(s8[13107200]{0:T(1024)(128)(4,1)} %bitcast.277), calls=%async_computation.25 | async-start | bytes 8388608
  361.6 18.9 %copy-start.45 = (bf16[128,1280]{1,0:T(8,128)(2,1)}, bf16[128,1280]{1,0:T(8,128)(2,1)S(1)}, u32[]{:S(2)}) copy-start(bf16[128,1280]{1,0:T(8,128)(2,1)S(1)} %fusion.27) | copy-start | bytes 983044
  378.5 79.5 %copy-start.60 = (bf16[2,1,1280]{2,1,0:T(2,128)(2,1)}, bf16[2,1,1280]{2,1,0:T(2,128)(2,1)S(1)}, u32[]{:S(2)}) copy-start(bf16[2,1,1280]{2,1,0:T(2,128)(2,1)S(1)} %all-gather.1) | copy-start | bytes 15364
  382.9 81.5 %copy-start.47 = (bf16[128,1280]{1,0:T(8,128)(2,1)}, bf16[128,1280]{1,0:T(8,128)(2,1)S(1)}, u32[]{:S(2)}) copy-start(bf16[128,1280]{1,0:T(8,128)(2,1)S(1)} %fusion.26) | copy-start | bytes 983044
  387.3 204.4 %copy-start.62 = (bf16[2,1,1280]{2,1,0:T(2,128)(2,1)}, bf16[2,1,1280]{2,1,0:T(2,128)(2,1)S(1)}, u32[]{:S(2)}) copy-start(bf16[2,1,1280]{2,1,0:T(2,128)(2,1)S(1)} %all-gather) | copy-start | bytes 15364
  572.8 18.9 %slice-start = ((s8[13107200]{0:T(1024)(128)(4,1)}), s8[4194304]{0:T(1024)(128)(4,1)S(1)}, s32[]{:S(2)}) async-start(s8[13107200]{0:T(1024)(128)(4,1)} %bitcast.251), calls=%async_computation.19 | async-start | bytes 8388608
  572.8 18.9 %slice-start.1 = ((s8[13107200]{0:T(1024)(128)(4,1)}), s8[4194304]{0:T(1024)(128)(4,1)S(1)}, s32[]{:S(2)}) async-start(s8[13107200]{0:T(1024)(128)(4,1)} %bitcast.251), calls=%async_computation.20 | async-start | bytes 8388608
  579.1 12.7 slice-start.2
  615.9 12.7 copy-start.4
  662.5 241.1 %reduce-scatter.11.cloned.1.call-start = ((), (), s32[]{:S(2)}) async-start(), calls=%async_computation.13 | async-start | bytes 3481600 | tf_op jit(solution)/shard_map/reduce_scatter | solution.py:271
  707.9 44.0 %copy-start.21 = (f32[128,1280]{1,0:T(8,128)}, f32[128,1280]{1,0:T(8,128)S(1)}, u32[]{:S(2)}) copy-start(f32[128,1280]{1,0:T(8,128)S(1)} %scatter-add.9) | copy-start | bytes 1966084
  709.0 31.6 %copy-start.23 = (f32[128,1280]{1,0:T(8,128)}, f32[128,1280]{1,0:T(8,128)S(1)}, u32[]{:S(2)}) copy-start(f32[128,1280]{1,0:T(8,128)S(1)} %scatter-add.6) | copy-start | bytes 1966084
  755.8 231.0 %reduce-scatter.9.cloned.1.call-start = ((), (), s32[]{:S(2)}) async-start(), calls=%async_computation.12 | async-start | bytes 10444800 | tf_op jit(solution)/shard_map/reduce_scatter | solution.py:268
  805.7 13.8 copy-start.6
  805.7 323.4 %reduce-scatter.13.cloned.1.call-start = ((), (), s32[]{:S(2)}) async-start(), calls=%async_computation.14 | async-start | bytes 13926400 | tf_op jit(solution)/shard_map/reduce_scatter | solution.py:274
  835.2 13.9 copy-start.22
  835.2 436.0 %reduce-scatter.15.cloned.1.call-start = ((), (), s32[]{:S(2)}) async-start(), calls=%async_computation.15 | async-start | bytes 13926400 | tf_op jit(solution)/shard_map/reduce_scatter | solution.py:277
  865.4 14.6 copy-start.61
  865.4 547.3 %reduce-scatter.17.cloned.1.call-start = ((), (), s32[]{:S(2)}) async-start(), calls=%async_computation.16 | async-start | bytes 13926400 | tf_op jit(solution)/shard_map/reduce_scatter | solution.py:289
  899.8 634.1 %all-reduce.19.cloned.1.call-start = ((), (), s32[]{:S(2)}) async-start(), calls=%async_computation.18 | async-start | bytes 9175040 | tf_op jit(solution)/shard_map/psum | solution.py:311
  1420.0 76.3 %copy-start.46 = (bf16[128,1280]{1,0:T(8,128)(2,1)S(1)}, bf16[128,1280]{1,0:T(8,128)(2,1)}, u32[]{:S(2)}) copy-start(bf16[128,1280]{1,0:T(8,128)(2,1)} %copy-done.45) | copy-start | bytes 983044
  1420.0 76.3 %copy-start.48 = (bf16[128,1280]{1,0:T(8,128)(2,1)S(1)}, bf16[128,1280]{1,0:T(8,128)(2,1)}, u32[]{:S(2)}) copy-start(bf16[128,1280]{1,0:T(8,128)(2,1)} %copy-done.47) | copy-start | bytes 983044
  1420.0 77.2 %copy-start.18 = (f32[128,1280]{1,0:T(8,128)S(1)}, f32[128,1280]{1,0:T(8,128)}, u32[]{:S(2)}) copy-start(f32[128,1280]{1,0:T(8,128)} %copy-done.17) | copy-start | bytes 1966084
  1420.0 77.2 %copy-start.20 = (f32[128,1280]{1,0:T(8,128)S(1)}, f32[128,1280]{1,0:T(8,128)}, u32[]{:S(2)}) copy-start(f32[128,1280]{1,0:T(8,128)} %copy-done.19) | copy-start | bytes 1966084
  (65 other events, 299.6 us)
Sparse Core Ops, SparseCore 0:
  10.4 87.1 all-gather.8
  99.9 44.1 all-gather.10
  146.4 102.8 all-gather.12
  251.4 102.1 all-gather.14
  355.7 102.1 all-gather.16
  460.1 102.1 all-gather.18
  662.6 136.5 reduce-scatter.18
  803.4 65.9 reduce-scatter.10
  873.6 113.1 reduce-scatter.8
  990.8 138.1 reduce-scatter.12
  1133.7 137.4 reduce-scatter.14
  1275.2 137.4 reduce-scatter.16
  1416.5 117.2 all-reduce.18
where the time goes:
time: 1560 us; the launch traced here: 1550 us
  waiting for transfers between devices  957 us (61%)
  matrix products  339 us (22%)
  blocking collectives  159 us (10%)
  local copies, waits for them, and re-layouts  41 us (3%)
  other arithmetic  33.2 us (2%)
  between operations  18 us (1%)
    reduce_scatter x1, waiting for transfers between devices, shards(): lax.psum_scatter(totals[2].astype(jnp.bfloat16), 'dp', scatter_dimension=...  142 us
    reduce_scatter x1, waiting for transfers between devices, shards(): lax.psum_scatter(totals[3].astype(jnp.bfloat16), 'dp', scatter_dimension=...  142 us
    reduce_scatter x1, waiting for transfers between devices, shards(): lax.psum_scatter(totals[7].astype(jnp.bfloat16), 'dp', scatter_dimension=...  141 us
    unnamed x3, blocking collectives  133 us
    dot_general x10, matrix products, row_product(): lax.dot_general(left, right, (((0,), (0,)), ((), ())), preferred_element_...  110 us
    all_gather x1, waiting for transfers between devices, shards(): lax.all_gather(up_weight, 'dp', axis=0, tiled=True)  98.3 us
    all_gather x1, waiting for transfers between devices, shards(): lax.all_gather(gene_weight, 'dp', axis=0, tiled=True)  97.8 us
    all_gather x1, waiting for transfers between devices, shards(): lax.all_gather(down_weight, 'dp', axis=0, tiled=True)  96.1 us
  transfers between devices with their start and end apart: 13, of which 11 were waited for; matrix products, arithmetic and copies ran while one was open for 19% of the time, Pallas kernels for 0%

commit v1 on v0

v1 whole, which is shorter than its diff:
```python
import functools

import jax
import jax.numpy as jnp
from jax import lax
from jax.experimental import pallas as pl
from jax.experimental.pallas import tpu as pltpu
from jax.sharding import PartitionSpec as P

HEAD = 64
EPSILON = 1e-05
F32 = jnp.float32
BF16 = jnp.bfloat16


def product(left, right):
    return jnp.dot(left, right, preferred_element_type=F32)


def row_product(left, right):
    return lax.dot_general(left, right, (((0,), (0,)), ((), ())), preferred_element_type=F32)


def times_transpose(left, right):
    return lax.dot_general(left, right, (((1,), (1,)), ((), ())), preferred_element_type=F32)


def layer_stats(values):
    average = jnp.mean(values, axis=-1, keepdims=True)
    centred = values - average
    variance = jnp.mean(centred * centred, axis=-1, keepdims=True)
    inverse = lax.rsqrt(variance + EPSILON)
    return (centred * inverse, inverse)


def norm_back(grad_scaled, gain, normal, inverse):
    grad_normal = grad_scaled * gain
    along_normal = jnp.mean(grad_normal * normal, axis=-1, keepdims=True)
    average = jnp.mean(grad_normal, axis=-1, keepdims=True)
    grad_values = inverse * (grad_normal - average - normal * along_normal)
    return (grad_values, jnp.sum(grad_scaled * normal, axis=0))


def softmax_of(queries, keys):
    scores = times_transpose(queries, keys) * 0.125
    row_max = jnp.max(scores, axis=-1, keepdims=True)
    shifted = jnp.exp(scores - row_max)
    return shifted / jnp.sum(shifted, axis=-1, keepdims=True)


def attend_kernel(projected_ref, mixed_ref):
    width = mixed_ref.shape[1]
    for start in range(0, width, HEAD):
        queries = projected_ref[:, start : start + HEAD]
        keys = projected_ref[:, width + start : width + start + HEAD]
        values = projected_ref[:, 2 * width + start : 2 * width + start + HEAD]
        probs = softmax_of(queries, keys).astype(BF16)
        mixed_ref[:, start : start + HEAD] = product(probs, values).astype(BF16)


def attend_back_kernel(projected_ref, grad_mixed_ref, first_ref, grad_ref):
    width = grad_mixed_ref.shape[1]
    is_first = lax.broadcasted_iota(jnp.int32, (grad_mixed_ref.shape[0], HEAD), 0) == 0
    for start in range(0, width, HEAD):
        queries = projected_ref[:, start : start + HEAD]
        keys = projected_ref[:, width + start : width + start + HEAD]
        values = projected_ref[:, 2 * width + start : 2 * width + start + HEAD]
        grad_mixed = jnp.where(
            is_first, first_ref[0, :, start : start + HEAD], grad_mixed_ref[:, start : start + HEAD]
        )
        probs = softmax_of(queries, keys)
        grad_values = row_product(probs.astype(BF16), grad_mixed)
        grad_probs = times_transpose(grad_mixed, values)
        along = jnp.sum(grad_probs * probs, axis=-1, keepdims=True)
        grad_scores = (probs * (grad_probs - along) * 0.125).astype(BF16)
        grad_queries = product(grad_scores, keys)
        grad_keys = row_product(grad_scores, queries)
        grad_ref[:, start : start + HEAD] = grad_queries.astype(BF16)
        grad_ref[:, width + start : width + start + HEAD] = grad_keys.astype(BF16)
        grad_ref[:, 2 * width + start : 2 * width + start + HEAD] = grad_values.astype(BF16)


def attend(projected, length, first, count):
    rows, wide = count * length, projected.shape[1]
    return pl.pallas_call(
        attend_kernel,
        grid=(count,),
        in_specs=[pl.BlockSpec((length, wide), lambda i: (first + i, 0))],
        out_specs=pl.BlockSpec((length, wide // 3), lambda i: (i, 0)),
        out_shape=jax.ShapeDtypeStruct((rows, wide // 3), BF16),
        cost_estimate=pl.CostEstimate(
            flops=4 * rows * length * wide // 3,
            bytes_accessed=rows * wide * 3,
            transcendentals=rows * length * wide // 3 // HEAD,
        ),
    )(projected)


def attend_back(projected, grad_mixed, first, length):
    rows, wide = projected.shape
    return pl.pallas_call(
        attend_back_kernel,
        grid=(rows // length,),
        in_specs=[
            pl.BlockSpec((length, wide), lambda i: (i, 0)),
            pl.BlockSpec((length, wide // 3), lambda i: (i, 0)),
            pl.BlockSpec((1, 1, wide // 3), lambda i: (i, 0, 0)),
        ],
        out_specs=pl.BlockSpec((length, wide), lambda i: (i, 0)),
        out_shape=jax.ShapeDtypeStruct((rows, wide), BF16),
        cost_estimate=pl.CostEstimate(
            flops=10 * rows * length * wide // 3,
            bytes_accessed=rows * wide * 5,
            transcendentals=rows * length * wide // 3 // HEAD,
        ),
    )(projected, grad_mixed, first)


def ring_chip(position, chips):
    position = lax.rem(position + 2 * chips, chips)
    return jnp.where(position < chips // 2, 2 * position, 2 * (chips - 1 - position) + 1)


def place_kernel(segments, position_ref, *refs):
    count = (len(refs) - len(segments)) // 2
    outs = refs[2 * count :]
    for step in range(count):
        for side in range(2):
            piece = refs[2 * step + side]
            source = ring_chip(position_ref[0] + (step if side else -step), count)
            begin = 0
            for out, rows in zip(outs, segments):
                start = pl.multiple_of((2 * source + side) * rows, rows)
                out[pl.ds(start, rows), :] = piece[pl.ds(begin, rows), :]
                begin += rows


def place(pieces, position, segments):
    tall, wide = pieces[0].shape
    whole = pl.BlockSpec(memory_space=pltpu.VMEM)
    return pl.pallas_call(
        functools.partial(place_kernel, segments),
        in_specs=[pl.BlockSpec(memory_space=pltpu.SMEM)] + [whole] * len(pieces),
        out_specs=[whole] * len(segments),
        out_shape=[jax.ShapeDtypeStruct((len(pieces) * rows, wide), BF16) for rows in segments],
        cost_estimate=pl.CostEstimate(
            flops=0, bytes_accessed=4 * len(pieces) * tall * wide, transcendentals=0
        ),
        compiler_params=pltpu.CompilerParams(vmem_limit_bytes=32 << 20),
    )(position.reshape(1), *pieces)


def column_places(kind, part, n_dp):
    if kind == "attention":
        model = 4 * part
        return [
            [(0, i * model + k * part, i * part, part) for i in range(3)] + [(1, k * part, 3 * part, part)]
            for k in range(4)
        ]
    width = part // n_dp
    return [[(0, (4 * i + k) * width, i * width, width) for i in range(n_dp)] for k in range(4)]


def join_kernel(places, index_ref, *refs):
    blocks = [ref[...].astype(F32) for ref in refs[:4]]
    core, half = index_ref[0], index_ref[1]

    def swap(index, i, j):
        first = jnp.where(index == 0, blocks[i], blocks[j])
        blocks[j] = jnp.where(index == 0, blocks[j], blocks[i])
        blocks[i] = first

    swap(core, 0, 1)
    swap(core, 2, 3)
    swap(half, 0, 2)
    swap(half, 1, 3)
    for block, moves in zip(blocks, places):
        for output, start, source, width in moves:
            refs[4 + output][:, start : start + width] = block[:, source : source + width]


def join(blocks, index, places, widths):
    rows = blocks[0].shape[0]
    whole = pl.BlockSpec(memory_space=pltpu.VMEM)
    return pl.pallas_call(
        functools.partial(join_kernel, places),
        in_specs=[pl.BlockSpec(memory_space=pltpu.SMEM)] + [whole] * 4,
        out_specs=[whole] * len(widths),
        out_shape=[jax.ShapeDtypeStruct((rows, width), F32) for width in widths],
        cost_estimate=pl.CostEstimate(
            flops=0, bytes_accessed=6 * rows * sum(widths), transcendentals=0
        ),
        compiler_params=pltpu.CompilerParams(vmem_limit_bytes=32 << 20),
    )(index, *blocks)


def split_first_kernel(n_dp, index_ref, qkv_ref, out_ref, up_ref, *refs):
    vectors, targets = refs[:-2], refs[-2:]
    rows, part = out_ref.shape[0], out_ref.shape[1] // 4
    width = up_ref.shape[1] // 4 // n_dp
    for k in range(4):
        for flip, target in enumerate(targets):

            @pl.when(index_ref[0] == k ^ flip)
            def _():
                for i in range(3):
                    target[0:rows, i * part : (i + 1) * part] = qkv_ref[
                        :, (4 * i + k) * part : (4 * i + k + 1) * part
                    ]
                target[0:rows, 3 * part :] = out_ref[:, k * part : (k + 1) * part]
                for i in range(n_dp):
                    target[rows : 2 * rows, i * width : (i + 1) * width] = up_ref[
                        :, (4 * i + k) * width : (4 * i + k + 1) * width
                    ]

    for target in targets:
        start = 0
        for vector in vectors:
            width = vector.shape[0]
            target[2 * rows : 2 * rows + 1, start : start + width] = vector[...].reshape(1, width)
            start += width


def split_first(qkv_weight, out_weight, up_weight, vectors, quarter, n_dp):
    rows, model = out_weight.shape
    whole = pl.BlockSpec(memory_space=pltpu.VMEM)
    return pl.pallas_call(
        functools.partial(split_first_kernel, n_dp),
        in_specs=[pl.BlockSpec(memory_space=pltpu.SMEM)] + [whole] * (3 + len(vectors)),
        out_specs=[whole] * 2,
        out_shape=[jax.ShapeDtypeStruct((2 * rows + 8, model), BF16)] * 2,
        cost_estimate=pl.CostEstimate(
            flops=0, bytes_accessed=24 * rows * model, transcendentals=0
        ),
    )(quarter.reshape(1), qkv_weight, out_weight, up_weight, *vectors)


def split_rest_kernel(index_ref, down_ref, cell_ref, gene_ref, *targets):
    wide = cell_ref.shape[1] // 4
    cut = down_ref.shape[0] // 4
    for flip in range(2):
        down, decoder = targets[flip::2]
        start = pl.multiple_of((index_ref[0] ^ flip) * cut, cut)
        down[...] = down_ref[pl.ds(start, cut), :]
        for k in range(4):

            @pl.when(index_ref[0] == k ^ flip)
            def _():
                decoder[:, :wide] = cell_ref[:, k * wide : (k + 1) * wide]
                decoder[:, wide:] = gene_ref[:, k * wide : (k + 1) * wide]


def split_rest(down_weight, cell_weight, gene_weight, quarter):
    rows, wide = cell_weight.shape[0], cell_weight.shape[1] // 4
    whole = pl.BlockSpec(memory_space=pltpu.VMEM)
    shorter = jax.ShapeDtypeStruct((down_weight.shape[0] // 4, down_weight.shape[1]), BF16)
    return pl.pallas_call(
        split_rest_kernel,
        in_specs=[pl.BlockSpec(memory_space=pltpu.SMEM)] + [whole] * 3,
        out_specs=[whole] * 4,
        out_shape=[shorter] * 2 + [jax.ShapeDtypeStruct((rows, 2 * wide), BF16)] * 2,
        cost_estimate=pl.CostEstimate(
            flops=0, bytes_accessed=32 * rows * wide, transcendentals=0
        ),
        compiler_params=pltpu.CompilerParams(vmem_limit_bytes=32 << 20),
    )(quarter.reshape(1), down_weight, cell_weight, gene_weight)


def pack_kernel(room, index_ref, starts_ref, *refs):
    sources, out_ref = refs[:4], refs[4]
    micro, slots = sources[0].shape[0], sources[0].shape[1]
    for pair in range(2):
        for batch in range(micro):
            segment = (batch * 2 + pair) * room
            start = starts_ref[batch * 2 + pair]

            def put(first, second):
                kept = min(room, slots)
                out_ref[segment : segment + kept, :] = first[batch, 0:kept, :]

                def move(i, carry):
                    source = pl.multiple_of(jnp.minimum(i * 16, slots - 16), 16)
                    target = pl.multiple_of(segment + start + i * 16, 16)
                    out_ref[pl.ds(target, 16), :] = second[batch, pl.ds(source, 16), :]
                    return carry

                lax.fori_loop(0, (room - start) // 16, move, 0)

            pl.when(index_ref[1] == 0)(functools.partial(put, sources[2 * pair], sources[2 * pair + 1]))
            pl.when(index_ref[1] == 1)(functools.partial(put, sources[2 * pair + 1], sources[2 * pair]))


def pack(sources, index, starts, room):
    micro, _, model = sources[0].shape
    whole = pl.BlockSpec(memory_space=pltpu.VMEM)
    scalars = pl.BlockSpec(memory_space=pltpu.SMEM)
    return pl.pallas_call(
        functools.partial(pack_kernel, room),
        in_specs=[scalars, scalars] + [whole] * 4,
        out_specs=whole,
        out_shape=jax.ShapeDtypeStruct((2 * micro * room, model), BF16),
        cost_estimate=pl.CostEstimate(
            flops=0, bytes_accessed=12 * micro * room * model, transcendentals=0
        ),
        compiler_params=pltpu.CompilerParams(vmem_limit_bytes=40 << 20),
    )(index, starts, *sources)


def paste_kernel(index_ref, qkv_ref, *refs):
    blocks = [ref[...] for ref in refs[:4]]
    out_ref = refs[4]
    core, half = index_ref[0], index_ref[1]
    wide, part = qkv_ref.shape[1], blocks[0].shape[0]

    def swap(index, i, j):
        first = jnp.where(index == 0, blocks[i], blocks[j])
        blocks[j] = jnp.where(index == 0, blocks[j], blocks[i])
        blocks[i] = first

    swap(core, 0, 1)
    swap(core, 2, 3)
    swap(half, 0, 2)
    swap(half, 1, 3)
    out_ref[:, 0:wide] = qkv_ref[...]
    for i, block in enumerate(blocks):
        out_ref[i * part : (i + 1) * part, wide:] = block


def paste(grad_qkv, blocks, index):
    rows, wide = grad_qkv.shape
    whole = pl.BlockSpec(memory_space=pltpu.VMEM)
    return pl.pallas_call(
        paste_kernel,
        in_specs=[pl.BlockSpec(memory_space=pltpu.SMEM)] + [whole] * 5,
        out_specs=whole,
        out_shape=jax.ShapeDtypeStruct((rows, wide + blocks[0].shape[1]), BF16),
        cost_estimate=pl.CostEstimate(
            flops=0, bytes_accessed=6 * rows * wide, transcendentals=0
        ),
        compiler_params=pltpu.CompilerParams(vmem_limit_bytes=32 << 20),
    )(index, grad_qkv, *blocks)


def shards(
    n_dp,
    n_query,
    tokens,
    out_cotangent,
    qkv_weight,
    out_weight,
    up_weight,
    down_weight,
    attn_gain,
    ffn_gain,
    up_bias,
    cell_weight,
    gene_weight,
    decoder_bias,
    readout,
    gene_embed,
    query_cell,
    query_label,
    query_live,
):
    micro, _, length, model = tokens.shape
    slots = gene_embed.shape[2]
    chips = n_dp // 2
    shard = model // n_dp
    ff_shard = up_bias.shape[0]
    dh_shard = decoder_bias.shape[0]
    part = model // 4
    ff_part = ff_shard * n_dp // 4
    dh_part = dh_shard * n_dp // 4
    room = 2 * slots if n_query > 2 else (2 * slots * 5 // 8 + 15) // 16 * 16 + 16
    dp_index = lax.axis_index("dp").astype(jnp.int32)
    query_index = lax.axis_index("query").astype(jnp.int32)
    core = dp_index % 2
    half = query_index % 2
    quarter = 2 * half + core
    index = jnp.stack([core, half])
    chip = dp_index // 2
    position = jnp.where(chip % 2 == 0, chip // 2, chips - 1 - chip // 2)
    ring = [2 * i for i in range(chips // 2)] + [2 * i + 1 for i in reversed(range(chips // 2))]
    same_core = [[2 * i + k for i in range(chips)] for k in range(2)]
    chip_bits = [1 << i for i in range(1, n_dp.bit_length() - 1)]
    query_bits = [1 << i for i in range(n_query.bit_length() - 1)]

    def ring_moves(step):
        return [
            (2 * ring[i] + k, 2 * ring[(i + step) % chips] + k) for i in range(chips) for k in range(2)
        ]

    ahead, behind = ring_moves(1), ring_moves(-1)

    def dp_swap(value, bit):
        return lax.ppermute(value, "dp", [(i, i ^ bit) for i in range(n_dp)])

    def core_swap(value):
        return dp_swap(value, 1)

    def query_swap(value, bit=1):
        return lax.ppermute(value, "query", [(i, i ^ bit) for i in range(n_query)])

    def gather_four(value):
        near = jnp.stack([value, query_swap(value)], axis=1)
        return jnp.concatenate([near, core_swap(near)], axis=1)

    def scatter_four(value, batches):
        blocks = value.reshape((batches, 4, -1) + value.shape[1:])
        received = core_swap(blocks[:, 2:].astype(BF16))
        far = query_swap((blocks[:, 1] + received[:, 1].astype(F32)).astype(BF16))
        total = blocks[:, 0] + received[:, 0].astype(F32) + far.astype(F32)
        return total.reshape((-1,) + value.shape[1:])

    def order(which, first, second):
        return jnp.where(which == 0, first, second), jnp.where(which == 0, second, first)

    def by_quarter(a, b, c, d):
        a, b = order(core, a, b)
        c, d = order(core, c, d)
        a, c = order(half, a, c)
        b, d = order(half, b, d)
        return [a, b, c, d]

    def exchange_four(blocks):
        own, near, far, both = by_quarter(*blocks)
        theirs = core_swap(jnp.stack([near, both]))
        beyond = query_swap(jnp.stack([far, theirs[1]]))
        return own, theirs[0], beyond[0], beyond[1]

    def ring_start(mine, theirs):
        low, high = order(core, mine, core_swap(theirs))
        return [low, high]

    def last(held):
        return tuple(held[-2:])

    def pin(value, *events):
        return lax.optimization_barrier((value, *events))[0]

    def ring_step(held, *events):
        if len(held) < 2 * chips:
            low, high = lax.optimization_barrier((*last(held), *events))[:2]
            held.append(lax.ppermute(low, "dp", ahead))
            held.append(lax.ppermute(high, "dp", behind))

    def other_pairs(value):
        for bit in query_bits[1:]:
            value = value + query_swap(value, bit)
        return value

    def to_owner(low, high):
        mine, theirs = order(core, low, high)
        theirs = core_swap(theirs)
        far = query_swap(jnp.stack([mine, theirs]))
        return mine, theirs, far[0], far[1]

    def cores(rows):
        return rows[:shard], rows[shard:]

    def ring_scatter(grads):
        rows = grads.shape[0] // n_dp

        def piece(offset, side):
            start = (2 * ring_chip(position + offset, chips) + side) * rows
            return lax.dynamic_slice(grads, (start, 0), (rows, grads.shape[1]))

        low, high = piece(-1, 0), piece(1, 1)
        for step in range(1, chips):
            low = lax.ppermute(low, "dp", ahead)
            high = lax.ppermute(high, "dp", behind)
            low = (low.astype(F32) + piece(-1 - step, 0).astype(F32)).astype(BF16)
            high = (high.astype(F32) + piece(1 + step, 1).astype(F32)).astype(BF16)
        return other_pairs(low), other_pairs(high)

    def ring_scatter(grads):
        rows = grads.shape[0] // n_dp

        def piece(offset, side):
            start = (2 * ring_chip(position + offset, chips) + side) * rows
            return lax.dynamic_slice(grads, (start, 0), (rows, grads.shape[1]))

        low, high = piece(-1, 0), piece(1, 1)
        for step in range(1, chips):
            low = lax.ppermute(low, "dp", ahead)
            high = lax.ppermute(high, "dp", behind)
            low = (low.astype(F32) + piece(-1 - step, 0).astype(F32)).astype(BF16)
            high = (high.astype(F32) + piece(1 + step, 1).astype(F32)).astype(BF16)
        return other_pairs(low), other_pairs(high)

    def chip_rows(mine, theirs):
        return jnp.concatenate(order(core, mine, core_swap(theirs)))

    def plane_gather(rows):
        return lax.all_gather(rows, "dp", axis=0, tiled=True, axis_index_groups=same_core)

    def plane_scatter(grads):
        return lax.psum_scatter(
            grads, "dp", scatter_dimension=0, tiled=True, axis_index_groups=same_core
        )

    def group_sum(values):
        values = values + core_swap(values)[:, ::-1]
        return values + query_swap(values)

    first_ring = ring_start(
        *split_first(
            qkv_weight,
            out_weight,
            up_weight,
            [attn_gain, ffn_gain, up_bias, decoder_bias, readout],
            quarter,
            n_dp,
        )
    )
    down_mine, down_theirs, decoder_mine, decoder_theirs = split_rest(
        down_weight, cell_weight, gene_weight, quarter
    )
    tokens_far = query_swap(tokens[:, 0])
    cotangent_far = query_swap(pin(out_cotangent, tokens_far)[:, 0])
    gene_far = query_swap(pin(gene_embed, tokens_far)[:, 0])

    def with_cores(own, far):
        near = jnp.stack([own, far], axis=1)
        return jnp.concatenate([near, core_swap(near)], axis=1).reshape(-1, model)

    live = jnp.arange(slots, dtype=jnp.int32)[None, :] < query_live[0, :, 0][:, None]
    facts = jnp.stack(
        [query_cell[:, 0].astype(F32), query_label[:, 0].astype(F32), live.astype(F32)], axis=1
    ).reshape(micro * 3, slots)
    facts = jnp.concatenate(
        [facts, jnp.broadcast_to(query_live[0, :, 0].astype(F32)[:, None], (micro, slots))]
    )
    facts = jnp.stack(order(half, facts, query_swap(facts)), axis=1)
    facts = jnp.stack([facts, core_swap(facts)], axis=1)
    starts = (facts[3 * micro :, :, 0, 0].astype(jnp.int32) + 15) // 16 * 16
    facts = facts[: 3 * micro].reshape(micro, 3, 2, 2, slots)
    packed = []
    for batch in range(micro):
        for pair in range(2):
            line = jnp.pad(facts[batch, :, pair, 0], ((0, 0), (0, room)))
            line = lax.dynamic_update_slice(line, facts[batch, :, pair, 1], (0, starts[batch, pair]))
            packed.append(line[:, :room])
    facts = jnp.stack(packed, axis=1).reshape(3, micro, 2, room)
    starts = starts.reshape(-1)
    own_tokens = tokens[:, 0].reshape(micro * length, model)
    for step in range(1, chips):
        arrived = {3: (tokens_far,), chips - 2: (cotangent_far,), chips - 1: (gene_far,)}.get(step, ())
        ring_step(first_ring, *arrived)
        if step == chips - 2:
            down_rows = pin(chip_rows(down_mine, down_theirs), *first_ring[-4:-2])
            decoder_rows = pin(chip_rows(decoder_mine, decoder_theirs), *first_ring[-4:-2])
            down_part, decoder_part = plane_gather(down_rows), plane_gather(decoder_rows)
        if step == 3:
            all_tokens = with_cores(tokens[:, 0], tokens_far)
            norm_all, _ = layer_stats(all_tokens.astype(F32))
    attention_part, up_part, vectors = place(first_ring, position, (shard, shard, 8))
    all_cotangent = with_cores(out_cotangent[:, 0], cotangent_far)

    vectors = vectors.reshape(n_dp, 8, model)[:, 0].astype(F32)
    bounds = [0, shard, 2 * shard, 2 * shard + ff_shard, 2 * shard + ff_shard + dh_shard]
    bounds.append(bounds[-1] + dh_shard)
    pieces = [vectors[:, low:high] for low, high in zip(bounds[:-1], bounds[1:])]
    attn_gain_all = pieces[0].reshape(model)
    ffn_gain_all = pieces[1].reshape(model)
    up_bias_part = lax.dynamic_index_in_dim(
        pieces[2].reshape(n_dp, 4, ff_shard // 4), quarter, 1, keepdims=False
    ).reshape(ff_part)
    decoder_bias_part = lax.dynamic_slice(pieces[3].reshape(-1), (quarter * dh_part,), (dh_part,))
    readout_part = lax.dynamic_slice(pieces[4].reshape(-1), (quarter * dh_part,), (dh_part,))
    qkv_part = attention_part[:, : 3 * part]
    out_blocks = attention_part[:, 3 * part :].reshape(4, part, part)
    out_part = jnp.concatenate(
        by_quarter(*exchange_four([out_blocks[i] for i in range(4)])), axis=1
    )

    normed = (norm_all * attn_gain_all).astype(BF16)
    projected = product(pin(normed, all_cotangent), qkv_part).astype(BF16)
    own_wide = own_tokens.astype(F32)
    mixed, second, hidden, norm_two, scale_two = [], [], [], [], []
    for batch in range(micro):
        mixed.append(attend(projected, length, 4 * batch, 4))
        partial = product(mixed[-1], out_part)
        projected = pin(projected, partial)
        hidden.append(own_wide[batch * length : (batch + 1) * length] + scatter_four(partial, 1))
    gene_far = pin(gene_far, partial)
    gene_rows = pack(
        [gene_embed[:, 0], gene_far, core_swap(gene_embed[:, 0]), core_swap(gene_far)], index, starts, room
    )
    for batch in range(micro):
        normal, scale = layer_stats(hidden[batch])
        norm_two.append(normal)
        scale_two.append(scale)
        second.append(gather_four((normal * ffn_gain_all).astype(BF16)[None]))
    hidden, norm_two, scale_two = (jnp.concatenate(parts) for parts in (hidden, norm_two, scale_two))
    second = jnp.concatenate(second).reshape(-1, model)
    mixed = jnp.concatenate(mixed)
    up_proj = product(pin(second, gene_rows), up_part) + up_bias_part
    active = jax.nn.gelu(up_proj, approximate=True).astype(BF16)
    branch = product(active, down_part)

    def first_of(rows):
        return rows.reshape((-1, length) + rows.shape[1:])[:, 0]

    first_output = first_of(hidden) + scatter_four(first_of(branch), micro)
    output = (hidden + scatter_four(branch, micro)).reshape(micro, length, model)
    block_out = output.astype(BF16).at[:, 0].set(first_output.astype(BF16))

    gelu_back = jax.vjp(lambda inner: jax.nn.gelu(inner, approximate=True), up_proj)[1]
    grad_down_part = row_product(pin(active, branch), all_cotangent).astype(BF16)
    down_total = plane_scatter(grad_down_part)
    cotangent_in = pin(all_cotangent, grad_down_part)
    grad_up_proj = gelu_back(times_transpose(cotangent_in, down_part))[0].astype(BF16)
    grad_up_part = row_product(second, grad_up_proj).astype(BF16)
    up_total = plane_scatter(grad_up_part)
    grad_second = times_transpose(pin(grad_up_proj, grad_up_part), up_part)
    grad_second = scatter_four(grad_second, micro)
    cell_part, gene_part = decoder_part[:, :dh_part], decoder_part[:, dh_part:]
    grad_hidden_norm, _ = norm_back(grad_second, ffn_gain_all, norm_two, scale_two)
    own_cotangent = out_cotangent[:, 0].reshape(micro * length, model).astype(F32)
    grad_hidden = own_cotangent + grad_hidden_norm

    summaries = first_output.astype(BF16)
    for bit in query_bits:
        summaries = jnp.stack([summaries, query_swap(summaries, bit)])
    summaries = jnp.stack([summaries, core_swap(summaries)])
    cells = 2 * n_query * micro
    summaries = summaries.reshape(cells, model)
    cell_values = product(summaries, cell_part)
    cell_values = cell_values.reshape(2, n_query, micro, dh_part).transpose(2, 0, 1, 3)
    asked = facts[0].astype(jnp.int32) ^ query_index
    chosen_cell = cell_values[:, :, 0, None]
    for i in range(1, n_query):
        chosen_cell = jnp.where(asked[..., None] == i, cell_values[:, :, i, None], chosen_cell)
    asked = (jnp.arange(2)[None, :, None] * n_query + asked) * micro + jnp.arange(micro)[:, None, None]
    onehot = (asked.reshape(-1, 1) == jnp.arange(cells, dtype=jnp.int32)).astype(BF16)
    pre_act = product(gene_rows, gene_part).reshape(micro, 2, room, dh_part) + chosen_cell
    pre_act = pre_act + decoder_bias_part
    chance = jax.nn.sigmoid(pre_act)
    activity = pre_act * chance
    logits = jnp.sum(activity * readout_part, axis=-1)
    grad_hidden = pin(grad_hidden, logits)
    grad_attn = gather_four(grad_hidden.astype(BF16).reshape(micro, length, model)).reshape(-1, model)
    logits = group_sum(logits)
    grad_logits = facts[2] * (jax.nn.sigmoid(logits) - facts[1])
    grad_readout = jnp.sum(grad_logits[..., None] * activity, axis=(0, 1, 2))
    slope = chance * (1.0 + pre_act * (1.0 - chance))
    grad_pre = (grad_logits[..., None] * readout_part * slope).astype(BF16).reshape(-1, dh_part)
    grad_decoder_bias = jnp.sum(grad_pre.astype(F32), axis=0)
    grad_cells = row_product(onehot, grad_pre).astype(BF16)
    grad_gene_part = row_product(gene_rows, pin(grad_pre, grad_cells)).astype(BF16)
    gene_total = plane_scatter(grad_gene_part)
    grad_mixed = times_transpose(grad_attn, out_part).astype(BF16)

    grad_summary = times_transpose(grad_cells, cell_part).reshape(2, n_query, micro, model)
    grad_summary = grad_summary[0] + core_swap(grad_summary[1].astype(BF16)).astype(F32)
    for bit in reversed(query_bits):
        grad_summary = grad_summary.reshape(2, -1, micro, model)
        far = query_swap(grad_summary[1].astype(BF16), bit)
        grad_summary = grad_summary[0] + far.astype(F32)
    grad_summary = grad_summary.reshape(micro, model)

    first_cotangent = first_of(own_cotangent)
    first_grad = first_cotangent + grad_summary
    first_branch = gather_four(first_grad.astype(BF16)[:, None]).reshape(-1, model)
    first_change = (first_branch.astype(F32) - first_of(all_cotangent).astype(F32)).astype(BF16)
    first_gelu_back = jax.vjp(
        lambda inner: jax.nn.gelu(inner, approximate=True), first_of(up_proj)
    )[1]
    first_up = first_gelu_back(times_transpose(first_branch, down_part))[0].astype(BF16)
    first_up_change = (first_up.astype(F32) - first_of(grad_up_proj).astype(F32)).astype(BF16)
    first_second = scatter_four(times_transpose(first_up, up_part), micro)
    first_norm, first_scale = first_of(norm_two), first_of(scale_two)
    first_hidden, first_gain = norm_back(first_second, ffn_gain_all, first_norm, first_scale)
    first_hidden = first_grad + first_hidden
    first_attn = gather_four(first_hidden.astype(BF16)[:, None]).reshape(-1, model)
    first_mixed = times_transpose(first_attn, out_part).astype(BF16)
    first_attn_change = (first_attn.astype(F32) - first_of(grad_attn).astype(F32)).astype(BF16)
    grad_up_bias = jnp.sum(grad_up_proj.astype(F32), axis=0) + jnp.sum(
        first_up_change.astype(F32), axis=0
    )
    is_first = jnp.arange(micro * length)[:, None] % length == 0
    grad_ffn_gain = first_gain + jnp.sum(jnp.where(is_first, 0.0, grad_second * norm_two), axis=0)
    grad_hidden = grad_hidden.reshape(micro, length, model).at[:, 0].set(first_hidden)
    grad_hidden = grad_hidden.reshape(micro * length, model)

    left = jnp.concatenate([first_of(active), first_of(second), summaries])[None]
    right = jnp.concatenate([first_change, first_up_change, grad_cells])[None]
    for bit in chip_bits:
        left = jnp.concatenate([left, dp_swap(left, bit)])
        right = jnp.concatenate([right, dp_swap(right, bit)])
    left = left.reshape(chips, left.shape[1], chips, 2 * shard)
    left = lax.dynamic_index_in_dim(left, chip, 2, keepdims=False)

    def few_rows(start, stop):
        return row_product(
            left[:, start:stop].reshape(-1, 2 * shard), right[:, start:stop].reshape(-1, ff_part)
        )

    firsts = 4 * micro
    grad_down_rows = few_rows(0, firsts)
    grad_up_rows = few_rows(firsts, 2 * firsts)
    grad_cell_rows = few_rows(2 * firsts, 2 * firsts + cells)

    grad_out_part = row_product(mixed, grad_attn) + row_product(first_of(mixed), first_attn_change)
    grad_out_part = grad_out_part.astype(BF16)
    out_blocks = exchange_four([grad_out_part[:, i * part : (i + 1) * part] for i in range(4)])
    few = jnp.stack([down_total, up_total, jnp.zeros_like(up_total)]).astype(F32)
    few = few + jnp.stack([grad_down_rows, grad_up_rows, grad_cell_rows])
    few = other_pairs(few.astype(BF16)).reshape(3, 2, shard, model)
    few_owned = to_owner(few[:, 0], few[:, 1])
    gene_owned = to_owner(*cores(other_pairs(gene_total)))
    grad_projected = attend_back(projected, grad_mixed, first_mixed[:, None], length)
    grad_projected = pin(grad_projected, *few_owned)
    grad_qkv_part = row_product(normed, grad_projected).astype(BF16)
    attention_grads = ring_scatter(paste(grad_qkv_part, out_blocks, index))
    grad_normed = times_transpose(pin(grad_projected, grad_qkv_part), qkv_part)
    grad_normed = scatter_four(grad_normed, micro)
    norm_one, scale_one = layer_stats(own_wide)
    grad_input_norm, grad_attn_gain = norm_back(grad_normed, attn_gain_all, norm_one, scale_one)
    grad_tokens = (grad_hidden + grad_input_norm).reshape(micro, 1, length, model)

    grad_gene = jnp.concatenate(by_quarter(*gene_owned), axis=1).astype(F32)
    down_rows, up_rows, cell_rows = zip(*((block[0], block[1], block[2]) for block in few_owned))
    grad_cell = jnp.concatenate(by_quarter(*cell_rows), axis=1).astype(F32)
    grad_down = jnp.concatenate(by_quarter(*down_rows)).astype(F32)
    (grad_up,) = join(up_rows, index, column_places("up", ff_part, n_dp), [4 * ff_part])
    grad_qkv, grad_out = join(
        to_owner(*attention_grads), index, column_places("attention", part, n_dp), [3 * model, model]
    )

    chosen = (jnp.arange(4) == quarter).astype(F32)
    owned = jnp.concatenate(
        [
            grad_attn_gain.reshape(n_dp, shard),
            grad_ffn_gain.reshape(n_dp, shard),
            (grad_up_bias.reshape(n_dp, 1, ff_shard // 4) * chosen[:, None]).reshape(n_dp, ff_shard),
            (chosen[:, None] * grad_decoder_bias).reshape(n_dp, dh_shard),
            (chosen[:, None] * grad_readout).reshape(n_dp, dh_shard),
        ],
        axis=1,
    )
    for bit in reversed([1] + chip_bits):
        owned = owned.reshape((2, owned.shape[0] // 2) + owned.shape[1:])
        kept, sent = order((dp_index // bit) % 2, owned[0], owned[1])
        owned = kept + dp_swap(sent, bit)
    for bit in query_bits:
        owned = owned + query_swap(owned, bit)
    small = [owned[0, low:high] for low, high in zip(bounds[:-1], bounds[1:])]
    return (
        block_out[:, None],
        grad_tokens,
        grad_qkv,
        grad_out,
        grad_up,
        grad_down,
        small[0],
        small[1],
        small[2],
        grad_cell,
        grad_gene,
        small[3],
        small[4],
    )


def solution(mesh):
    cells = P(None, ("dp", "query"), None, None)
    rows = P("dp", None)
    vector = P("dp")
    slots = P(None, ("dp", "query"), None)
    return jax.shard_map(
        functools.partial(shards, mesh.shape["dp"], mesh.shape["query"]),
        mesh=mesh,
        in_specs=(
            cells, cells, rows, rows, rows, rows, vector, vector, vector, rows, rows, vector, vector,
            cells, slots, slots, P("dp", None, "query"),
        ),
        out_specs=(
            cells, cells, rows, rows, rows, rows, vector, vector, vector, rows, rows, vector, vector,
        ),
        check_vma=False,
    )
```

time: 1560 us -> 663 us (0.42)
  waiting for transfers between devices: 957 us -> 208 us
  matrix products: 339 us -> 95.5 us
  blocking collectives: 159 us -> 0 us
  other arithmetic: 33.2 us -> 113 us
  starting transfers between devices: 1.09 us -> 76.4 us
  Pallas kernels: 0 us -> 55.9 us
  local copies, waits for them, and re-layouts: 41 us -> 79.4 us
    reduce_scatter x5 -> x3, waiting for transfers between devices: 509 us -> 0.04 us  [plane_scatter(): lax.psum_scatter(grads, 'dp', scatter_dimension=0, tiled=True, axis_index...]
    all_gather x6 -> x2, waiting for transfers between devices: 411 us -> 0.01 us  [plane_gather(): lax.all_gather(rows, 'dp', axis=0, tiled=True, axis_index_groups=same_core)]
    ppermute x0 -> x91, waiting for transfers between devices: none -> 208 us  [the longest x25 99.2 us: query_swap(): return lax.ppermute(value, 'query', [(i, i ^ bit) for i in range(n_query)])]
    unnamed x3 -> x0, blocking collectives: 133 us -> none
    dot_general x32 -> x7, matrix products: 166 us -> 33.7 us  [product(): return jnp.dot(left, right, preferred_element_type=F32)]
    dot_general x10, matrix products: 110 us -> 32 us  [row_product(): lax.dot_general(left, right, (((0,), (0,)), ((), ())), preferred_element_...]
    ppermute x0 -> x91, starting transfers between devices: none -> 75.3 us  [the longest x25 31.9 us: query_swap(): return lax.ppermute(value, 'query', [(i, i ^ bit) for i in range(n_query)])]
    pallas_call x0 -> x10, Pallas kernels: none -> 55.9 us  [the longest x1 23.3 us: attend_back(): pl.pallas_call(attend_back_kernel, grid=(rows // length,), in_specs=[pl.B...]
  transfers between devices with their start and end apart: 13 -> 96, of which waited for: 11 -> 47; matrix products, arithmetic and copies ran while one was open for 19% -> 39% of each run, Pallas kernels for 0% -> 9%
where the time goes in v1:
time: 663 us; the launch traced here: 653 us
  waiting for transfers between devices  208 us (31%)
  other arithmetic  113 us (17%)
  matrix products  95.5 us (14%)
  local copies, waits for them, and re-layouts  79.4 us (12%)
  starting transfers between devices  76.4 us (12%)
  Pallas kernels  55.9 us (8%)
  between operations  24.7 us (4%)
    ppermute x25, waiting for transfers between devices, query_swap(): return lax.ppermute(value, 'query', [(i, i ^ bit) for i in range(n_query)])  99.2 us
    ppermute x38, waiting for transfers between devices, dp_swap(): return lax.ppermute(value, 'dp', [(i, i ^ bit) for i in range(n_dp)])  47.6 us
    unnamed x280, local copies, waits for them, and re-layouts  34 us
    dot_general x7, matrix products, product(): return jnp.dot(left, right, preferred_element_type=F32)  33.7 us
    dot_general x10, matrix products, row_product(): lax.dot_general(left, right, (((0,), (0,)), ((), ())), preferred_element_...  32 us
    ppermute x25, starting transfers between devices, query_swap(): return lax.ppermute(value, 'query', [(i, i ^ bit) for i in range(n_query)])  31.9 us
    ppermute x7, waiting for transfers between devices, ring_step(): held.append(lax.ppermute(low, 'dp', ahead))  30.6 us
    dot_general x8, matrix products, times_transpose(): lax.dot_general(left, right, (((1,), (1,)), ((), ())), preferred_element_...  29.7 us
  transfers between devices with their start and end apart: 96, of which 47 were waited for; matrix products, arithmetic and copies ran while one was open for 39% of the time, Pallas kernels for 9%

profile of v1, /device:TPU:0, one launch (start us, length us, event | category | flops | bytes accessed | tf_op | source)
XLA Modules:
  0.0 652.9 jit_solution(18201655238024618)
XLA Ops:
  10.2 2.9 collective-permute-start.30
  13.2 3.0 shard_map.264
  29.8 6.9 %collective-permute-done.3.refs_2_ = bf16[168,1280]{1,0:T(8,128)(2,1)S(1)} collective-permute-done((bf16[168,1280]{1,0:T(8,128)(2,1)S(1)}, bf16[168,1280]{1,0:T(8,128)(2,1)S(1)}, u32[]{:S(2)}, u32[]{:S(2)}) %collective-permute-start.3) | collective-permute-done | bytes 430112 | tf_op jit(solution)/shard_map/ppermute | solution.py:444
  42.6 7.0 %collective-permute-done.5.refs_4_ = bf16[168,1280]{1,0:T(8,128)(2,1)S(1)} collective-permute-done((bf16[168,1280]{1,0:T(8,128)(2,1)S(1)}, bf16[168,1280]{1,0:T(8,128)(2,1)S(1)}, u32[]{:S(2)}, u32[]{:S(2)}) %collective-permute-start.5) | collective-permute-done | bytes 430112 | tf_op jit(solution)/shard_map/ppermute | solution.py:444
  54.3 6.8 %collective-permute-done.7.refs_6_ = bf16[168,1280]{1,0:T(8,128)(2,1)S(1)} collective-permute-done((bf16[168,1280]{1,0:T(8,128)(2,1)S(1)}, bf16[168,1280]{1,0:T(8,128)(2,1)S(1)}, u32[]{:S(2)}, u32[]{:S(2)}) %collective-permute-start.7) | collective-permute-done | bytes 430112 | tf_op jit(solution)/shard_map/ppermute | solution.py:444
  76.6 4.3 collective-permute-done.11.refs_10_
  101.9 11.2 %collective-permute-done.13 = bf16[2,128,1280]{2,1,0:T(8,128)(2,1)} collective-permute-done((bf16[2,128,1280]{2,1,0:T(8,128)(2,1)}, bf16[2,128,1280]{2,1,0:T(8,128)(2,1)}, u32[]{:S(2)}, u32[]{:S(2)}) %collective-permute-start.13) | collective-permute-done | bytes 655392 | tf_op jit(solution)/shard_map/ppermute | solution.py:402
  122.0 4.1 maximum_convert_fusion
  126.1 24.0 %collective-permute-done.16.refs_1_ = bf16[2,384,1280]{2,1,0:T(8,128)(2,1)S(1)} collective-permute-done((bf16[2,384,1280]{2,1,0:T(8,128)(2,1)}, bf16[2,384,1280]{2,1,0:T(8,128)(2,1)S(1)}, u32[]{:S(2)}, u32[]{:S(2)}) %collective-permute-start.16) | collective-permute-done | bytes 1966112 | tf_op jit(solution)/shard_map/ppermute | solution.py:402
  152.5 3.7 pad_maximum_fusion
  156.2 3.0 collective-permute-done.17.refs_14_
  170.0 3.4 fusion.12
  175.9 4.1 fusion.29.projected_ref
  180.0 8.9 %shard_map.266 = bf16[512,320]{1,0:T(8,128)(2,1)} custom-call(bf16[1024,960]{1,0:T(8,128)(2,1)} %fusion.29.projected_ref), custom_call_target="tpu_custom_call" | custom-call | flops 83886080 | bytes 1474560 | tf_op jit(solution)/shard_map/pallas_call | solution.py:85
  199.8 8.9 %shard_map.267 = bf16[512,320]{1,0:T(8,128)(2,1)} custom-call(bf16[1024,960]{1,0:T(8,128)(2,1)} %fusion.29.projected_ref), custom_call_target="tpu_custom_call" | custom-call | flops 83886080 | bytes 1474560 | tf_op jit(solution)/shard_map/pallas_call | solution.py:85
  218.9 7.2 %collective-permute-done.23 = bf16[1,128,1280]{2,1,0:T(8,128)(2,1)S(1)} collective-permute-done((bf16[1,128,1280]{2,1,0:T(8,128)(2,1)S(1)}, bf16[1,128,1280]{2,1,0:T(8,128)(2,1)S(1)}, u32[]{:S(2)}, u32[]{:S(2)}) %collective-permute-start.23) | collective-permute-done | bytes 327712 | tf_op jit(solution)/shard_map/ppermute | solution.py:402
  227.7 4.8 collective-permute-done.25
  244.3 5.3 collective-permute-done.28
  251.6 3.6 collective-permute-done.26
  263.7 3.9 shard_map.268
  267.6 6.0 multiply_convert_fusion.1
  277.6 6.4 fusion.149
  287.0 5.2 convolution_convert_fusion.1
  293.2 10.5 %convert_reduce_fusion.1 = (f32[1280]{0:T(1024)}, bf16[1024,1280]{1,0:T(8,128)(2,1)S(1)}) fusion(f32[1024,1280]{1,0:T(8,128)} %get-tuple-element.339, bf16[1024,1280]{1,0:T(8,128)(2,1)} %bitcast.567, bf16[1280,1280]{1,0:T(8,128)(2,1)} %all-gather.3.cloned.1.call-done), kind=kOutput, calls=%fused_computation.25 | convolution fusion | flops 3384277760 | bytes 13767680 | tf_op jit(solution)/shard_map/dot_general | solution.py:25
  305.2 5.1 convolution_convert_fusion
  318.3 5.3 fusion.150
  341.8 3.3 collective-permute-done.58
  355.1 12.8 %collective-permute-done.36 = bf16[2,128,1280]{2,1,0:T(8,128)(2,1)S(1)} collective-permute-done((bf16[2,128,1280]{2,1,0:T(8,128)(2,1)S(1)}, bf16[2,128,1280]{2,1,0:T(8,128)(2,1)S(1)}, u32[]{:S(2)}, u32[]{:S(2)}) %collective-permute-start.36) | collective-permute-done | bytes 655392 | tf_op jit(solution)/shard_map/ppermute | solution.py:402
  372.8 10.3 %fusion.1 = f32[1984,1280]{1,0:T(8,128)S(1)} fusion(bf16[1984,1280]{1,0:T(8,128)(2,1)} %copy-done, f32[1280]{0:T(1024)S(1)} %copy-done.121, f32[2,2,1280]{2,1,0:T(2,128)S(1)} %copy.329, f32[2,2,1280]{2,1,0:T(2,128)S(1)} %copy.328, pred[1984]{0:T(1024)(128)(4,1)S(1)} %copy-done.124, bf16[1280,2560]{1,0:T(8,128)(2,1)} %all-gather.5.cloned.1.call-done), kind=kOutput, calls=%fused_computation.2 | convolution fusion | flops 6508789760 | bytes 18561984 | tf_op jit(solution)/shard_map/dot_general | solution.py:17
  383.2 3.8 copy-done.47
  387.0 3.0 multiply_reduce_fusion.1
  390.2 4.5 multiply_reduce_fusion.7
  398.7 7.9 %convert_reduce_fusion = (f32[1280]{0:T(1024)S(1)}, bf16[1984,1280]{1,0:T(8,128)(2,1)S(1)}, f32[1280]{0:T(1024)S(1)}) fusion(f32[1984,1280]{1,0:T(8,128)} %copy-done.47, f32[1280]{0:T(1024)S(1)} %copy-done.104, f32[1984]{0:T(1024)S(1)} %mul.692), kind=kLoop, calls=%fused_computation.4 | loop fusion | flops 38090240 | bytes 15260416 | tf_op jit(solution)/shard_map/reduce_sum | solution.py:649
  407.7 3.7 fusion.16
  411.5 3.3 convert_add_fusion
  421.2 12.0 %convolution_convert_fusion.2 = bf16[1280,1280]{1,0:T(8,128)(2,1)} fusion(bf16[1984,1280]{1,0:T(8,128)(2,1)} %copy-done, bf16[1984,1280]{1,0:T(8,128)(2,1)} %copy-done.48), kind=kOutput, calls=%fused_computation.11 | convolution fusion | flops 6502809600 | bytes 13434880 | tf_op jit(solution)/shard_map/dot_general | solution.py:21
  442.1 4.1 convert_reduce_fusion.3
  459.4 9.2 %collective-permute-done.60 = bf16[2,24,1280]{2,1,0:T(8,128)(2,1)S(1)} collective-permute-done((bf16[2,24,1280]{2,1,0:T(8,128)(2,1)S(1)}, bf16[2,24,1280]{2,1,0:T(8,128)(2,1)S(1)}, u32[]{:S(2)}, u32[]{:S(2)}) %collective-permute-start.60) | collective-permute-done | bytes 122912 | tf_op jit(solution)/shard_map/ppermute | solution.py:396
  471.6 21.0 %collective-permute-done.61 = bf16[4,24,1280]{2,1,0:T(8,128)(2,1)S(1)} collective-permute-done((bf16[4,24,1280]{2,1,0:T(8,128)(2,1)S(1)}, bf16[4,24,1280]{2,1,0:T(8,128)(2,1)S(1)}, u32[]{:S(2)}, u32[]{:S(2)}) %collective-permute-start.61) | collective-permute-done | bytes 245792 | tf_op jit(solution)/shard_map/ppermute | solution.py:396
  508.7 23.3 %shard_map.270 = bf16[1024,960]{1,0:T(8,128)(2,1)} custom-call(bf16[1024,960]{1,0:T(8,128)(2,1)} %fusion.29.projected_ref, bf16[1024,320]{1,0:T(8,128)(2,1)} %copy.346.grad_mixed_ref, bf16[8,1,320]{2,1,0:T(2,128)(2,1)} %copy.347.first_ref), custom_call_target="tpu_custom_call" | custom-call | flops 419430400 | bytes 4915200 | tf_op jit(solution)/shard_map/pallas_call | solution.py:101
  532.1 5.5 convolution_convert_fusion.3.qkv_ref
  549.9 8.8 %collective-permute-done.66 = bf16[2,320,320]{2,1,0:T(8,128)(2,1)S(1)} collective-permute-done((bf16[2,320,320]{2,1,0:T(8,128)(2,1)S(1)}, bf16[2,320,320]{2,1,0:T(8,128)(2,1)S(1)}, u32[]{:S(2)}, u32[]{:S(2)}) %collective-permute-start.66) | collective-permute-done | bytes 409632 | tf_op jit(solution)/shard_map/ppermute | solution.py:402
  563.2 3.0 collective-permute-done.74
  604.7 3.3 collective-permute-done.85
  608.8 2.9 collective-permute-done.86
  616.2 3.7 collective-permute-done.80
  628.4 7.5 %collective-permute-done.82 = bf16[2,80,1280]{2,1,0:T(8,128)(2,1)S(1)} collective-permute-done((bf16[2,80,1280]{2,1,0:T(8,128)(2,1)S(1)}, bf16[2,80,1280]{2,1,0:T(8,128)(2,1)S(1)}, u32[]{:S(2)}, u32[]{:S(2)}) %collective-permute-start.82) | collective-permute-done | bytes 409632 | tf_op jit(solution)/shard_map/ppermute | solution.py:402
  637.9 6.5 %collective-permute-done.90 = bf16[2,80,1280]{2,1,0:T(8,128)(2,1)S(1)} collective-permute-done((bf16[2,80,1280]{2,1,0:T(8,128)(2,1)S(1)}, bf16[2,80,1280]{2,1,0:T(8,128)(2,1)S(1)}, u32[]{:S(2)}, u32[]{:S(2)}) %collective-permute-start.90) | collective-permute-done | bytes 409632 | tf_op jit(solution)/shard_map/ppermute | solution.py:402
  (737 shorter events, 299.2 us)
Async XLA Ops:
  7.2 270.4 %all-gather.3.cloned.1.call-start = ((), (), s32[]{:S(2)}) async-start(), calls=%async_computation.3 | async-start | bytes 3686400 | tf_op jit(solution)/shard_map/all_gather | solution.py:495
  10.2 44.0 %collective-permute-start.30 = (f32[8,384]{1,0:T(8,128)S(1)}, f32[8,384]{1,0:T(8,128)S(1)}, u32[]{:S(2)}, u32[]{:S(2)}) collective-permute-start(f32[8,384]{1,0:T(8,128)S(1)} %pad_maximum_fusion.34), channel_id=1, source_target_pairs={{0,1},{1,0},{2,3},{3,2},{4,5},{5,4},{6,7},{7,6},{8,9},{9,8},{10,11... | collective-permute-start | bytes 36872 | tf_op jit(solution)/shard_map/ppermute | solution.py:402
  13.2 29.3 %collective-permute-start = (bf16[2,128,1280]{2,1,0:T(8,128)(2,1)}, bf16[2,128,1280]{2,1,0:T(8,128)(2,1)S(1)}, u32[]{:S(2)}, u32[]{:S(2)}) collective-permute-start(bf16[2,128,1280]{2,1,0:T(8,128)(2,1)} %bitcast.533), channel_id=1, source_target_pairs={{0,1},{1,0},{2,3},{3,2},{4,5},{5,4},{6,7},{7,6},{8,9},{9,8},{10,11... | collective-permute-start | bytes 1966088 | tf_op jit(solution)/shard_map/ppermute | solution.py:402
  22.1 52.7 %collective-permute-start.34 = (bf16[80,1280]{1,0:T(8,128)(2,1)}, bf16[80,1280]{1,0:T(8,128)(2,1)}, u32[]{:S(2)}, u32[]{:S(2)}) collective-permute-start(bf16[80,1280]{1,0:T(8,128)(2,1)} %get-tuple-element.104), channel_id=1, source_target_pairs={{0,2},{2,0},{4,6},{6,4},{8,10},{10,8},{12,14},{14,12},{16,18},{18,... | collective-permute-start | bytes 614408 | tf_op jit(solution)/shard_map/ppermute | solution.py:396
  24.5 12.1 %collective-permute-start.3 = (bf16[168,1280]{1,0:T(8,128)(2,1)S(1)}, bf16[168,1280]{1,0:T(8,128)(2,1)S(1)}, u32[]{:S(2)}, u32[]{:S(2)}) collective-permute-start(bf16[168,1280]{1,0:T(8,128)(2,1)S(1)} %get-tuple-element.80.refs_0_), channel_id=1, source_target_pairs={{0,8},{2,10},{8,16},{10,18},{16,24},{18,26},{24,28},{26,30},{28,20... | collective-permute-start | bytes 1290248 | tf_op jit(solution)/shard_map/ppermute | solution.py:444
  27.4 11.5 %collective-permute-start.4 = (bf16[168,1280]{1,0:T(8,128)(2,1)S(1)}, bf16[168,1280]{1,0:T(8,128)(2,1)S(1)}, u32[]{:S(2)}, u32[]{:S(2)}) collective-permute-start(bf16[168,1280]{1,0:T(8,128)(2,1)S(1)} %get-tuple-element.81.refs_1_), channel_id=1, source_target_pairs={{0,4},{2,6},{8,0},{10,2},{16,8},{18,10},{24,16},{26,18},{28,24},{3... | collective-permute-start | bytes 1290248 | tf_op jit(solution)/shard_map/ppermute | solution.py:445
  38.9 10.6 %collective-permute-start.5 = (bf16[168,1280]{1,0:T(8,128)(2,1)S(1)}, bf16[168,1280]{1,0:T(8,128)(2,1)S(1)}, u32[]{:S(2)}, u32[]{:S(2)}) collective-permute-start(bf16[168,1280]{1,0:T(8,128)(2,1)S(1)} %collective-permute-done.3.refs_2_), channel_id=1, source_target_pairs={{0,8},{2,10},{8,16},{10,18},{16,24},{18,26},{24,28},{26,30},{28,20... | collective-permute-start | bytes 1290248 | tf_op jit(solution)/shard_map/ppermute | solution.py:444
  41.3 10.4 %collective-permute-start.6 = (bf16[168,1280]{1,0:T(8,128)(2,1)S(1)}, bf16[168,1280]{1,0:T(8,128)(2,1)S(1)}, u32[]{:S(2)}, u32[]{:S(2)}) collective-permute-start(bf16[168,1280]{1,0:T(8,128)(2,1)S(1)} %collective-permute-done.4.refs_3_), channel_id=1, source_target_pairs={{0,4},{2,6},{8,0},{10,2},{16,8},{18,10},{24,16},{26,18},{28,24},{3... | collective-permute-start | bytes 1290248 | tf_op jit(solution)/shard_map/ppermute | solution.py:445
  42.5 57.3 %collective-permute-start.41 = (bf16[80,2560]{1,0:T(8,128)(2,1)}, bf16[80,2560]{1,0:T(8,128)(2,1)}, u32[]{:S(2)}, u32[]{:S(2)}) collective-permute-start(bf16[80,2560]{1,0:T(8,128)(2,1)} %get-tuple-element.110), channel_id=1, source_target_pairs={{0,2},{2,0},{4,6},{6,4},{8,10},{10,8},{12,14},{14,12},{16,18},{18,... | collective-permute-start | bytes 1228808 | tf_op jit(solution)/shard_map/ppermute | solution.py:396
  54.3 13.5 %collective-permute-start.31 = (f32[8,2,384]{2,0,1:T(8,128)S(1)}, f32[8,2,384]{2,0,1:T(8,128)S(1)}, u32[]{:S(2)}, u32[]{:S(2)}) collective-permute-start(f32[8,2,384]{2,0,1:T(8,128)S(1)} %get-tuple-element.320), channel_id=1, source_target_pairs={{0,2},{2,0},{4,6},{6,4},{8,10},{10,8},{12,14},{14,12},{16,18},{18,... | collective-permute-start | bytes 73736 | tf_op jit(solution)/shard_map/ppermute | solution.py:396
  67.8 195.8 %collective-permute-start.32 = (bf16[2,384,1280]{2,1,0:T(8,128)(2,1)}, bf16[2,384,1280]{2,1,0:T(8,128)(2,1)}, u32[]{:S(2)}, u32[]{:S(2)}) collective-permute-start(bf16[2,384,1280]{2,1,0:T(8,128)(2,1)} %bitcast.45.refs_0_), channel_id=1, source_target_pairs={{0,2},{2,0},{4,6},{6,4},{8,10},{10,8},{12,14},{14,12},{16,18},{18,... | collective-permute-start | bytes 5898248 | tf_op jit(solution)/shard_map/ppermute | solution.py:396
  81.9 288.3 %all-gather.5.cloned.1.call-start = ((), (), s32[]{:S(2)}) async-start(), calls=%async_computation.4 | async-start | bytes 7372800 | tf_op jit(solution)/shard_map/all_gather | solution.py:495
  95.1 18.0 %collective-permute-start.13 = (bf16[2,128,1280]{2,1,0:T(8,128)(2,1)}, bf16[2,128,1280]{2,1,0:T(8,128)(2,1)}, u32[]{:S(2)}, u32[]{:S(2)}) collective-permute-start(bf16[2,128,1280]{2,1,0:T(8,128)(2,1)} %bitcast.538), channel_id=1, source_target_pairs={{0,1},{1,0},{2,3},{3,2},{4,5},{5,4},{6,7},{7,6},{8,9},{9,8},{10,11... | collective-permute-start | bytes 1966088 | tf_op jit(solution)/shard_map/ppermute | solution.py:402
  99.1 16.6 %collective-permute-start.1 = (bf16[2,2,128,1280]{3,2,1,0:T(8,128)(2,1)}, bf16[2,2,128,1280]{3,2,1,0:T(8,128)(2,1)}, u32[]{:S(2)}, u32[]{:S(2)}) collective-permute-start(bf16[2,2,128,1280]{3,2,1,0:T(8,128)(2,1)} %pad_maximum_fusion.2), channel_id=1, source_target_pairs={{0,2},{2,0},{4,6},{6,4},{8,10},{10,8},{12,14},{14,12},{16,18},{18,... | collective-permute-start | bytes 3932168 | tf_op jit(solution)/shard_map/ppermute | solution.py:396
  99.2 50.9 %collective-permute-start.16 = (bf16[2,384,1280]{2,1,0:T(8,128)(2,1)}, bf16[2,384,1280]{2,1,0:T(8,128)(2,1)S(1)}, u32[]{:S(2)}, u32[]{:S(2)}) collective-permute-start(bf16[2,384,1280]{2,1,0:T(8,128)(2,1)} %bitcast.11), channel_id=1, source_target_pairs={{0,1},{1,0},{2,3},{3,2},{4,5},{5,4},{6,7},{7,6},{8,9},{9,8},{10,11... | collective-permute-start | bytes 5898248 | tf_op jit(solution)/shard_map/ppermute | solution.py:402
  115.7 36.8 %collective-permute-start.19 = (bf16[2,2,128,1280]{3,2,1,0:T(8,128)(2,1)}, bf16[2,2,128,1280]{3,2,1,0:T(8,128)(2,1)}, u32[]{:S(2)}, u32[]{:S(2)}) collective-permute-start(bf16[2,2,128,1280]{3,2,1,0:T(8,128)(2,1)} %pad_maximum_fusion.3), channel_id=1, source_target_pairs={{0,2},{2,0},{4,6},{6,4},{8,10},{10,8},{12,14},{14,12},{16,18},{18,... | collective-permute-start | bytes 3932168 | tf_op jit(solution)/shard_map/ppermute | solution.py:396
  119.9 30.1 %collective-permute-start.14 = (bf16[168,1280]{1,0:T(8,128)(2,1)S(1)}, bf16[168,1280]{1,0:T(8,128)(2,1)S(1)}, u32[]{:S(2)}, u32[]{:S(2)}) collective-permute-start(bf16[168,1280]{1,0:T(8,128)(2,1)S(1)} %collective-permute-done.11.refs_10_), channel_id=1, source_target_pairs={{0,8},{2,10},{8,16},{10,18},{16,24},{18,26},{24,28},{26,30},{28,20... | collective-permute-start | bytes 1290248 | tf_op jit(solution)/shard_map/ppermute | solution.py:444
  120.7 29.4 %collective-permute-start.15 = (bf16[168,1280]{1,0:T(8,128)(2,1)S(1)}, bf16[168,1280]{1,0:T(8,128)(2,1)}, u32[]{:S(2)}, u32[]{:S(2)}) collective-permute-start(bf16[168,1280]{1,0:T(8,128)(2,1)S(1)} %collective-permute-done.12.refs_11_), channel_id=1, source_target_pairs={{0,4},{2,6},{8,0},{10,2},{16,8},{18,10},{24,16},{26,18},{28,24},{3... | collective-permute-start | bytes 1290248 | tf_op jit(solution)/shard_map/ppermute | solution.py:445
  152.2 343.9 %reduce-scatter.4.cloned.1.call-start = ((), (), s32[]{:S(2)}) async-start(), calls=%async_computation.5 | async-start | bytes 3686400 | tf_op jit(solution)/shard_map/reduce_scatter | solution.py:498
  174.4 14.5 %collective-permute-start.21 = (bf16[2,320,320]{2,1,0:T(8,128)(2,1)}, bf16[2,320,320]{2,1,0:T(8,128)(2,1)}, u32[]{:S(2)}, u32[]{:S(2)}) collective-permute-start(bf16[2,320,320]{2,1,0:T(8,128)(2,1)} %pad_maximum_fusion.13), channel_id=1, source_target_pairs={{0,1},{1,0},{2,3},{3,2},{4,5},{5,4},{6,7},{7,6},{8,9},{9,8},{10,11... | collective-permute-start | bytes 1228808 | tf_op jit(solution)/shard_map/ppermute | solution.py:402
  198.3 15.9 %collective-permute-start.22 = (bf16[1,2,128,1280]{3,2,1,0:T(8,128)(2,1)}, bf16[1,2,128,1280]{3,2,1,0:T(8,128)(2,1)}, u32[]{:S(2)}, u32[]{:S(2)}) collective-permute-start(bf16[1,2,128,1280]{3,2,1,0:T(8,128)(2,1)} %slice.1138), channel_id=1, source_target_pairs={{0,2},{2,0},{4,6},{6,4},{8,10},{10,8},{12,14},{14,12},{16,18},{18,... | collective-permute-start | bytes 1966088 | tf_op jit(solution)/shard_map/ppermute | solution.py:396
  214.0 49.6 %collective-permute-start.33 = (bf16[2,384,1280]{2,1,0:T(8,128)(2,1)}, bf16[2,384,1280]{2,1,0:T(8,128)(2,1)}, u32[]{:S(2)}, u32[]{:S(2)}) collective-permute-start(bf16[2,384,1280]{2,1,0:T(8,128)(2,1)} %copy-done.1), channel_id=1, source_target_pairs={{0,2},{2,0},{4,6},{6,4},{8,10},{10,8},{12,14},{14,12},{16,18},{18,... | collective-permute-start | bytes 5898248 | tf_op jit(solution)/shard_map/ppermute | solution.py:396
  215.5 10.6 %collective-permute-start.23 = (bf16[1,128,1280]{2,1,0:T(8,128)(2,1)S(1)}, bf16[1,128,1280]{2,1,0:T(8,128)(2,1)S(1)}, u32[]{:S(2)}, u32[]{:S(2)}) collective-permute-start(bf16[1,128,1280]{2,1,0:T(8,128)(2,1)S(1)} %fusion.66), channel_id=1, source_target_pairs={{0,1},{1,0},{2,3},{3,2},{4,5},{5,4},{6,7},{7,6},{8,9},{9,8},{10,11... | collective-permute-start | bytes 983048 | tf_op jit(solution)/shard_map/ppermute | solution.py:402
  217.8 14.8 %collective-permute-start.25 = (bf16[1,128,1280]{2,1,0:T(8,128)(2,1)S(1)}, bf16[1,128,1280]{2,1,0:T(8,128)(2,1)S(1)}, u32[]{:S(2)}, u32[]{:S(2)}) collective-permute-start(bf16[1,128,1280]{2,1,0:T(8,128)(2,1)S(1)} %fusion.67), channel_id=1, source_target_pairs={{0,1},{1,0},{2,3},{3,2},{4,5},{5,4},{6,7},{7,6},{8,9},{9,8},{10,11... | collective-permute-start | bytes 983048 | tf_op jit(solution)/shard_map/ppermute | solution.py:402
  238.7 10.9 %collective-permute-start.28 = (bf16[1,128,1280]{2,1,0:T(8,128)(2,1)}, bf16[1,128,1280]{2,1,0:T(8,128)(2,1)}, u32[]{:S(2)}, u32[]{:S(2)}) collective-permute-start(bf16[1,128,1280]{2,1,0:T(8,128)(2,1)} %fusion.76), channel_id=1, source_target_pairs={{0,1},{1,0},{2,3},{3,2},{4,5},{5,4},{6,7},{7,6},{8,9},{9,8},{10,11... | collective-permute-start | bytes 983048 | tf_op jit(solution)/shard_map/ppermute | solution.py:402
  241.2 14.0 %collective-permute-start.26 = (bf16[1,128,1280]{2,1,0:T(8,128)(2,1)}, bf16[1,128,1280]{2,1,0:T(8,128)(2,1)S(1)}, u32[]{:S(2)}, u32[]{:S(2)}) collective-permute-start(bf16[1,128,1280]{2,1,0:T(8,128)(2,1)} %get-tuple-element.325), channel_id=1, source_target_pairs={{0,1},{1,0},{2,3},{3,2},{4,5},{5,4},{6,7},{7,6},{8,9},{9,8},{10,11... | collective-permute-start | bytes 983048 | tf_op jit(solution)/shard_map/ppermute | solution.py:402
  251.6 9.5 %collective-permute-start.29 = (bf16[1,2,128,1280]{3,2,1,0:T(8,128)(2,1)}, bf16[1,2,128,1280]{3,2,1,0:T(8,128)(2,1)}, u32[]{:S(2)}, u32[]{:S(2)}) collective-permute-start(bf16[1,2,128,1280]{3,2,1,0:T(8,128)(2,1)} %pad_maximum_fusion.11), channel_id=1, source_target_pairs={{0,2},{2,0},{4,6},{6,4},{8,10},{10,8},{12,14},{14,12},{16,18},{18,... | collective-permute-start | bytes 1966088 | tf_op jit(solution)/shard_map/ppermute | solution.py:396
  292.2 204.0 %reduce-scatter.6.cloned.1.call-start = ((), (), s32[]{:S(2)}) async-start(), calls=%async_computation.6 | async-start | bytes 3686400 | tf_op jit(solution)/shard_map/reduce_scatter | solution.py:498
  292.5 11.2 %collective-permute-start.38 = (bf16[2,1,1280]{2,0,1:T(2,128)(2,1)S(1)}, bf16[2,1,1280]{2,0,1:T(2,128)(2,1)S(1)}, u32[]{:S(2)}, u32[]{:S(2)}) collective-permute-start(bf16[2,1,1280]{2,0,1:T(2,128)(2,1)S(1)} %fusion.114), channel_id=1, source_target_pairs={{0,1},{1,0},{2,3},{3,2},{4,5},{5,4},{6,7},{7,6},{8,9},{9,8},{10,11... | collective-permute-start | bytes 15368 | tf_op jit(solution)/shard_map/ppermute | solution.py:402
  303.7 9.6 %collective-permute-start.42 = (bf16[2,1280]{1,0:T(2,128)(2,1)S(1)}, bf16[2,1280]{1,0:T(2,128)(2,1)S(1)}, u32[]{:S(2)}, u32[]{:S(2)}) collective-permute-start(bf16[2,1280]{1,0:T(2,128)(2,1)S(1)} %bitcast.596), channel_id=1, source_target_pairs={{0,1},{1,0},{2,3},{3,2},{4,5},{5,4},{6,7},{7,6},{8,9},{9,8},{10,11... | collective-permute-start | bytes 15368 | tf_op jit(solution)/shard_map/ppermute | solution.py:402
  313.3 35.2 %collective-permute-start.35 = (bf16[2,2,128,1280]{3,2,0,1:T(8,128)(2,1)}, bf16[2,2,128,1280]{3,2,0,1:T(8,128)(2,1)}, u32[]{:S(2)}, u32[]{:S(2)}) collective-permute-start(bf16[2,2,128,1280]{3,2,0,1:T(8,128)(2,1)} %copy.516), channel_id=1, source_target_pairs={{0,2},{2,0},{4,6},{6,4},{8,10},{10,8},{12,14},{14,12},{16,18},{18,... | collective-permute-start | bytes 3932168 | tf_op jit(solution)/shard_map/ppermute | solution.py:396
  328.0 24.7 %collective-permute-start.39 = (bf16[2,2,128,1280]{3,2,0,1:T(8,128)(2,1)}, bf16[2,2,128,1280]{3,2,0,1:T(8,128)(2,1)}, u32[]{:S(2)}, u32[]{:S(2)}) collective-permute-start(bf16[2,2,128,1280]{3,2,0,1:T(8,128)(2,1)} %copy.515), channel_id=1, source_target_pairs={{0,2},{2,0},{4,6},{6,4},{8,10},{10,8},{12,14},{14,12},{16,18},{18,... | collective-permute-start | bytes 3932168 | tf_op jit(solution)/shard_map/ppermute | solution.py:396
  330.8 14.3 %collective-permute-start.58 = (bf16[4,24,1280]{2,1,0:T(8,128)(2,1)}, bf16[4,24,1280]{2,1,0:T(8,128)(2,1)}, u32[]{:S(2)}, u32[]{:S(2)}) collective-permute-start(bf16[4,24,1280]{2,1,0:T(8,128)(2,1)} %pad_maximum_fusion.20), channel_id=1, source_target_pairs={{0,16},{2,18},{4,20},{6,22},{8,24},{10,26},{12,28},{14,30},{16,0},... | collective-permute-start | bytes 737288 | tf_op jit(solution)/shard_map/ppermute | solution.py:396
  335.8 289.8 %reduce-scatter.8.cloned.1.call-start = ((), (), s32[]{:S(2)}) async-start(), calls=%async_computation.7 | async-start | bytes 3686400 | tf_op jit(solution)/shard_map/reduce_scatter | solution.py:498
  350.3 17.7 %collective-permute-start.36 = (bf16[2,128,1280]{2,1,0:T(8,128)(2,1)S(1)}, bf16[2,128,1280]{2,1,0:T(8,128)(2,1)S(1)}, u32[]{:S(2)}, u32[]{:S(2)}) collective-permute-start(bf16[2,128,1280]{2,1,0:T(8,128)(2,1)S(1)} %fusion.52), channel_id=1, source_target_pairs={{0,1},{1,0},{2,3},{3,2},{4,5},{5,4},{6,7},{7,6},{8,9},{9,8},{10,11... | collective-permute-start | bytes 1966088 | tf_op jit(solution)/shard_map/ppermute | solution.py:402
  354.7 35.4 %collective-permute-start.40 = (bf16[2,128,1280]{2,1,0:T(8,128)(2,1)}, bf16[2,128,1280]{2,1,0:T(8,128)(2,1)}, u32[]{:S(2)}, u32[]{:S(2)}) collective-permute-start(bf16[2,128,1280]{2,1,0:T(8,128)(2,1)} %fusion.53), channel_id=1, source_target_pairs={{0,1},{1,0},{2,3},{3,2},{4,5},{5,4},{6,7},{7,6},{8,9},{9,8},{10,11... | collective-permute-start | bytes 1966088 | tf_op jit(solution)/shard_map/ppermute | solution.py:402
  418.5 76.1 %collective-permute-start.52 = (bf16[2,128,1280]{2,1,0:T(8,128)(2,1)}, bf16[2,128,1280]{2,1,0:T(8,128)(2,1)}, u32[]{:S(2)}, u32[]{:S(2)}) collective-permute-start(bf16[2,128,1280]{2,1,0:T(8,128)(2,1)} %bitcast.108), channel_id=1, source_target_pairs={{0,1},{1,0},{2,3},{3,2},{4,5},{5,4},{6,7},{7,6},{8,9},{9,8},{10,11... | collective-permute-start | bytes 1966088 | tf_op jit(solution)/shard_map/ppermute | solution.py:402
  420.8 15.3 %collective-permute-start.47 = (bf16[1,2,1280]{2,1,0:T(2,128)(2,1)}, bf16[1,2,1280]{2,1,0:T(2,128)(2,1)}, u32[]{:S(2)}, u32[]{:S(2)}) collective-permute-start(bf16[1,2,1280]{2,1,0:T(2,128)(2,1)} %slice.1140), channel_id=1, source_target_pairs={{0,1},{1,0},{2,3},{3,2},{4,5},{5,4},{6,7},{7,6},{8,9},{9,8},{10,11... | collective-permute-start | bytes 15368 | tf_op jit(solution)/shard_map/ppermute | solution.py:402
  457.1 11.4 %collective-permute-start.60 = (bf16[2,24,1280]{2,1,0:T(8,128)(2,1)S(1)}, bf16[2,24,1280]{2,1,0:T(8,128)(2,1)S(1)}, u32[]{:S(2)}, u32[]{:S(2)}) collective-permute-start(bf16[2,24,1280]{2,1,0:T(8,128)(2,1)S(1)} %pad_maximum_fusion.23), channel_id=1, source_target_pairs={{0,8},{2,10},{4,12},{6,14},{8,0},{10,2},{12,4},{14,6},{16,24},{18,... | collective-permute-start | bytes 368648 | tf_op jit(solution)/shard_map/ppermute | solution.py:396
  459.3 12.3 %collective-permute-start.55 = (bf16[2,2,1,1280]{3,1,2,0:T(2,128)(2,1)S(1)}, bf16[2,2,1,1280]{3,1,2,0:T(2,128)(2,1)S(1)}, u32[]{:S(2)}, u32[]{:S(2)}) collective-permute-start(bf16[2,2,1,1280]{3,1,2,0:T(2,128)(2,1)S(1)} %pad_maximum_fusion.37), channel_id=1, source_target_pairs={{0,2},{2,0},{4,6},{6,4},{8,10},{10,8},{12,14},{14,12},{16,18},{18,... | collective-permute-start | bytes 30728 | tf_op jit(solution)/shard_map/ppermute | solution.py:396
  468.6 24.0 %collective-permute-start.61 = (bf16[4,24,1280]{2,1,0:T(8,128)(2,1)S(1)}, bf16[4,24,1280]{2,1,0:T(8,128)(2,1)S(1)}, u32[]{:S(2)}, u32[]{:S(2)}) collective-permute-start(bf16[4,24,1280]{2,1,0:T(8,128)(2,1)S(1)} %pad_maximum_fusion.21), channel_id=1, source_target_pairs={{0,16},{2,18},{4,20},{6,22},{8,24},{10,26},{12,28},{14,30},{16,0},... | collective-permute-start | bytes 737288 | tf_op jit(solution)/shard_map/ppermute | solution.py:396
  501.4 45.7 %collective-permute-start.83 = (bf16[2,3,80,1280]{3,2,1,0:T(8,128)(2,1)}, bf16[2,3,80,1280]{3,2,1,0:T(8,128)(2,1)}, u32[]{:S(2)}, u32[]{:S(2)}) collective-permute-start(bf16[2,3,80,1280]{3,2,1,0:T(8,128)(2,1)} %pad_maximum_fusion.7), channel_id=1, source_target_pairs={{0,1},{1,0},{2,3},{3,2},{4,5},{5,4},{6,7},{7,6},{8,9},{9,8},{10,11... | collective-permute-start | bytes 3686408 | tf_op jit(solution)/shard_map/ppermute | solution.py:402
  540.8 35.1 %collective-permute-start.63 = (bf16[2,2,128,1280]{3,2,0,1:T(8,128)(2,1)S(1)}, bf16[2,2,128,1280]{3,2,0,1:T(8,128)(2,1)S(1)}, u32[]{:S(2)}, u32[]{:S(2)}) collective-permute-start(bf16[2,2,128,1280]{3,2,0,1:T(8,128)(2,1)S(1)} %copy.514), channel_id=1, source_target_pairs={{0,2},{2,0},{4,6},{6,4},{8,10},{10,8},{12,14},{14,12},{16,18},{18,... | collective-permute-start | bytes 3932168 | tf_op jit(solution)/shard_map/ppermute | solution.py:396
  545.3 13.4 %collective-permute-start.66 = (bf16[2,320,320]{2,1,0:T(8,128)(2,1)S(1)}, bf16[2,320,320]{2,1,0:T(8,128)(2,1)S(1)}, u32[]{:S(2)}, u32[]{:S(2)}) collective-permute-start(bf16[2,320,320]{2,1,0:T(8,128)(2,1)S(1)} %pad_maximum_fusion.16), channel_id=1, source_target_pairs={{0,1},{1,0},{2,3},{3,2},{4,5},{5,4},{6,7},{7,6},{8,9},{9,8},{10,11... | collective-permute-start | bytes 1228808 | tf_op jit(solution)/shard_map/ppermute | solution.py:402
  576.0 17.0 %collective-permute-start.64 = (bf16[2,128,1280]{2,1,0:T(8,128)(2,1)S(1)}, bf16[2,128,1280]{2,1,0:T(8,128)(2,1)S(1)}, u32[]{:S(2)}, u32[]{:S(2)}) collective-permute-start(bf16[2,128,1280]{2,1,0:T(8,128)(2,1)S(1)} %fusion.54), channel_id=1, source_target_pairs={{0,1},{1,0},{2,3},{3,2},{4,5},{5,4},{6,7},{7,6},{8,9},{9,8},{10,11... | collective-permute-start | bytes 1966088 | tf_op jit(solution)/shard_map/ppermute | solution.py:402
  601.8 10.1 %collective-permute-start.79 = (bf16[80,1280]{1,0:T(8,128)(2,1)S(1)}, bf16[80,1280]{1,0:T(8,128)(2,1)S(1)}, u32[]{:S(2)}, u32[]{:S(2)}) collective-permute-start(bf16[80,1280]{1,0:T(8,128)(2,1)S(1)} %get-tuple-element.246), channel_id=1, source_target_pairs={{0,4},{2,6},{8,0},{10,2},{16,8},{18,10},{24,16},{26,18},{28,24},{3... | collective-permute-start | bytes 614408 | tf_op jit(solution)/shard_map/ppermute | solution.py:486
  623.2 12.7 %collective-permute-start.82 = (bf16[2,80,1280]{2,1,0:T(8,128)(2,1)S(1)}, bf16[2,80,1280]{2,1,0:T(8,128)(2,1)S(1)}, u32[]{:S(2)}, u32[]{:S(2)}) collective-permute-start(bf16[2,80,1280]{2,1,0:T(8,128)(2,1)S(1)} %pad_maximum_fusion.18), channel_id=1, source_target_pairs={{0,1},{1,0},{2,3},{3,2},{4,5},{5,4},{6,7},{7,6},{8,9},{9,8},{10,11... | collective-permute-start | bytes 1228808 | tf_op jit(solution)/shard_map/ppermute | solution.py:402
  628.2 16.3 %collective-permute-start.90 = (bf16[2,80,1280]{2,1,0:T(8,128)(2,1)S(1)}, bf16[2,80,1280]{2,1,0:T(8,128)(2,1)S(1)}, u32[]{:S(2)}, u32[]{:S(2)}) collective-permute-start(bf16[2,80,1280]{2,1,0:T(8,128)(2,1)S(1)} %pad_maximum_fusion.19), channel_id=1, source_target_pairs={{0,1},{1,0},{2,3},{3,2},{4,5},{5,4},{6,7},{7,6},{8,9},{9,8},{10,11... | collective-permute-start | bytes 1228808 | tf_op jit(solution)/shard_map/ppermute | solution.py:402
  (180 other events, 1850.9 us)
Sparse Core Ops, SparseCore 0:
  82.0 63.8 all-gather.2
  152.3 101.0 all-gather.4
  292.3 75.7 reduce-scatter.3
  372.0 75.1 reduce-scatter.5
  450.6 85.8 reduce-scatter.7

commit v2 on v1

v2 whole, which is shorter than its diff:
```python
import functools

import jax
import jax.numpy as jnp
from jax import lax
from jax.experimental import pallas as pl
from jax.experimental.pallas import tpu as pltpu
from jax.sharding import PartitionSpec as P

HEAD = 64
EPSILON = 1e-05
F32 = jnp.float32
BF16 = jnp.bfloat16


def product(left, right):
    return jnp.dot(left, right, preferred_element_type=F32)


def row_product(left, right):
    return lax.dot_general(left, right, (((0,), (0,)), ((), ())), preferred_element_type=F32)


def times_transpose(left, right):
    return lax.dot_general(left, right, (((1,), (1,)), ((), ())), preferred_element_type=F32)


def layer_stats(values):
    average = jnp.mean(values, axis=-1, keepdims=True)
    centred = values - average
    variance = jnp.mean(centred * centred, axis=-1, keepdims=True)
    inverse = lax.rsqrt(variance + EPSILON)
    return (centred * inverse, inverse)


def norm_back(grad_scaled, gain, normal, inverse):
    grad_normal = grad_scaled * gain
    along_normal = jnp.mean(grad_normal * normal, axis=-1, keepdims=True)
    average = jnp.mean(grad_normal, axis=-1, keepdims=True)
    grad_values = inverse * (grad_normal - average - normal * along_normal)
    return (grad_values, jnp.sum(grad_scaled * normal, axis=0))


def norm_kernel(gain_ref, *refs):
    sources, out_ref = refs[:-1], refs[-1]
    micro, length, _ = sources[0].shape
    for batch in range(micro):
        for i, source in enumerate(sources):
            normal, _ = layer_stats(source[batch].astype(F32))
            start = (batch * len(sources) + i) * length
            out_ref[start : start + length, :] = (normal * gain_ref[...]).astype(BF16)


def norm_four(sources, gain):
    micro, length, model = sources[0].shape
    rows = len(sources) * micro * length
    whole = pl.BlockSpec(memory_space=pltpu.VMEM)
    return pl.pallas_call(
        norm_kernel,
        in_specs=[whole] * (1 + len(sources)),
        out_specs=whole,
        out_shape=jax.ShapeDtypeStruct((rows, model), BF16),
        cost_estimate=pl.CostEstimate(
            flops=8 * rows * model, bytes_accessed=4 * rows * model, transcendentals=rows
        ),
        compiler_params=pltpu.CompilerParams(vmem_limit_bytes=32 << 20),
    )(gain[None], *sources)


def softmax_all(scores):
    shifted = [jnp.exp(value - jnp.max(value, axis=-1, keepdims=True)) for value in scores]
    return [value * (1.0 / jnp.sum(value, axis=-1, keepdims=True)) for value in shifted]


def heads_of(ref, width, part):
    return [ref[:, part * width + i : part * width + i + HEAD] for i in range(0, width, HEAD)]


def attend_kernel(projected_ref, mixed_ref):
    width = mixed_ref.shape[1]
    queries, keys, values = (heads_of(projected_ref, width, part) for part in range(3))
    probs = softmax_all([times_transpose(q, k) * 0.125 for q, k in zip(queries, keys)])
    mixed = [product(p.astype(BF16), v).astype(BF16) for p, v in zip(probs, values)]
    for i, value in enumerate(mixed):
        mixed_ref[:, i * HEAD : (i + 1) * HEAD] = value


def attend_back_kernel(projected_ref, grad_mixed_ref, first_ref, grad_ref):
    width = grad_mixed_ref.shape[1]
    is_first = lax.broadcasted_iota(jnp.int32, (grad_mixed_ref.shape[0], width), 0) == 0
    grad_ref[:, 0:width] = jnp.where(is_first, first_ref[0], grad_mixed_ref[...])
    grads = heads_of(grad_ref, width, 0)
    queries, keys, values = (heads_of(projected_ref, width, part) for part in range(3))
    scores = [times_transpose(q, k) * 0.125 for q, k in zip(queries, keys)]
    grad_probs = [times_transpose(g, v) for g, v in zip(grads, values)]
    probs = softmax_all(scores)
    grad_values = [row_product(p.astype(BF16), g) for p, g in zip(probs, grads)]
    along = [jnp.sum(g * p, axis=-1, keepdims=True) for g, p in zip(grad_probs, probs)]
    grad_scores = [
        (p * (g - a) * 0.125).astype(BF16) for p, g, a in zip(probs, grad_probs, along)
    ]
    grad_queries = [product(g, k) for g, k in zip(grad_scores, keys)]
    grad_keys = [row_product(g, q) for g, q in zip(grad_scores, queries)]
    for part, parts in enumerate((grad_queries, grad_keys, grad_values)):
        for i, value in enumerate(parts):
            start = part * width + i * HEAD
            grad_ref[:, start : start + HEAD] = value.astype(BF16)


def attend(projected, length, first, count):
    rows, wide = count * length, projected.shape[1]
    return pl.pallas_call(
        attend_kernel,
        grid=(count,),
        in_specs=[pl.BlockSpec((length, wide), lambda i: (first + i, 0))],
        out_specs=pl.BlockSpec((length, wide // 3), lambda i: (i, 0)),
        out_shape=jax.ShapeDtypeStruct((rows, wide // 3), BF16),
        cost_estimate=pl.CostEstimate(
            flops=4 * rows * length * wide // 3,
            bytes_accessed=rows * wide * 3,
            transcendentals=rows * length * wide // 3 // HEAD,
        ),
    )(projected)


def attend_back(projected, grad_mixed, first, length):
    rows, wide = projected.shape
    return pl.pallas_call(
        attend_back_kernel,
        grid=(rows // length,),
        in_specs=[
            pl.BlockSpec((length, wide), lambda i: (i, 0)),
            pl.BlockSpec((length, wide // 3), lambda i: (i, 0)),
            pl.BlockSpec((1, 1, wide // 3), lambda i: (i, 0, 0)),
        ],
        out_specs=pl.BlockSpec((length, wide), lambda i: (i, 0)),
        out_shape=jax.ShapeDtypeStruct((rows, wide), BF16),
        cost_estimate=pl.CostEstimate(
            flops=10 * rows * length * wide // 3,
            bytes_accessed=rows * wide * 5,
            transcendentals=rows * length * wide // 3 // HEAD,
        ),
    )(projected, grad_mixed, first)


def ring_chip(position, chips):
    position = lax.rem(position + 2 * chips, chips)
    return jnp.where(position < chips // 2, 2 * position, 2 * (chips - 1 - position) + 1)


def place_kernel(segments, position_ref, *refs):
    outs, sems = refs[-1 - len(segments) : -1], refs[-1]
    count = (len(refs) - 1 - len(segments)) // 2
    copies = []
    for step in range(count):
        for side in range(2):
            piece = refs[2 * step + side]
            source = ring_chip(position_ref[0] + (step if side else -step), count)
            begin = 0
            for out, rows in zip(outs, segments):
                start = pl.multiple_of((2 * source + side) * rows, rows)
                copies.append(
                    pltpu.make_async_copy(
                        piece.at[pl.ds(begin, rows), :], out.at[pl.ds(start, rows), :], sems.at[len(copies)]
                    )
                )
                begin += rows
    for copy in copies:
        copy.start()
    for copy in copies:
        copy.wait()


def place(pieces, position, segments):
    tall, wide = pieces[0].shape
    whole = pl.BlockSpec(memory_space=pltpu.VMEM)
    return pl.pallas_call(
        functools.partial(place_kernel, segments),
        in_specs=[pl.BlockSpec(memory_space=pltpu.SMEM)]
        + [pl.BlockSpec(memory_space=pl.ANY)] * len(pieces),
        out_specs=[whole] * len(segments),
        scratch_shapes=[pltpu.SemaphoreType.DMA((len(pieces) * len(segments),))],
        out_shape=[jax.ShapeDtypeStruct((len(pieces) * rows, wide), BF16) for rows in segments],
        cost_estimate=pl.CostEstimate(
            flops=0, bytes_accessed=4 * len(pieces) * tall * wide, transcendentals=0
        ),
        compiler_params=pltpu.CompilerParams(vmem_limit_bytes=32 << 20),
    )(position.reshape(1), *pieces)


def column_places(kind, part, n_dp):
    if kind == "attention":
        model = 4 * part
        return [
            [(0, i * model + k * part, i * part, part) for i in range(3)] + [(1, k * part, 3 * part, part)]
            for k in range(4)
        ]
    width = part // n_dp
    return [[(0, (4 * i + k) * width, i * width, width) for i in range(n_dp)] for k in range(4)]


def join_kernel(places, index_ref, *refs):
    blocks = [ref[...].astype(F32) for ref in refs[:4]]
    core, half = index_ref[0], index_ref[1]

    def swap(index, i, j):
        first = jnp.where(index == 0, blocks[i], blocks[j])
        blocks[j] = jnp.where(index == 0, blocks[j], blocks[i])
        blocks[i] = first

    swap(core, 0, 1)
    swap(core, 2, 3)
    swap(half, 0, 2)
    swap(half, 1, 3)
    for block, moves in zip(blocks, places):
        for output, start, source, width in moves:
            refs[4 + output][:, start : start + width] = block[:, source : source + width]


def join(blocks, index, places, widths):
    rows = blocks[0].shape[0]
    whole = pl.BlockSpec(memory_space=pltpu.VMEM)
    return pl.pallas_call(
        functools.partial(join_kernel, places),
        in_specs=[pl.BlockSpec(memory_space=pltpu.SMEM)] + [whole] * 4,
        out_specs=[whole] * len(widths),
        out_shape=[jax.ShapeDtypeStruct((rows, width), F32) for width in widths],
        cost_estimate=pl.CostEstimate(
            flops=0, bytes_accessed=6 * rows * sum(widths), transcendentals=0
        ),
        compiler_params=pltpu.CompilerParams(vmem_limit_bytes=32 << 20),
    )(index, *blocks)


def split_attention_kernel(index_ref, qkv_ref, out_ref, *refs):
    vectors, targets = refs[:-2], refs[-2:]
    rows, part = out_ref.shape[0], out_ref.shape[1] // 4
    for k in range(4):
        for flip, target in enumerate(targets):

            @pl.when(index_ref[0] == k ^ flip)
            def _():
                for i in range(3):
                    target[0:rows, i * part : (i + 1) * part] = qkv_ref[
                        :, (4 * i + k) * part : (4 * i + k + 1) * part
                    ]
                target[0:rows, 3 * part :] = out_ref[:, k * part : (k + 1) * part]

    for target in targets:
        start = 0
        for vector in vectors:
            width = vector.shape[0]
            target[rows : rows + 1, start : start + width] = vector[...].reshape(1, width)
            start += width


def split_attention(qkv_weight, out_weight, vectors, quarter):
    rows, model = out_weight.shape
    whole = pl.BlockSpec(memory_space=pltpu.VMEM)
    return pl.pallas_call(
        split_attention_kernel,
        in_specs=[pl.BlockSpec(memory_space=pltpu.SMEM)] + [whole] * (2 + len(vectors)),
        out_specs=[whole] * 2,
        out_shape=[jax.ShapeDtypeStruct((rows + 8, model), BF16)] * 2,
        cost_estimate=pl.CostEstimate(
            flops=0, bytes_accessed=12 * rows * model, transcendentals=0
        ),
    )(quarter.reshape(1), qkv_weight, out_weight, *vectors)


def split_rest_kernel(n_dp, index_ref, up_ref, down_ref, cell_ref, gene_ref, *targets):
    wide = cell_ref.shape[1] // 4
    cut = down_ref.shape[0] // 4
    width = wide // n_dp
    for flip in range(2):
        up, down, decoder = targets[flip::2]
        start = pl.multiple_of((index_ref[0] ^ flip) * cut, cut)
        down[...] = down_ref[pl.ds(start, cut), :]
        for k in range(4):

            @pl.when(index_ref[0] == k ^ flip)
            def _():
                for i in range(n_dp):
                    up[:, i * width : (i + 1) * width] = up_ref[
                        :, (4 * i + k) * width : (4 * i + k + 1) * width
                    ]
                decoder[:, :wide] = cell_ref[:, k * wide : (k + 1) * wide]
                decoder[:, wide:] = gene_ref[:, k * wide : (k + 1) * wide]


def split_rest(up_weight, down_weight, cell_weight, gene_weight, quarter, n_dp):
    rows, wide = cell_weight.shape[0], cell_weight.shape[1] // 4
    whole = pl.BlockSpec(memory_space=pltpu.VMEM)
    narrow = jax.ShapeDtypeStruct((rows, wide), BF16)
    shorter = jax.ShapeDtypeStruct((down_weight.shape[0] // 4, down_weight.shape[1]), BF16)
    return pl.pallas_call(
        functools.partial(split_rest_kernel, n_dp),
        in_specs=[pl.BlockSpec(memory_space=pltpu.SMEM)] + [whole] * 4,
        out_specs=[whole] * 6,
        out_shape=[narrow] * 2 + [shorter] * 2 + [jax.ShapeDtypeStruct((rows, 2 * wide), BF16)] * 2,
        cost_estimate=pl.CostEstimate(
            flops=0, bytes_accessed=40 * rows * wide, transcendentals=0
        ),
        compiler_params=pltpu.CompilerParams(vmem_limit_bytes=32 << 20),
    )(quarter.reshape(1), up_weight, down_weight, cell_weight, gene_weight)


def first_kernel(*refs):
    count = len(refs) // 2
    for source, target in zip(refs[:count], refs[count:]):
        for i in range(source.shape[0]):
            target[i : i + 1, :] = source[i, 0:1, :]


def first_rows_of(values, length):
    cells = values[0].shape[0] // length
    values = [value.reshape(cells, length, value.shape[1]) for value in values]
    specs = [pl.BlockSpec((cells, 16, value.shape[2]), lambda i: (0, 0, 0)) for value in values]
    outs = [pl.BlockSpec((cells, value.shape[2]), lambda i: (0, 0)) for value in values]
    return pl.pallas_call(
        first_kernel,
        grid=(1,),
        in_specs=specs,
        out_specs=outs,
        out_shape=[jax.ShapeDtypeStruct((cells, value.shape[2]), value.dtype) for value in values],
        cost_estimate=pl.CostEstimate(
            flops=0, bytes_accessed=64 * cells * sum(value.shape[2] for value in values), transcendentals=0
        ),
    )(*values)


def pack_kernel(room, index_ref, starts_ref, *refs):
    sources, out_ref = refs[:-1], refs[-1]
    micro = len(sources) // 4
    slots = sources[0].shape[0]
    for pair in range(2):
        for batch in range(micro):
            segment = (batch * 2 + pair) * room
            start = starts_ref[batch * 2 + pair]

            def put(first, second):
                kept = min(room, slots)
                out_ref[segment : segment + kept, :] = first[0:kept, :]

                def move(i, carry):
                    source = pl.multiple_of(jnp.minimum(i * 16, slots - 16), 16)
                    target = pl.multiple_of(segment + start + i * 16, 16)
                    out_ref[pl.ds(target, 16), :] = second[pl.ds(source, 16), :]
                    return carry

                lax.fori_loop(0, (room - start) // 16, move, 0)

            own = sources[2 * pair * micro + batch]
            far = sources[(2 * pair + 1) * micro + batch]
            pl.when(index_ref[1] == 0)(functools.partial(put, own, far))
            pl.when(index_ref[1] == 1)(functools.partial(put, far, own))


def pack(sources, index, starts, room):
    model = sources[0].shape[1]
    whole = pl.BlockSpec(memory_space=pltpu.VMEM)
    scalars = pl.BlockSpec(memory_space=pltpu.SMEM)
    total = len(sources) // 2 * room
    return pl.pallas_call(
        functools.partial(pack_kernel, room),
        in_specs=[scalars, scalars] + [whole] * len(sources),
        out_specs=whole,
        out_shape=jax.ShapeDtypeStruct((total, model), BF16),
        cost_estimate=pl.CostEstimate(flops=0, bytes_accessed=5 * total * model, transcendentals=0),
        compiler_params=pltpu.CompilerParams(vmem_limit_bytes=40 << 20),
    )(index, starts, *sources)


def facts_kernel(live_ref, cell_ref, label_ref, out_ref):
    micro, slots = cell_ref.shape
    lane = lax.broadcasted_iota(jnp.int32, (1, slots), 1)
    for batch in range(micro):
        out_ref[batch, 0:1, :] = cell_ref[batch : batch + 1, :].astype(F32)
        out_ref[batch, 1:2, :] = label_ref[batch : batch + 1, :].astype(F32)
        out_ref[batch, 2:3, :] = (lane < live_ref[batch]).astype(F32)
        out_ref[batch, 3:8, :] = jnp.full((5, slots), live_ref[batch], jnp.int32).astype(F32)


def facts_of(live, cell, label):
    whole = pl.BlockSpec(memory_space=pltpu.VMEM)
    return pl.pallas_call(
        facts_kernel,
        in_specs=[pl.BlockSpec(memory_space=pltpu.SMEM)] + [whole] * 2,
        out_specs=whole,
        out_shape=jax.ShapeDtypeStruct((cell.shape[0], 8, cell.shape[1]), F32),
        cost_estimate=pl.CostEstimate(flops=0, bytes_accessed=40 * cell.size, transcendentals=0),
    )(live, cell, label)


def line_kernel(index_ref, starts_ref, *refs):
    sources, out_ref = refs[:4], refs[4]
    micro, facts, slots = sources[0].shape
    room = out_ref.shape[3]
    wide = -(-(room + slots) // 128) * 128
    lane = lax.broadcasted_iota(jnp.int32, (facts, wide), 1)
    beyond = jnp.zeros((facts, wide - slots), F32)
    for batch in range(micro):
        for pair in range(2):
            own, far = sources[2 * pair][batch], sources[2 * pair + 1][batch]
            first = jnp.where(index_ref[1] == 0, own, far)
            second = jnp.where(index_ref[1] == 0, far, own)
            start = starts_ref[2 * batch + pair]
            moved = pltpu.roll(jnp.concatenate([second, beyond], axis=1), start, 1)
            line = jnp.where(lane < start, jnp.concatenate([first, beyond], axis=1), moved)
            out_ref[batch, pair] = line[:, :room]


def line_up(sources, index, starts, room):
    micro, facts, slots = sources[0].shape
    whole = pl.BlockSpec(memory_space=pltpu.VMEM)
    scalars = pl.BlockSpec(memory_space=pltpu.SMEM)
    return pl.pallas_call(
        functools.partial(line_kernel),
        in_specs=[scalars, scalars] + [whole] * 4,
        out_specs=whole,
        out_shape=jax.ShapeDtypeStruct((micro, 2, facts, room), F32),
        cost_estimate=pl.CostEstimate(
            flops=0, bytes_accessed=64 * micro * facts * slots, transcendentals=0
        ),
    )(index, starts, *sources)


def paste_kernel(index_ref, qkv_ref, *refs):
    blocks = [ref[...] for ref in refs[:4]]
    out_ref = refs[4]
    core, half = index_ref[0], index_ref[1]
    wide, part = qkv_ref.shape[1], blocks[0].shape[0]

    def swap(index, i, j):
        first = jnp.where(index == 0, blocks[i], blocks[j])
        blocks[j] = jnp.where(index == 0, blocks[j], blocks[i])
        blocks[i] = first

    swap(core, 0, 1)
    swap(core, 2, 3)
    swap(half, 0, 2)
    swap(half, 1, 3)
    out_ref[:, 0:wide] = qkv_ref[...]
    for i, block in enumerate(blocks):
        out_ref[i * part : (i + 1) * part, wide:] = block


def paste(grad_qkv, blocks, index):
    rows, wide = grad_qkv.shape
    whole = pl.BlockSpec(memory_space=pltpu.VMEM)
    return pl.pallas_call(
        paste_kernel,
        in_specs=[pl.BlockSpec(memory_space=pltpu.SMEM)] + [whole] * 5,
        out_specs=whole,
        out_shape=jax.ShapeDtypeStruct((rows, wide + blocks[0].shape[1]), BF16),
        cost_estimate=pl.CostEstimate(
            flops=0, bytes_accessed=6 * rows * wide, transcendentals=0
        ),
        compiler_params=pltpu.CompilerParams(vmem_limit_bytes=32 << 20),
    )(index, grad_qkv, *blocks)


def shards(
    n_dp,
    n_query,
    tokens,
    out_cotangent,
    qkv_weight,
    out_weight,
    up_weight,
    down_weight,
    attn_gain,
    ffn_gain,
    up_bias,
    cell_weight,
    gene_weight,
    decoder_bias,
    readout,
    gene_embed,
    query_cell,
    query_label,
    query_live,
):
    micro, _, length, model = tokens.shape
    slots = gene_embed.shape[2]
    chips = n_dp // 2
    shard = model // n_dp
    ff_shard = up_bias.shape[0]
    dh_shard = decoder_bias.shape[0]
    part = model // 4
    ff_part = ff_shard * n_dp // 4
    dh_part = dh_shard * n_dp // 4
    room = 2 * slots if n_query > 2 else (2 * slots * 5 // 8 + 15) // 16 * 16 + 16
    dp_index = lax.axis_index("dp").astype(jnp.int32)
    query_index = lax.axis_index("query").astype(jnp.int32)
    core = dp_index % 2
    half = query_index % 2
    quarter = 2 * half + core
    index = jnp.stack([core, half])
    chip = dp_index // 2
    position = jnp.where(chip % 2 == 0, chip // 2, chips - 1 - chip // 2)
    ring = [2 * i for i in range(chips // 2)] + [2 * i + 1 for i in reversed(range(chips // 2))]
    same_line = [[4 * i + k for i in range(n_dp // 4)] for k in range(4)]
    same_core = [[2 * i + k for i in range(chips)] for k in range(2)]
    chip_bits = [1 << i for i in range(1, n_dp.bit_length() - 1)]
    query_bits = [1 << i for i in range(n_query.bit_length() - 1)]

    def ring_moves(step):
        return [
            (2 * ring[i] + k, 2 * ring[(i + step) % chips] + k) for i in range(chips) for k in range(2)
        ]

    ahead, behind = ring_moves(1), ring_moves(-1)

    def dp_swap(value, bit):
        return lax.ppermute(value, "dp", [(i, i ^ bit) for i in range(n_dp)])

    def core_swap(value):
        return dp_swap(value, 1)

    def query_swap(value, bit=1):
        return lax.ppermute(value, "query", [(i, i ^ bit) for i in range(n_query)])

    def gather_four(value):
        near = jnp.stack([value, query_swap(value)], axis=1)
        return jnp.concatenate([near, core_swap(near)], axis=1)

    def scatter_four(value, batches):
        blocks = value.reshape((batches, 4, -1) + value.shape[1:])
        received = core_swap(blocks[:, 2:].astype(BF16))
        far = query_swap((blocks[:, 1] + received[:, 1].astype(F32)).astype(BF16))
        total = blocks[:, 0] + received[:, 0].astype(F32) + far.astype(F32)
        return total.reshape((-1,) + value.shape[1:])

    def order(which, first, second):
        return jnp.where(which == 0, first, second), jnp.where(which == 0, second, first)

    def by_quarter(a, b, c, d):
        a, b = order(core, a, b)
        c, d = order(core, c, d)
        a, c = order(half, a, c)
        b, d = order(half, b, d)
        return [a, b, c, d]

    def exchange_four(blocks):
        own, near, far, both = by_quarter(*blocks)
        theirs = core_swap(jnp.stack([near, both]))
        beyond = query_swap(jnp.stack([far, theirs[1]]))
        return own, theirs[0], beyond[0], beyond[1]

    def ring_start(mine, theirs):
        low, high = order(core, mine, core_swap(theirs))
        return [low, high]

    def last(held):
        return tuple(held[-2:])

    def pin(value, *events):
        return lax.optimization_barrier((value, *events))[0]

    def ring_step(held, *events):
        if len(held) < 2 * chips:
            low, high = lax.optimization_barrier((*last(held), *events))[:2]
            held.append(lax.ppermute(low, "dp", ahead))
            held.append(lax.ppermute(high, "dp", behind))

    def other_pairs(value):
        for bit in query_bits[1:]:
            value = value + query_swap(value, bit)
        return value

    def to_owner(low, high):
        mine, theirs = order(core, low, high)
        theirs = core_swap(theirs)
        far = query_swap(jnp.stack([mine, theirs]))
        return mine, theirs, far[0], far[1]

    def cores(rows):
        return rows[:shard], rows[shard:]

    def chip_rows(mine, theirs):
        return jnp.concatenate(order(core, mine, core_swap(theirs)))

    def plane_gather(rows):
        return lax.all_gather(rows, "dp", axis=0, tiled=True, axis_index_groups=same_core)

    def plane_scatter(grads):
        return lax.psum_scatter(
            grads, "dp", scatter_dimension=0, tiled=True, axis_index_groups=same_core
        )

    def ring_scatter(grads, *lines):
        rows = grads.shape[0] // n_dp

        def piece(offset, side):
            start = (2 * ring_chip(position + offset, chips) + side) * rows
            return lax.dynamic_slice(grads, (start, 0), (rows, grads.shape[1]))

        low, high = piece(-1, 0), piece(1, 1)
        events = ()
        for step in range(1, chips):
            low = lax.ppermute(low, "dp", ahead)
            high = lax.ppermute(high, "dp", behind)
            low = (low.astype(F32) + piece(-1 - step, 0).astype(F32)).astype(BF16)
            high = (high.astype(F32) + piece(1 + step, 1).astype(F32)).astype(BF16)
            low, high = lax.optimization_barrier((low, high, *events))[:2]
            events = ()
            for line in lines:
                events += tuple(line[step - 1](low)) if step <= len(line) else ()
        for line in lines:
            for work in line[chips - 1 :]:
                work(low)
        return other_pairs(low), other_pairs(high)

    def y_half(grads, which):
        held = grads.reshape(-1, 2, 2 * shard, grads.shape[1])
        held = lax.dynamic_index_in_dim(held, which, 1, keepdims=False)
        return held.reshape(-1, grads.shape[1])

    def y_sum(grads, far):
        return (y_half(grads, chip % 2).astype(F32) + far.astype(F32)).astype(BF16)

    def line_scatter(total):
        return lax.psum_scatter(
            total, "dp", scatter_dimension=0, tiled=True, axis_index_groups=same_line
        )

    def group_sum(values):
        values = values + core_swap(values)[:, ::-1]
        return values + query_swap(values)

    first_ring = ring_start(
        *split_attention(
            qkv_weight, out_weight, [attn_gain, ffn_gain, up_bias, decoder_bias, readout], quarter
        )
    )
    ring_step(first_ring)
    pieces = split_rest(
        pin(up_weight, *first_ring[:2]), down_weight, cell_weight, gene_weight, quarter, n_dp
    )
    tokens_far = query_swap(tokens[:, 0])
    cotangent_far = query_swap(pin(out_cotangent, tokens_far)[:, 0])
    gene_own = [gene_embed[batch, 0] for batch in range(micro)]
    gene_far = [query_swap(pin(value, tokens_far)) for value in gene_own]

    def with_cores(own, far):
        near = jnp.stack([own, far], axis=1)
        return jnp.concatenate([near, core_swap(near)], axis=1).reshape(-1, model)

    own_tokens = tokens[:, 0].reshape(micro * length, model)
    for step in range(2, chips):
        arrived = {2: (tokens_far,), chips - 3: (cotangent_far,), chips - 1: (gene_far[0],)}.get(step, ())
        ring_step(first_ring, *arrived)
        if step == chips - 1:
            rows = [pin(chip_rows(*pieces[2 * i : 2 * i + 2]), *last(first_ring)) for i in range(3)]
            up_part, down_part, decoder_part = (plane_gather(value) for value in rows)
        if step == 3:
            all_tokens = [tokens[:, 0], tokens_far]
            all_tokens += [core_swap(value) for value in all_tokens]
    attention_part, vectors = place(first_ring, position, (shard, 8))
    vectors = vectors.reshape(n_dp, 8, model)[:, 0].astype(F32)
    bounds = [0, shard, 2 * shard, 2 * shard + ff_shard, 2 * shard + ff_shard + dh_shard]
    bounds.append(bounds[-1] + dh_shard)
    pieces = [vectors[:, low:high] for low, high in zip(bounds[:-1], bounds[1:])]
    attn_gain_all = pieces[0].reshape(model)
    qkv_part = attention_part[:, : 3 * part]
    out_blocks = attention_part[:, 3 * part :].reshape(4, part, part)
    out_part = jnp.concatenate(
        by_quarter(*exchange_four([out_blocks[i] for i in range(4)])), axis=1
    )

    normed = norm_four(all_tokens, attn_gain_all)
    projected = product(normed, qkv_part).astype(BF16)
    projected = pin(projected, gene_far[-1])
    own_wide = own_tokens.astype(F32)
    mixed, second, hidden, norm_two, scale_two = [], [], [], [], []
    for batch in range(micro):
        mixed.append(attend(projected, length, 4 * batch, 4))
        if batch == 0:
            pieces = [pin(piece, mixed[0]) for piece in pieces]
        partial = product(mixed[-1], out_part)
        projected = pin(projected, partial)
        hidden.append(own_wide[batch * length : (batch + 1) * length] + scatter_four(partial, 1))
    all_cotangent = with_cores(out_cotangent[:, 0], pin(cotangent_far, partial))
    facts = [facts_of(pin(query_live[0, :, 0], partial), query_cell[:, 0], query_label[:, 0])]
    facts.append(query_swap(facts[0]))
    facts += [core_swap(value) for value in facts]
    counts = [jnp.where(half == 0, facts[i][:, 3, 0], facts[i + 1][:, 3, 0]) for i in (0, 2)]
    starts = (jnp.stack(counts, axis=1).reshape(-1).astype(jnp.int32) + 15) // 16 * 16
    facts = line_up(facts, index, starts, room)
    facts = [facts[:, :, i] for i in range(3)]
    gene_near = [pin(value, partial) for value in gene_own + gene_far]
    gene_rows = pack(gene_near + [core_swap(value) for value in gene_near], index, starts, room)
    ffn_gain_all = pieces[1].reshape(model)
    up_bias_part = lax.dynamic_index_in_dim(
        pieces[2].reshape(n_dp, 4, ff_shard // 4), quarter, 1, keepdims=False
    ).reshape(ff_part)
    decoder_bias_part = lax.dynamic_slice(pieces[3].reshape(-1), (quarter * dh_part,), (dh_part,))
    readout_part = lax.dynamic_slice(pieces[4].reshape(-1), (quarter * dh_part,), (dh_part,))
    for batch in range(micro):
        normal, scale = layer_stats(hidden[batch])
        norm_two.append(normal)
        scale_two.append(scale)
        second.append(gather_four((normal * ffn_gain_all).astype(BF16)[None]))
    hidden, norm_two, scale_two = (jnp.concatenate(parts) for parts in (hidden, norm_two, scale_two))
    second = jnp.concatenate(second).reshape(-1, model)
    mixed = jnp.concatenate(mixed)
    up_proj = product(pin(second, gene_rows), up_part) + up_bias_part
    active = jax.nn.gelu(up_proj, approximate=True).astype(BF16)
    branch = product(active, down_part)

    (first_branch_out,) = first_rows_of([branch], length)

    def first_of(rows):
        return rows.reshape((-1, length) + rows.shape[1:])[:, 0]

    first_output = first_of(hidden) + scatter_four(first_branch_out, micro)
    output = (hidden + scatter_four(branch, micro)).reshape(micro, length, model)
    block_out = output.astype(BF16).at[:, 0].set(first_output.astype(BF16))

    gelu_back = jax.vjp(lambda inner: jax.nn.gelu(inner, approximate=True), up_proj)[1]
    grad_down_part = row_product(pin(active, branch), all_cotangent).astype(BF16)
    down_sent = y_half(grad_down_part, 1 - chip % 2)
    down_far = dp_swap(down_sent, 2)
    cotangent_in = pin(all_cotangent, down_sent)
    grad_up_proj = gelu_back(times_transpose(cotangent_in, down_part))[0].astype(BF16)
    grad_up_part = row_product(second, grad_up_proj).astype(BF16)
    up_sent = y_half(grad_up_part, 1 - chip % 2)
    up_far = dp_swap(up_sent, 2)
    grad_second = times_transpose(pin(grad_up_proj, up_sent), up_part)
    grad_second = scatter_four(grad_second, micro)
    down_total = y_sum(grad_down_part, down_far)
    grad_second = pin(grad_second, down_total)
    down_total = line_scatter(down_total)
    cell_part, gene_part = decoder_part[:, :dh_part], decoder_part[:, dh_part:]
    grad_hidden_norm, grad_ffn_gain = norm_back(grad_second, ffn_gain_all, norm_two, scale_two)
    own_cotangent = out_cotangent[:, 0].reshape(micro * length, model).astype(F32)
    grad_hidden = own_cotangent + grad_hidden_norm

    attn_own = grad_hidden.astype(BF16).reshape(micro, length, model)
    attn_far = query_swap(attn_own)

    summaries = first_output.astype(BF16)
    for bit in query_bits:
        summaries = jnp.stack([summaries, query_swap(summaries, bit)])
    summaries = jnp.stack([summaries, core_swap(summaries)])
    cells = 2 * n_query * micro
    summaries = summaries.reshape(cells, model)
    cell_values = product(summaries, cell_part)
    cell_values = cell_values.reshape(2, n_query, micro, dh_part).transpose(2, 0, 1, 3)
    asked = facts[0].astype(jnp.int32) ^ query_index
    chosen_cell = cell_values[:, :, 0, None]
    for i in range(1, n_query):
        chosen_cell = jnp.where(asked[..., None] == i, cell_values[:, :, i, None], chosen_cell)
    asked = (jnp.arange(2)[None, :, None] * n_query + asked) * micro + jnp.arange(micro)[:, None, None]
    onehot = (asked.reshape(-1, 1) == jnp.arange(cells, dtype=jnp.int32)).astype(BF16)
    pre_act = product(pin(gene_rows, attn_own), gene_part).reshape(micro, 2, room, dh_part) + chosen_cell
    pre_act = pre_act + decoder_bias_part
    chance = jax.nn.sigmoid(pre_act)
    activity = pre_act * chance
    logits = jnp.sum(activity * readout_part, axis=-1)
    up_total = y_sum(grad_up_part, pin(up_far, logits))
    attn_near = jnp.stack([attn_own, pin(attn_far, up_total)], axis=1)
    logits = pin(logits, up_total)
    up_total = line_scatter(up_total)
    grad_attn = jnp.concatenate([attn_near, core_swap(attn_near)], axis=1).reshape(-1, model)
    logits = group_sum(logits)
    grad_logits = facts[2] * (jax.nn.sigmoid(logits) - facts[1])
    grad_readout = jnp.sum(grad_logits[..., None] * activity, axis=(0, 1, 2))
    slope = chance * (1.0 + pre_act * (1.0 - chance))
    grad_pre = (grad_logits[..., None] * readout_part * slope).astype(BF16).reshape(-1, dh_part)
    grad_decoder_bias = jnp.sum(grad_pre.astype(F32), axis=0)
    grad_cells = row_product(onehot, grad_pre).astype(BF16)
    grad_summary = times_transpose(grad_cells, cell_part).reshape(2, n_query, micro, model)
    grad_summary = grad_summary[0] + core_swap(grad_summary[1].astype(BF16)).astype(F32)
    grad_gene_part = row_product(gene_rows, pin(grad_pre, grad_summary)).astype(BF16)
    gene_total = plane_scatter(grad_gene_part)
    grad_mixed = times_transpose(grad_attn, out_part).astype(BF16)

    for bit in reversed(query_bits):
        grad_summary = grad_summary.reshape(2, -1, micro, model)
        far = query_swap(grad_summary[1].astype(BF16), bit)
        grad_summary = grad_summary[0] + far.astype(F32)
    grad_summary = grad_summary.reshape(micro, model)

    first_active, first_in, first_proj, first_base, first_cot = first_rows_of(
        [active, second, up_proj, grad_up_proj, all_cotangent], length
    )
    first_cotangent = first_of(own_cotangent)
    first_grad = first_cotangent + grad_summary
    first_branch = gather_four(first_grad.astype(BF16)[:, None]).reshape(-1, model)
    first_change = (first_branch.astype(F32) - first_cot.astype(F32)).astype(BF16)
    first_gelu_back = jax.vjp(
        lambda inner: jax.nn.gelu(inner, approximate=True), first_proj
    )[1]
    first_up = first_gelu_back(times_transpose(first_branch, down_part))[0].astype(BF16)
    first_up_change = (first_up.astype(F32) - first_base.astype(F32)).astype(BF16)
    first_second = scatter_four(times_transpose(first_up, up_part), micro)
    first_norm, first_scale = first_of(norm_two), first_of(scale_two)
    first_hidden, first_gain = norm_back(first_second, ffn_gain_all, first_norm, first_scale)
    first_hidden = first_grad + first_hidden
    first_attn = gather_four(first_hidden.astype(BF16)[:, None]).reshape(-1, model)
    first_mixed = times_transpose(first_attn, out_part).astype(BF16)
    first_attn_base, first_mixed_rows = first_rows_of([grad_attn, mixed], length)
    first_attn_change = (first_attn.astype(F32) - first_attn_base.astype(F32)).astype(BF16)
    grad_up_bias = jnp.sum(grad_up_proj.astype(F32), axis=0) + jnp.sum(
        first_up_change.astype(F32), axis=0
    )
    grad_ffn_gain = grad_ffn_gain + first_gain - jnp.sum(first_of(grad_second) * first_norm, axis=0)
    grad_hidden = grad_hidden.reshape(micro, length, model).at[:, 0].set(first_hidden)
    grad_hidden = grad_hidden.reshape(micro * length, model)

    grad_out_part = row_product(mixed, grad_attn) + row_product(first_mixed_rows, first_attn_change)
    grad_out_part = grad_out_part.astype(BF16)
    out_blocks = exchange_four([grad_out_part[:, i * part : (i + 1) * part] for i in range(4)])
    grad_projected = attend_back(projected, pin(grad_mixed, grad_gene_part), first_mixed[:, None], length)
    grad_qkv_part = row_product(normed, grad_projected).astype(BF16)
    attention_in = paste(grad_qkv_part, out_blocks, index)
    grad_normed = times_transpose(pin(grad_projected, attention_in), qkv_part)
    norm_one, scale_one = layer_stats(own_wide)
    blocks = grad_normed.reshape(micro, 4, length, model)
    received = core_swap(blocks[:, 2:].astype(BF16)).astype(F32)
    near_sum = blocks[:, 0] + received[:, 0]
    far_sum = query_swap((blocks[:, 1] + received[:, 1]).astype(BF16))

    left = jnp.concatenate([first_active, first_in, summaries])[None]
    for bit in chip_bits:
        left = jnp.concatenate([left, dp_swap(left, bit)])
    left = left.reshape(chips, left.shape[1], chips, 2 * shard)
    left = lax.dynamic_index_in_dim(left, chip, 2, keepdims=False)
    travelling = [jnp.concatenate([first_change, first_up_change, grad_cells])[None]]
    owned = {}

    def few_step(bit, event):
        value = pin(travelling[-1], event)
        travelling.append(jnp.concatenate([value, dp_swap(value, bit)]))
        return (travelling[-1],)

    def few_rows(start, stop):
        rows = travelling[-1][:, start:stop].reshape(-1, ff_part)
        return row_product(left[:, start:stop].reshape(-1, 2 * shard), rows)

    def few_sums(event):
        firsts = 4 * micro
        few = jnp.stack([down_total, up_total, jnp.zeros_like(up_total)]).astype(F32)
        few = few + jnp.stack(
            [
                few_rows(0, firsts),
                few_rows(firsts, 2 * firsts),
                few_rows(2 * firsts, 2 * firsts + cells),
            ]
        )
        few = other_pairs(pin(few.astype(BF16), event)).reshape(3, 2, shard, model)
        mine, theirs = order(core, few[:, 0], few[:, 1])
        owned["few"] = mine, core_swap(theirs)
        return owned["few"][1:]

    def few_far(event):
        far = query_swap(pin(jnp.stack(owned["few"]), event))
        owned["few"] = (*owned["few"], far[0], far[1])
        return ()

    def few_here(event):
        return owned["few"][2:]

    sums = {}

    def norm_step(event):
        grad_normed = (near_sum + far_sum.astype(F32)).reshape(micro * length, model)
        grad_input_norm, grad_attn_gain = norm_back(grad_normed, attn_gain_all, norm_one, scale_one)
        sums["tokens"] = (grad_hidden + grad_input_norm).reshape(micro, 1, length, model)
        chosen = (jnp.arange(4) == quarter).astype(F32)
        sums["small"] = jnp.concatenate(
            [
                grad_attn_gain.reshape(n_dp, shard),
                grad_ffn_gain.reshape(n_dp, shard),
                (grad_up_bias.reshape(n_dp, 1, ff_shard // 4) * chosen[:, None]).reshape(n_dp, ff_shard),
                (chosen[:, None] * grad_decoder_bias).reshape(n_dp, dh_shard),
                (chosen[:, None] * grad_readout).reshape(n_dp, dh_shard),
            ],
            axis=1,
        )
        return (sums["small"],)

    def sum_step(bit, event):
        value = pin(sums["small"], event)
        value = value.reshape((2, value.shape[0] // 2) + value.shape[1:])
        kept, sent = order((dp_index // bit) % 2, value[0], value[1])
        sums["small"] = kept + dp_swap(sent, bit)
        return (sums["small"],)

    def sum_query(bit, event):
        value = pin(sums["small"], event)
        sums["small"] = value + query_swap(value, bit)
        return (sums["small"],)

    first_line = [functools.partial(few_step, bit) for bit in chip_bits] + [few_sums, few_far]
    first_line += [few_here] if len(chip_bits) + 3 < chips else []
    second_line = [lambda event: (), lambda event: (far_sum,), norm_step]
    second_line += [functools.partial(sum_step, bit) for bit in reversed([1] + chip_bits)]
    second_line += [functools.partial(sum_query, bit) for bit in query_bits]
    attention_grads = ring_scatter(attention_in, first_line, second_line)
    few_owned = owned["few"]
    gene_owned = to_owner(*cores(other_pairs(gene_total)))
    grad_tokens, vector_sums = sums["tokens"], sums["small"]

    grad_gene = jnp.concatenate(by_quarter(*gene_owned), axis=1).astype(F32)
    down_rows, up_rows, cell_rows = zip(*((block[0], block[1], block[2]) for block in few_owned))
    grad_cell = jnp.concatenate(by_quarter(*cell_rows), axis=1).astype(F32)
    grad_down = jnp.concatenate(by_quarter(*down_rows)).astype(F32)
    (grad_up,) = join(up_rows, index, column_places("up", ff_part, n_dp), [4 * ff_part])
    grad_qkv, grad_out = join(
        to_owner(*attention_grads), index, column_places("attention", part, n_dp), [3 * model, model]
    )

    small = [vector_sums[0, low:high] for low, high in zip(bounds[:-1], bounds[1:])]
    return (
        block_out[:, None],
        grad_tokens,
        grad_qkv,
        grad_out,
        grad_up,
        grad_down,
        small[0],
        small[1],
        small[2],
        grad_cell,
        grad_gene,
        small[3],
        small[4],
    )


def solution(mesh):
    cells = P(None, ("dp", "query"), None, None)
    rows = P("dp", None)
    vector = P("dp")
    slots = P(None, ("dp", "query"), None)
    return jax.shard_map(
        functools.partial(shards, mesh.shape["dp"], mesh.shape["query"]),
        mesh=mesh,
        in_specs=(
            cells, cells, rows, rows, rows, rows, vector, vector, vector, rows, rows, vector, vector,
            cells, slots, slots, P("dp", None, "query"),
        ),
        out_specs=(
            cells, cells, rows, rows, rows, rows, vector, vector, vector, rows, rows, vector, vector,
        ),
        check_vma=False,
    )
```

time: 663 us -> 626 us (0.944)
  waiting for transfers between devices: 208 us -> 170 us
  starting transfers between devices: 76.4 us -> 89.9 us
  local copies, waits for them, and re-layouts: 79.4 us -> 89.8 us
  other arithmetic: 113 us -> 104 us
  between operations: 24.7 us -> 16.6 us
  Pallas kernels: 55.9 us -> 48.4 us
    ppermute x38 -> x45, waiting for transfers between devices: 47.6 us -> 31.2 us  [dp_swap(): return lax.ppermute(value, 'dp', [(i, i ^ bit) for i in range(n_dp)])]
    ppermute x25 -> x26, waiting for transfers between devices: 99.2 us -> 83.6 us  [query_swap(): return lax.ppermute(value, 'query', [(i, i ^ bit) for i in range(n_query)])]
    ppermute x7, waiting for transfers between devices: 14.7 us -> 29.5 us  [ring_scatter(): high = lax.ppermute(high, 'dp', behind)]
    ppermute x7, waiting for transfers between devices: 30.6 us -> 16 us  [ring_step(): held.append(lax.ppermute(low, 'dp', ahead))]
    pallas_call x1, Pallas kernels: 23.3 us -> 10.1 us  [attend_back(): pl.pallas_call(attend_back_kernel, grid=(rows // length,), in_specs=[pl.B...]
    pallas_call x2 -> x8, Pallas kernels: 3.97 us -> 14.9 us  [the longest x3 5.95 us: first_rows_of(): pl.pallas_call(first_kernel, grid=(1,), in_specs=specs, out_specs=outs, o...]
    ppermute x38 -> x45, starting transfers between devices: 12.8 us -> 23.3 us  [dp_swap(): return lax.ppermute(value, 'dp', [(i, i ^ bit) for i in range(n_dp)])]
    dot_general x7, matrix products: 33.7 us -> 42.9 us  [product(): return jnp.dot(left, right, preferred_element_type=F32)]
  transfers between devices with their start and end apart: 96 -> 105, of which waited for: 47 -> 52; matrix products, arithmetic and copies ran while one was open for 39% -> 42% of each run, Pallas kernels for 9% -> 7%
where the time goes in v2:
time: 626 us; the launch traced here: 619 us
  waiting for transfers between devices  170 us (27%)
  other arithmetic  104 us (17%)
  matrix products  101 us (16%)
  starting transfers between devices  89.9 us (14%)
  local copies, waits for them, and re-layouts  89.8 us (14%)
  Pallas kernels  48.4 us (8%)
  between operations  16.6 us (3%)
    ppermute x26, waiting for transfers between devices, query_swap(): return lax.ppermute(value, 'query', [(i, i ^ bit) for i in range(n_query)])  83.6 us
    dot_general x7, matrix products, product(): return jnp.dot(left, right, preferred_element_type=F32)  42.9 us
    unnamed x262, local copies, waits for them, and re-layouts  39.8 us
    ppermute x26, starting transfers between devices, query_swap(): return lax.ppermute(value, 'query', [(i, i ^ bit) for i in range(n_query)])  35.9 us
    dot_general x10, matrix products, row_product(): lax.dot_general(left, right, (((0,), (0,)), ((), ())), preferred_element_...  34.3 us
    ppermute x45, waiting for transfers between devices, dp_swap(): return lax.ppermute(value, 'dp', [(i, i ^ bit) for i in range(n_dp)])  31.2 us
    ppermute x7, waiting for transfers between devices, ring_scatter(): high = lax.ppermute(high, 'dp', behind)  29.5 us
    dot_general x8, matrix products, times_transpose(): lax.dot_general(left, right, (((1,), (1,)), ((), ())), preferred_element_...  23.6 us
  transfers between devices with their start and end apart: 105, of which 52 were waited for; matrix products, arithmetic and copies ran while one was open for 42% of the time, Pallas kernels for 7%

profile of v2, /device:TPU:0, one launch (start us, length us, event | category | flops | bytes accessed | tf_op | source)
XLA Modules:
  0.0 619.0 jit_solution(6847897503443235874)
XLA Ops:
  15.6 5.6 collective-permute-done.1.refs_2_
  22.6 5.5 collective-permute-done.3.refs_1_
  64.4 4.6 collective-permute-done.15.refs_2_
  74.9 4.3 collective-permute-done.16.refs_14_
  107.6 5.6 shard_map.265
  118.3 3.1 shard_map.266
  124.2 4.1 fusion.27.projected_ref
  129.0 4.7 shard_map.267
  140.9 3.6 fusion.136
  144.6 4.7 shard_map.268
  151.4 3.4 fusion.137
  174.9 7.3 %collective-permute-done.26 = bf16[1,128,1280]{2,1,0:T(8,128)(2,1)S(1)} collective-permute-done((bf16[1,128,1280]{2,1,0:T(8,128)(2,1)S(1)}, bf16[1,128,1280]{2,1,0:T(8,128)(2,1)S(1)}, u32[]{:S(2)}, u32[]{:S(2)}) %collective-permute-start.26) | collective-permute-done | bytes 327712 | tf_op jit(solution)/shard_map/ppermute | solution.py:522
  185.0 6.5 %collective-permute-done.24 = bf16[1,128,1280]{2,1,0:T(8,128)(2,1)S(1)} collective-permute-done((bf16[1,128,1280]{2,1,0:T(8,128)(2,1)S(1)}, bf16[1,128,1280]{2,1,0:T(8,128)(2,1)S(1)}, u32[]{:S(2)}, u32[]{:S(2)}) %collective-permute-start.24) | collective-permute-done | bytes 327712 | tf_op jit(solution)/shard_map/ppermute | solution.py:522
  197.2 3.1 shard_map.270
  205.3 5.7 collective-permute-done.27
  213.9 3.2 pad_maximum_fusion
  220.1 10.3 %multiply_convert_fusion.1 = (bf16[1024,1280]{1,0:T(8,128)(2,1)}, f32[1024,1280]{1,0:T(8,128)}) fusion(f32[1280]{0:T(1024)S(1)} %copy-done.110, bf16[1024,1280]{1,0:T(8,128)(2,1)} %bitcast.476, bf16[1280,1280]{1,0:T(8,128)(2,1)} %all-gather.4.cloned.1.call-done), kind=kOutput, calls=%fused_computation.22 | convolution fusion | flops 3368550400 | bytes 13767680 | tf_op jit(solution)/shard_map/dot_general | solution.py:17
  230.3 8.6 %fusion.138 = f32[1024,1280]{1,0:T(8,128)} fusion(bf16[1024,1280]{1,0:T(8,128)(2,1)} %get-tuple-element.165, bf16[1280,1280]{1,0:T(8,128)(2,1)} %all-gather.6.cloned.1.call-done), kind=kOutput, calls=%fused_computation.411 | convolution fusion | flops 3355443200 | bytes 11141120 | tf_op jit(solution)/shard_map/dot_general | solution.py:17
  242.2 6.3 %convolution_convert_fusion.1 = bf16[1280,1280]{1,0:T(8,128)(2,1)S(1)} fusion(bf16[1024,1280]{1,0:T(8,128)(2,1)} %get-tuple-element.165, bf16[1024,1280]{1,0:T(8,128)(2,1)} %bitcast.473), kind=kOutput, calls=%fused_computation.10 | convolution fusion | flops 3357081600 | bytes 8519680 | tf_op jit(solution)/shard_map/dot_general | solution.py:21
  252.5 6.8 %convert_reduce_fusion.1 = (f32[1280]{0:T(1024)}, bf16[1024,1280]{1,0:T(8,128)(2,1)S(1)}) fusion(f32[1024,1280]{1,0:T(8,128)S(1)} %bitcast.492, bf16[1024,1280]{1,0:T(8,128)(2,1)S(1)} %bitcast.475, bf16[1280,1280]{1,0:T(8,128)(2,1)S(1)} %copy-done.63), kind=kOutput, calls=%fused_computation.21 | convolution fusion | flops 3384277760 | bytes 13767680 | tf_op jit(solution)/shard_map/dot_general | solution.py:25
  260.6 4.1 convolution_convert_fusion
  274.0 6.3 %fusion.139 = f32[1024,1280]{1,0:T(8,128)S(1)} fusion(bf16[1024,1280]{1,0:T(8,128)(2,1)} %copy-done.73, bf16[1280,1280]{1,0:T(8,128)(2,1)} %all-gather.4.cloned.1.call-done), kind=kOutput, calls=%fused_computation.412 | convolution fusion | flops 3355443200 | bytes 11141120 | tf_op jit(solution)/shard_map/dot_general | solution.py:25
  297.4 17.8 %collective-permute-done.83 = bf16[4,24,1280]{2,1,0:T(8,128)(2,1)S(1)} collective-permute-done((bf16[4,24,1280]{2,1,0:T(8,128)(2,1)S(1)}, bf16[4,24,1280]{2,1,0:T(8,128)(2,1)S(1)}, u32[]{:S(2)}, u32[]{:S(2)}) %collective-permute-start.83) | collective-permute-done | bytes 245792 | tf_op jit(solution)/shard_map/ppermute | solution.py:516
  323.4 3.0 fusion.14
  326.9 10.1 %collective-permute-done.46 = bf16[2,128,1280]{2,1,0:T(8,128)(2,1)} collective-permute-done((bf16[2,128,1280]{2,1,0:T(8,128)(2,1)}, bf16[2,128,1280]{2,1,0:T(8,128)(2,1)}, u32[]{:S(2)}, u32[]{:S(2)}) %collective-permute-start.46) | collective-permute-done | bytes 655392 | tf_op jit(solution)/shard_map/ppermute | solution.py:522
  338.9 3.1 multiply_reduce_fusion.2
  348.0 10.4 %fusion.1 = f32[1984,1280]{1,0:T(8,128)S(1)} fusion(bf16[1984,1280]{1,0:T(8,128)(2,1)} %copy-done.2, f32[1280]{0:T(1024)S(1)} %copy-done.109, f32[2,2,1280]{2,1,0:T(2,128)S(1)} %copy.131, f32[2,2,1280]{2,1,0:T(2,128)S(1)} %copy.130, pred[1984]{0:T(1024)(128)(4,1)S(1)} %copy-done.117, bf16[1280,2560]{1,0:T(8,128)(2,1)} %all-gather.8.cloned.1.call-done), kind=kOutput, calls=%fused_computation.2 | convolution fusion | flops 6508789760 | bytes 18561984 | tf_op jit(solution)/shard_map/dot_general | solution.py:17
  358.4 3.8 copy-done.41
  365.8 3.6 fusion.11
  378.8 8.1 %convert_reduce_fusion = (f32[1280]{0:T(1024)S(1)}, bf16[1984,1280]{1,0:T(8,128)(2,1)S(1)}, f32[1280]{0:T(1024)S(1)}) fusion(f32[1984,1280]{1,0:T(8,128)} %copy-done.41, f32[1280]{0:T(1024)S(1)} %copy-done.90, f32[1984]{0:T(1024)S(1)} %mul.652), kind=kLoop, calls=%fused_computation.4 | loop fusion | flops 38090240 | bytes 15260416 | tf_op jit(solution)/shard_map/reduce_sum | solution.py:772
  399.1 12.0 %convolution_convert_fusion.2 = bf16[1280,1280]{1,0:T(8,128)(2,1)} fusion(bf16[1984,1280]{1,0:T(8,128)(2,1)} %copy-done.2, bf16[1984,1280]{1,0:T(8,128)(2,1)} %copy-done.43), kind=kOutput, calls=%fused_computation.11 | convolution fusion | flops 6502809600 | bytes 13434880 | tf_op jit(solution)/shard_map/dot_general | solution.py:21
  411.2 3.0 fusion.140
  430.0 3.0 pad_maximum_fusion.1
  444.0 10.1 %shard_map.275 = bf16[1024,960]{1,0:T(8,128)(2,1)} custom-call(bf16[1024,960]{1,0:T(8,128)(2,1)} %fusion.27.projected_ref, bf16[1024,320]{1,0:T(8,128)(2,1)} %convolution_convert_fusion.5.grad_mixed_ref, bf16[8,1,320]{2,1,0:T(2,128)(2,1)} %copy.148.first_ref), custom_call_target="tpu_custom_call" | custom-call | flops 419430400 | bytes 4915200 | tf_op jit(solution)/shard_map/pallas_call | solution.py:128
  459.5 5.9 convolution_convert_fusion.3
  465.4 3.0 copy.149.qkv_ref
  476.1 2.9 fusion.20
  482.0 10.3 %collective-permute-done.69 = bf16[80,1280]{1,0:T(8,128)(2,1)S(1)} collective-permute-done((bf16[80,1280]{1,0:T(8,128)(2,1)S(1)}, bf16[80,1280]{1,0:T(8,128)(2,1)S(1)}, u32[]{:S(2)}, u32[]{:S(2)}) %collective-permute-start.69) | collective-permute-done | bytes 204832 | tf_op jit(solution)/shard_map/ppermute | solution.py:603
  492.4 2.9 collective-permute-start.72
  498.1 3.0 collective-permute-done.71
  511.4 8.0 %collective-permute-done.67 = bf16[2,128,1280]{2,1,0:T(8,128)(2,1)S(1)} collective-permute-done((bf16[2,128,1280]{2,1,0:T(8,128)(2,1)S(1)}, bf16[2,128,1280]{2,1,0:T(8,128)(2,1)S(1)}, u32[]{:S(2)}, u32[]{:S(2)}) %collective-permute-start.67) | collective-permute-done | bytes 655392 | tf_op jit(solution)/shard_map/ppermute | solution.py:522
  532.9 4.0 collective-permute-done.78
  544.9 3.7 collective-permute-done.80
  554.1 3.8 collective-permute-done.87
  565.2 3.7 collective-permute-done.90
  573.5 15.9 %collective-permute-done.96 = f32[1,1120]{1,0:T(1,128)S(1)} collective-permute-done((f32[1,1120]{1,0:T(1,128)S(1)}, f32[1,1120]{1,0:T(1,128)S(1)}, u32[]{:S(2)}, u32[]{:S(2)}) %collective-permute-start.96) | collective-permute-done | bytes 4512 | tf_op jit(solution)/shard_map/ppermute | solution.py:522
  590.7 3.1 collective-permute-done.93
  604.2 6.3 %collective-permute-done.98 = bf16[2,80,1280]{2,1,0:T(8,128)(2,1)S(1)} collective-permute-done((bf16[2,80,1280]{2,1,0:T(8,128)(2,1)S(1)}, bf16[2,80,1280]{2,1,0:T(8,128)(2,1)S(1)}, u32[]{:S(2)}, u32[]{:S(2)}) %collective-permute-start.98) | collective-permute-done | bytes 409632 | tf_op jit(solution)/shard_map/ppermute | solution.py:522
  (713 shorter events, 320.6 us)
Async XLA Ops:
  7.2 212.9 %all-gather.4.cloned.1.call-start = ((), (), s32[]{:S(2)}) async-start(), calls=%async_computation.3 | async-start | bytes 3686400 | tf_op jit(solution)/shard_map/all_gather | solution.py:585
  10.0 18.1 %collective-permute-start.3 = (bf16[2,128,1280]{2,1,0:T(8,128)(2,1)}, bf16[2,128,1280]{2,1,0:T(8,128)(2,1)S(1)}, u32[]{:S(2)}, u32[]{:S(2)}) collective-permute-start(bf16[2,128,1280]{2,1,0:T(8,128)(2,1)} %bitcast.456), channel_id=1, source_target_pairs={{0,1},{1,0},{2,3},{3,2},{4,5},{5,4},{6,7},{7,6},{8,9},{9,8},{10,11... | collective-permute-start | bytes 1966088 | tf_op jit(solution)/shard_map/ppermute | solution.py:522
  31.5 17.9 %collective-permute-start.10 = (bf16[2,128,1280]{2,1,0:T(8,128)(2,1)}, bf16[2,128,1280]{2,1,0:T(8,128)(2,1)S(1)}, u32[]{:S(2)}, u32[]{:S(2)}) collective-permute-start(bf16[2,128,1280]{2,1,0:T(8,128)(2,1)} %bitcast.472), channel_id=1, source_target_pairs={{0,1},{1,0},{2,3},{3,2},{4,5},{5,4},{6,7},{7,6},{8,9},{9,8},{10,11... | collective-permute-start | bytes 1966088 | tf_op jit(solution)/shard_map/ppermute | solution.py:522
  41.2 27.8 %collective-permute-start.15 = (bf16[384,1280]{1,0:T(8,128)(2,1)S(1)}, bf16[384,1280]{1,0:T(8,128)(2,1)}, u32[]{:S(2)}, u32[]{:S(2)}) collective-permute-start(bf16[384,1280]{1,0:T(8,128)(2,1)S(1)} %get-tuple-element.151.refs_0_), channel_id=1, source_target_pairs={{0,1},{1,0},{2,3},{3,2},{4,5},{5,4},{6,7},{7,6},{8,9},{9,8},{10,11... | collective-permute-start | bytes 2949128 | tf_op jit(solution)/shard_map/ppermute | solution.py:522
  79.6 150.7 %all-gather.6.cloned.1.call-start = ((), (), s32[]{:S(2)}) async-start(), calls=%async_computation.4 | async-start | bytes 3686400 | tf_op jit(solution)/shard_map/all_gather | solution.py:585
  83.2 262.2 %all-gather.8.cloned.1.call-start = ((), (), s32[]{:S(2)}) async-start(), calls=%async_computation.5 | async-start | bytes 7372800 | tf_op jit(solution)/shard_map/all_gather | solution.py:585
  83.6 34.8 %collective-permute-start.18 = (bf16[2,128,1280]{2,1,0:T(8,128)(2,1)S(1)}, bf16[2,128,1280]{2,1,0:T(8,128)(2,1)}, u32[]{:S(2)}, u32[]{:S(2)}) collective-permute-start(bf16[2,128,1280]{2,1,0:T(8,128)(2,1)S(1)} %bitcast.457), channel_id=1, source_target_pairs={{0,2},{2,0},{4,6},{6,4},{8,10},{10,8},{12,14},{14,12},{16,18},{18,... | collective-permute-start | bytes 1966088 | tf_op jit(solution)/shard_map/ppermute | solution.py:516
  96.8 32.2 %collective-permute-start.20 = (bf16[384,1280]{1,0:T(8,128)(2,1)S(1)}, bf16[384,1280]{1,0:T(8,128)(2,1)}, u32[]{:S(2)}, u32[]{:S(2)}) collective-permute-start(bf16[384,1280]{1,0:T(8,128)(2,1)S(1)} %get-tuple-element.152.refs_1_), channel_id=1, source_target_pairs={{0,1},{1,0},{2,3},{3,2},{4,5},{5,4},{6,7},{7,6},{8,9},{9,8},{10,11... | collective-permute-start | bytes 2949128 | tf_op jit(solution)/shard_map/ppermute | solution.py:522
  98.3 20.1 %collective-permute-start.19 = (bf16[2,128,1280]{2,1,0:T(8,128)(2,1)}, bf16[2,128,1280]{2,1,0:T(8,128)(2,1)}, u32[]{:S(2)}, u32[]{:S(2)}) collective-permute-start(bf16[2,128,1280]{2,1,0:T(8,128)(2,1)} %copy-done.10), channel_id=1, source_target_pairs={{0,2},{2,0},{4,6},{6,4},{8,10},{10,8},{12,14},{14,12},{16,18},{18,... | collective-permute-start | bytes 1966088 | tf_op jit(solution)/shard_map/ppermute | solution.py:516
  123.7 13.5 %collective-permute-start.22 = (bf16[2,320,320]{2,1,0:T(8,128)(2,1)}, bf16[2,320,320]{2,1,0:T(8,128)(2,1)}, u32[]{:S(2)}, u32[]{:S(2)}) collective-permute-start(bf16[2,320,320]{2,1,0:T(8,128)(2,1)} %pad_maximum_fusion.12), channel_id=1, source_target_pairs={{0,1},{1,0},{2,3},{3,2},{4,5},{5,4},{6,7},{7,6},{8,9},{9,8},{10,11... | collective-permute-start | bytes 1228808 | tf_op jit(solution)/shard_map/ppermute | solution.py:522
  136.2 406.4 %reduce-scatter.4.cloned.1.call-start = ((), (), s32[]{:S(2)}) async-start(), calls=%async_computation.6 | async-start | bytes 2048000 | tf_op jit(solution)/shard_map/reduce_scatter | solution.py:624
  159.5 12.9 %collective-permute-start.23 = (bf16[1,2,128,1280]{3,2,1,0:T(8,128)(2,1)}, bf16[1,2,128,1280]{3,2,1,0:T(8,128)(2,1)}, u32[]{:S(2)}, u32[]{:S(2)}) collective-permute-start(bf16[1,2,128,1280]{3,2,1,0:T(8,128)(2,1)} %slice.1047), channel_id=1, source_target_pairs={{0,2},{2,0},{4,6},{6,4},{8,10},{10,8},{12,14},{14,12},{16,18},{18,... | collective-permute-start | bytes 1966088 | tf_op jit(solution)/shard_map/ppermute | solution.py:516
  162.2 31.6 %collective-permute-start.34 = (bf16[384,1280]{1,0:T(8,128)(2,1)S(1)}, bf16[384,1280]{1,0:T(8,128)(2,1)}, u32[]{:S(2)}, u32[]{:S(2)}) collective-permute-start(bf16[384,1280]{1,0:T(8,128)(2,1)S(1)} %get-tuple-element.151.refs_0_), channel_id=1, source_target_pairs={{0,2},{2,0},{4,6},{6,4},{8,10},{10,8},{12,14},{14,12},{16,18},{18,... | collective-permute-start | bytes 2949128 | tf_op jit(solution)/shard_map/ppermute | solution.py:516
  164.7 31.1 %collective-permute-start.35 = (bf16[384,1280]{1,0:T(8,128)(2,1)S(1)}, bf16[384,1280]{1,0:T(8,128)(2,1)}, u32[]{:S(2)}, u32[]{:S(2)}) collective-permute-start(bf16[384,1280]{1,0:T(8,128)(2,1)S(1)} %get-tuple-element.152.refs_1_), channel_id=1, source_target_pairs={{0,2},{2,0},{4,6},{6,4},{8,10},{10,8},{12,14},{14,12},{16,18},{18,... | collective-permute-start | bytes 2949128 | tf_op jit(solution)/shard_map/ppermute | solution.py:516
  165.5 31.7 %collective-permute-start.36 = (bf16[384,1280]{1,0:T(8,128)(2,1)}, bf16[384,1280]{1,0:T(8,128)(2,1)}, u32[]{:S(2)}, u32[]{:S(2)}) collective-permute-start(bf16[384,1280]{1,0:T(8,128)(2,1)} %collective-permute-done.15.refs_2_), channel_id=1, source_target_pairs={{0,2},{2,0},{4,6},{6,4},{8,10},{10,8},{12,14},{14,12},{16,18},{18,... | collective-permute-start | bytes 2949128 | tf_op jit(solution)/shard_map/ppermute | solution.py:516
  170.7 26.5 %collective-permute-start.37 = (bf16[384,1280]{1,0:T(8,128)(2,1)}, bf16[384,1280]{1,0:T(8,128)(2,1)S(1)}, u32[]{:S(2)}, u32[]{:S(2)}) collective-permute-start(bf16[384,1280]{1,0:T(8,128)(2,1)} %collective-permute-done.20.refs_3_), channel_id=1, source_target_pairs={{0,2},{2,0},{4,6},{6,4},{8,10},{10,8},{12,14},{14,12},{16,18},{18,... | collective-permute-start | bytes 2949128 | tf_op jit(solution)/shard_map/ppermute | solution.py:516
  172.4 9.9 %collective-permute-start.26 = (bf16[1,128,1280]{2,1,0:T(8,128)(2,1)S(1)}, bf16[1,128,1280]{2,1,0:T(8,128)(2,1)S(1)}, u32[]{:S(2)}, u32[]{:S(2)}) collective-permute-start(bf16[1,128,1280]{2,1,0:T(8,128)(2,1)S(1)} %fusion.61), channel_id=1, source_target_pairs={{0,1},{1,0},{2,3},{3,2},{4,5},{5,4},{6,7},{7,6},{8,9},{9,8},{10,11... | collective-permute-start | bytes 983048 | tf_op jit(solution)/shard_map/ppermute | solution.py:522
  191.4 22.4 %collective-permute-start.44 = (bf16[2,2,128,1280]{3,2,1,0:T(8,128)(2,1)}, bf16[2,2,128,1280]{3,2,1,0:T(8,128)(2,1)}, u32[]{:S(2)}, u32[]{:S(2)}) collective-permute-start(bf16[2,2,128,1280]{3,2,1,0:T(8,128)(2,1)} %pad_maximum_fusion.3), channel_id=1, source_target_pairs={{0,2},{2,0},{4,6},{6,4},{8,10},{10,8},{12,14},{14,12},{16,18},{18,... | collective-permute-start | bytes 3932168 | tf_op jit(solution)/shard_map/ppermute | solution.py:516
  193.9 10.6 %collective-permute-start.29 = (bf16[1,128,1280]{2,1,0:T(8,128)(2,1)S(1)}, bf16[1,128,1280]{2,1,0:T(8,128)(2,1)S(1)}, u32[]{:S(2)}, u32[]{:S(2)}) collective-permute-start(bf16[1,128,1280]{2,1,0:T(8,128)(2,1)S(1)} %fusion.67), channel_id=1, source_target_pairs={{0,1},{1,0},{2,3},{3,2},{4,5},{5,4},{6,7},{7,6},{8,9},{9,8},{10,11... | collective-permute-start | bytes 983048 | tf_op jit(solution)/shard_map/ppermute | solution.py:522
  195.8 15.3 %collective-permute-start.27 = (bf16[1,128,1280]{2,1,0:T(8,128)(2,1)S(1)}, bf16[1,128,1280]{2,1,0:T(8,128)(2,1)S(1)}, u32[]{:S(2)}, u32[]{:S(2)}) collective-permute-start(bf16[1,128,1280]{2,1,0:T(8,128)(2,1)S(1)} %get-tuple-element.383), channel_id=1, source_target_pairs={{0,1},{1,0},{2,3},{3,2},{4,5},{5,4},{6,7},{7,6},{8,9},{9,8},{10,11... | collective-permute-start | bytes 983048 | tf_op jit(solution)/shard_map/ppermute | solution.py:522
  205.3 11.8 %collective-permute-start.30 = (bf16[1,2,128,1280]{3,2,1,0:T(8,128)(2,1)}, bf16[1,2,128,1280]{3,2,1,0:T(8,128)(2,1)}, u32[]{:S(2)}, u32[]{:S(2)}) collective-permute-start(bf16[1,2,128,1280]{3,2,1,0:T(8,128)(2,1)} %pad_maximum_fusion.10), channel_id=1, source_target_pairs={{0,2},{2,0},{4,6},{6,4},{8,10},{10,8},{12,14},{14,12},{16,18},{18,... | collective-permute-start | bytes 1966088 | tf_op jit(solution)/shard_map/ppermute | solution.py:516
  241.6 17.6 %collective-permute-start.42 = (bf16[2,2,1,1280]{3,0,2,1:T(2,128)(2,1)S(1)}, bf16[2,2,1,1280]{3,0,2,1:T(2,128)(2,1)S(1)}, u32[]{:S(2)}, u32[]{:S(2)}) collective-permute-start(bf16[2,2,1,1280]{3,0,2,1:T(2,128)(2,1)S(1)} %copy.292), channel_id=1, source_target_pairs={{0,2},{2,0},{4,6},{6,4},{8,10},{10,8},{12,14},{14,12},{16,18},{18,... | collective-permute-start | bytes 30728 | tf_op jit(solution)/shard_map/ppermute | solution.py:516
  281.6 35.0 %collective-permute-start.45 = (bf16[2,2,128,1280]{3,2,0,1:T(8,128)(2,1)}, bf16[2,2,128,1280]{3,2,0,1:T(8,128)(2,1)}, u32[]{:S(2)}, u32[]{:S(2)}) collective-permute-start(bf16[2,2,128,1280]{3,2,0,1:T(8,128)(2,1)} %copy.289), channel_id=1, source_target_pairs={{0,2},{2,0},{4,6},{6,4},{8,10},{10,8},{12,14},{14,12},{16,18},{18,... | collective-permute-start | bytes 3932168 | tf_op jit(solution)/shard_map/ppermute | solution.py:516
  284.4 39.0 %collective-permute-start.47 = (bf16[640,1280]{1,0:T(8,128)(2,1)}, bf16[640,1280]{1,0:T(8,128)(2,1)}, u32[]{:S(2)}, u32[]{:S(2)}) collective-permute-start(bf16[640,1280]{1,0:T(8,128)(2,1)} %bitcast.53), channel_id=1, source_target_pairs={{0,4},{2,6},{4,0},{6,2},{8,12},{10,14},{12,8},{14,10},{16,20},{18,... | collective-permute-start | bytes 4915208 | tf_op jit(solution)/shard_map/ppermute | solution.py:516
  286.6 34.2 %collective-permute-start.40 = (bf16[2,2,128,1280]{3,2,0,1:T(8,128)(2,1)}, bf16[2,2,128,1280]{3,2,0,1:T(8,128)(2,1)}, u32[]{:S(2)}, u32[]{:S(2)}) collective-permute-start(bf16[2,2,128,1280]{3,2,0,1:T(8,128)(2,1)} %copy.290), channel_id=1, source_target_pairs={{0,2},{2,0},{4,6},{6,4},{8,10},{10,8},{12,14},{14,12},{16,18},{18,... | collective-permute-start | bytes 3932168 | tf_op jit(solution)/shard_map/ppermute | solution.py:516
  288.4 26.8 %collective-permute-start.83 = (bf16[4,24,1280]{2,1,0:T(8,128)(2,1)S(1)}, bf16[4,24,1280]{2,1,0:T(8,128)(2,1)S(1)}, u32[]{:S(2)}, u32[]{:S(2)}) collective-permute-start(bf16[4,24,1280]{2,1,0:T(8,128)(2,1)S(1)} %pad_maximum_fusion.19), channel_id=1, source_target_pairs={{0,16},{2,18},{4,20},{6,22},{8,24},{10,26},{12,28},{14,30},{16,0},... | collective-permute-start | bytes 737288 | tf_op jit(solution)/shard_map/ppermute | solution.py:516
  292.1 73.7 %collective-permute-start.51 = (bf16[640,1280]{1,0:T(8,128)(2,1)}, bf16[640,1280]{1,0:T(8,128)(2,1)}, u32[]{:S(2)}, u32[]{:S(2)}) collective-permute-start(bf16[640,1280]{1,0:T(8,128)(2,1)} %bitcast.55), channel_id=1, source_target_pairs={{0,4},{2,6},{4,0},{6,2},{8,12},{10,14},{12,8},{14,10},{16,20},{18,... | collective-permute-start | bytes 4915208 | tf_op jit(solution)/shard_map/ppermute | solution.py:516
  319.1 17.9 %collective-permute-start.46 = (bf16[2,128,1280]{2,1,0:T(8,128)(2,1)}, bf16[2,128,1280]{2,1,0:T(8,128)(2,1)}, u32[]{:S(2)}, u32[]{:S(2)}) collective-permute-start(bf16[2,128,1280]{2,1,0:T(8,128)(2,1)} %fusion.47), channel_id=1, source_target_pairs={{0,1},{1,0},{2,3},{3,2},{4,5},{5,4},{6,7},{7,6},{8,9},{9,8},{10,11... | collective-permute-start | bytes 1966088 | tf_op jit(solution)/shard_map/ppermute | solution.py:522
  322.9 50.4 %collective-permute-start.41 = (bf16[2,128,1280]{2,1,0:T(8,128)(2,1)}, bf16[2,128,1280]{2,1,0:T(8,128)(2,1)}, u32[]{:S(2)}, u32[]{:S(2)}) collective-permute-start(bf16[2,128,1280]{2,1,0:T(8,128)(2,1)} %fusion.46), channel_id=1, source_target_pairs={{0,1},{1,0},{2,3},{3,2},{4,5},{5,4},{6,7},{7,6},{8,9},{9,8},{10,11... | collective-permute-start | bytes 1966088 | tf_op jit(solution)/shard_map/ppermute | solution.py:522
  326.5 216.1 %reduce-scatter.6.cloned.1.call-start = ((), (), s32[]{:S(2)}) async-start(), calls=%async_computation.7 | async-start | bytes 2048000 | tf_op jit(solution)/shard_map/reduce_scatter | solution.py:624
  343.7 34.7 %collective-permute-start.60 = (bf16[2,128,1280]{2,1,0:T(8,128)(2,1)}, bf16[2,128,1280]{2,1,0:T(8,128)(2,1)}, u32[]{:S(2)}, u32[]{:S(2)}) collective-permute-start(bf16[2,128,1280]{2,1,0:T(8,128)(2,1)} %bitcast.65), channel_id=1, source_target_pairs={{0,1},{1,0},{2,3},{3,2},{4,5},{5,4},{6,7},{7,6},{8,9},{9,8},{10,11... | collective-permute-start | bytes 1966088 | tf_op jit(solution)/shard_map/ppermute | solution.py:522
  378.4 217.7 %reduce-scatter.8.cloned.1.call-start = ((), (), s32[]{:S(2)}) async-start(), calls=%async_computation.8 | async-start | bytes 3686400 | tf_op jit(solution)/shard_map/reduce_scatter | solution.py:588
  390.9 39.1 %collective-permute-start.61 = (bf16[2,2,128,1280]{3,2,1,0:T(8,128)(2,1)S(1)}, bf16[2,2,128,1280]{3,2,1,0:T(8,128)(2,1)S(1)}, u32[]{:S(2)}, u32[]{:S(2)}) collective-permute-start(bf16[2,2,128,1280]{3,2,1,0:T(8,128)(2,1)S(1)} %pad_maximum_fusion.5), channel_id=1, source_target_pairs={{0,2},{2,0},{4,6},{6,4},{8,10},{10,8},{12,14},{14,12},{16,18},{18,... | collective-permute-start | bytes 3932168 | tf_op jit(solution)/shard_map/ppermute | solution.py:516
  399.0 12.1 %collective-permute-start.57 = (bf16[2,2,1,1280]{3,0,2,1:T(2,128)(2,1)S(1)}, bf16[2,2,1,1280]{3,0,2,1:T(2,128)(2,1)S(1)}, u32[]{:S(2)}, u32[]{:S(2)}) collective-permute-start(bf16[2,2,1,1280]{3,0,2,1:T(2,128)(2,1)S(1)} %pad_maximum_fusion.26), channel_id=1, source_target_pairs={{0,2},{2,0},{4,6},{6,4},{8,10},{10,8},{12,14},{14,12},{16,18},{18,... | collective-permute-start | bytes 30728 | tf_op jit(solution)/shard_map/ppermute | solution.py:516
  440.1 14.0 %collective-permute-start.64 = (bf16[2,320,320]{2,1,0:T(8,128)(2,1)}, bf16[2,320,320]{2,1,0:T(8,128)(2,1)}, u32[]{:S(2)}, u32[]{:S(2)}) collective-permute-start(bf16[2,320,320]{2,1,0:T(8,128)(2,1)} %pad_maximum_fusion.13), channel_id=1, source_target_pairs={{0,2},{2,0},{4,6},{6,4},{8,10},{10,8},{12,14},{14,12},{16,18},{18,... | collective-permute-start | bytes 1228808 | tf_op jit(solution)/shard_map/ppermute | solution.py:516
  457.7 13.5 %collective-permute-start.65 = (bf16[2,320,320]{2,1,0:T(8,128)(2,1)}, bf16[2,320,320]{2,1,0:T(8,128)(2,1)}, u32[]{:S(2)}, u32[]{:S(2)}) collective-permute-start(bf16[2,320,320]{2,1,0:T(8,128)(2,1)} %pad_maximum_fusion.14), channel_id=1, source_target_pairs={{0,1},{1,0},{2,3},{3,2},{4,5},{5,4},{6,7},{7,6},{8,9},{9,8},{10,11... | collective-permute-start | bytes 1228808 | tf_op jit(solution)/shard_map/ppermute | solution.py:522
  479.1 13.2 %collective-permute-start.69 = (bf16[80,1280]{1,0:T(8,128)(2,1)S(1)}, bf16[80,1280]{1,0:T(8,128)(2,1)S(1)}, u32[]{:S(2)}, u32[]{:S(2)}) collective-permute-start(bf16[80,1280]{1,0:T(8,128)(2,1)S(1)} %get-tuple-element.313), channel_id=1, source_target_pairs={{0,4},{2,6},{8,0},{10,2},{16,8},{18,10},{24,16},{26,18},{28,24},{3... | collective-permute-start | bytes 614408 | tf_op jit(solution)/shard_map/ppermute | solution.py:603
  479.9 12.3 %collective-permute-start.68 = (bf16[80,1280]{1,0:T(8,128)(2,1)S(1)}, bf16[80,1280]{1,0:T(8,128)(2,1)S(1)}, u32[]{:S(2)}, u32[]{:S(2)}) collective-permute-start(bf16[80,1280]{1,0:T(8,128)(2,1)S(1)} %get-tuple-element.314), channel_id=1, source_target_pairs={{0,8},{2,10},{8,16},{10,18},{16,24},{18,26},{24,28},{26,30},{28,20... | collective-permute-start | bytes 614408 | tf_op jit(solution)/shard_map/ppermute | solution.py:602
  481.9 23.4 %collective-permute-start.66 = (bf16[2,2,128,1280]{3,2,0,1:T(8,128)(2,1)S(1)}, bf16[2,2,128,1280]{3,2,0,1:T(8,128)(2,1)S(1)}, u32[]{:S(2)}, u32[]{:S(2)}) collective-permute-start(bf16[2,2,128,1280]{3,2,0,1:T(8,128)(2,1)S(1)} %copy.288), channel_id=1, source_target_pairs={{0,2},{2,0},{4,6},{6,4},{8,10},{10,8},{12,14},{14,12},{16,18},{18,... | collective-permute-start | bytes 3932168 | tf_op jit(solution)/shard_map/ppermute | solution.py:516
  501.3 9.2 %collective-permute-start.73 = (bf16[80,1280]{1,0:T(8,128)(2,1)S(1)}, bf16[80,1280]{1,0:T(8,128)(2,1)S(1)}, u32[]{:S(2)}, u32[]{:S(2)}) collective-permute-start(bf16[80,1280]{1,0:T(8,128)(2,1)S(1)} %get-tuple-element.190), channel_id=1, source_target_pairs={{0,8},{2,10},{8,16},{10,18},{16,24},{18,26},{24,28},{26,30},{28,20... | collective-permute-start | bytes 614408 | tf_op jit(solution)/shard_map/ppermute | solution.py:602
  505.7 13.7 %collective-permute-start.67 = (bf16[2,128,1280]{2,1,0:T(8,128)(2,1)S(1)}, bf16[2,128,1280]{2,1,0:T(8,128)(2,1)S(1)}, u32[]{:S(2)}, u32[]{:S(2)}) collective-permute-start(bf16[2,128,1280]{2,1,0:T(8,128)(2,1)S(1)} %fusion.48), channel_id=1, source_target_pairs={{0,1},{1,0},{2,3},{3,2},{4,5},{5,4},{6,7},{7,6},{8,9},{9,8},{10,11... | collective-permute-start | bytes 1966088 | tf_op jit(solution)/shard_map/ppermute | solution.py:522
  519.4 11.5 %collective-permute-start.76 = (bf16[80,1280]{1,0:T(8,128)(2,1)}, bf16[80,1280]{1,0:T(8,128)(2,1)}, u32[]{:S(2)}, u32[]{:S(2)}) collective-permute-start(bf16[80,1280]{1,0:T(8,128)(2,1)} %get-tuple-element.193), channel_id=1, source_target_pairs={{0,8},{2,10},{8,16},{10,18},{16,24},{18,26},{24,28},{26,30},{28,20... | collective-permute-start | bytes 614408 | tf_op jit(solution)/shard_map/ppermute | solution.py:602
  525.4 11.5 %collective-permute-start.78 = (bf16[4,24,1280]{2,1,0:T(8,128)(2,1)S(1)}, bf16[4,24,1280]{2,1,0:T(8,128)(2,1)}, u32[]{:S(2)}, u32[]{:S(2)}) collective-permute-start(bf16[4,24,1280]{2,1,0:T(8,128)(2,1)S(1)} %constant_dynamic-update-slice_fusion.2), channel_id=1, source_target_pairs={{0,16},{2,18},{4,20},{6,22},{8,24},{10,26},{12,28},{14,30},{16,0},... | collective-permute-start | bytes 737288 | tf_op jit(solution)/shard_map/ppermute | solution.py:516
  537.9 10.7 %collective-permute-start.79 = (bf16[80,1280]{1,0:T(8,128)(2,1)}, bf16[80,1280]{1,0:T(8,128)(2,1)S(1)}, u32[]{:S(2)}, u32[]{:S(2)}) collective-permute-start(bf16[80,1280]{1,0:T(8,128)(2,1)} %get-tuple-element.196), channel_id=1, source_target_pairs={{0,8},{2,10},{8,16},{10,18},{16,24},{18,26},{24,28},{26,30},{28,20... | collective-permute-start | bytes 614408 | tf_op jit(solution)/shard_map/ppermute | solution.py:602
  561.3 34.6 %collective-permute-start.94 = (bf16[2,3,80,1280]{3,2,1,0:T(8,128)(2,1)S(1)}, bf16[2,3,80,1280]{3,2,1,0:T(8,128)(2,1)S(1)}, u32[]{:S(2)}, u32[]{:S(2)}) collective-permute-start(bf16[2,3,80,1280]{3,2,1,0:T(8,128)(2,1)S(1)} %pad_maximum_fusion.6), channel_id=1, source_target_pairs={{0,1},{1,0},{2,3},{3,2},{4,5},{5,4},{6,7},{7,6},{8,9},{9,8},{10,11... | collective-permute-start | bytes 3686408 | tf_op jit(solution)/shard_map/ppermute | solution.py:522
  571.3 18.1 %collective-permute-start.96 = (f32[1,1120]{1,0:T(1,128)S(1)}, f32[1,1120]{1,0:T(1,128)S(1)}, u32[]{:S(2)}, u32[]{:S(2)}) collective-permute-start(f32[1,1120]{1,0:T(1,128)S(1)} %fusion.107), channel_id=1, source_target_pairs={{0,1},{1,0},{2,3},{3,2},{4,5},{5,4},{6,7},{7,6},{8,9},{9,8},{10,11... | collective-permute-start | bytes 13448 | tf_op jit(solution)/shard_map/ppermute | solution.py:522
  571.9 22.0 %collective-permute-start.93 = (bf16[2,80,1280]{2,1,0:T(8,128)(2,1)S(1)}, bf16[2,80,1280]{2,1,0:T(8,128)(2,1)S(1)}, u32[]{:S(2)}, u32[]{:S(2)}) collective-permute-start(bf16[2,80,1280]{2,1,0:T(8,128)(2,1)S(1)} %pad_maximum_fusion.17), channel_id=1, source_target_pairs={{0,1},{1,0},{2,3},{3,2},{4,5},{5,4},{6,7},{7,6},{8,9},{9,8},{10,11... | collective-permute-start | bytes 1228808 | tf_op jit(solution)/shard_map/ppermute | solution.py:522
  598.7 11.8 %collective-permute-start.98 = (bf16[2,80,1280]{2,1,0:T(8,128)(2,1)S(1)}, bf16[2,80,1280]{2,1,0:T(8,128)(2,1)S(1)}, u32[]{:S(2)}, u32[]{:S(2)}) collective-permute-start(bf16[2,80,1280]{2,1,0:T(8,128)(2,1)S(1)} %pad_maximum_fusion.18), channel_id=1, source_target_pairs={{0,1},{1,0},{2,3},{3,2},{4,5},{5,4},{6,7},{7,6},{8,9},{9,8},{10,11... | collective-permute-start | bytes 1228808 | tf_op jit(solution)/shard_map/ppermute | solution.py:522
  (182 other events, 1125.7 us)
Sparse Core Ops, SparseCore 0:
  79.7 60.0 all-gather.3
  142.0 60.5 all-gather.5
  205.3 112.6 all-gather.7
  326.6 34.6 reduce-scatter.3
  378.6 34.9 reduce-scatter.5
  417.0 79.0 reduce-scatter.7

commit v3 on v2

--- a/solution.py
+++ b/solution.py
@@ -589,29 +589,6 @@
             grads, "dp", scatter_dimension=0, tiled=True, axis_index_groups=same_core
         )
 
-    def ring_scatter(grads, *lines):
-        rows = grads.shape[0] // n_dp
-
-        def piece(offset, side):
-            start = (2 * ring_chip(position + offset, chips) + side) * rows
-            return lax.dynamic_slice(grads, (start, 0), (rows, grads.shape[1]))
-
-        low, high = piece(-1, 0), piece(1, 1)
-        events = ()
-        for step in range(1, chips):
-            low = lax.ppermute(low, "dp", ahead)
-            high = lax.ppermute(high, "dp", behind)
-            low = (low.astype(F32) + piece(-1 - step, 0).astype(F32)).astype(BF16)
-            high = (high.astype(F32) + piece(1 + step, 1).astype(F32)).astype(BF16)
-            low, high = lax.optimization_barrier((low, high, *events))[:2]
-            events = ()
-            for line in lines:
-                events += tuple(line[step - 1](low)) if step <= len(line) else ()
-        for line in lines:
-            for work in line[chips - 1 :]:
-                work(low)
-        return other_pairs(low), other_pairs(high)
-
     def y_half(grads, which):
         held = grads.reshape(-1, 2, 2 * shard, grads.shape[1])
         held = lax.dynamic_index_in_dim(held, which, 1, keepdims=False)
@@ -816,7 +793,9 @@
     grad_projected = attend_back(projected, pin(grad_mixed, grad_gene_part), first_mixed[:, None], length)
     grad_qkv_part = row_product(normed, grad_projected).astype(BF16)
     attention_in = paste(grad_qkv_part, out_blocks, index)
-    grad_normed = times_transpose(pin(grad_projected, attention_in), qkv_part)
+    attention_sent = y_half(attention_in, 1 - chip % 2)
+    attention_far = dp_swap(attention_sent, 2)
+    grad_normed = times_transpose(pin(grad_projected, attention_sent), qkv_part)
     norm_one, scale_one = layer_stats(own_wide)
     blocks = grad_normed.reshape(micro, 4, length, model)
     received = core_swap(blocks[:, 2:].astype(BF16)).astype(F32)
@@ -894,12 +873,21 @@
         sums["small"] = value + query_swap(value, bit)
         return (sums["small"],)
 
-    first_line = [functools.partial(few_step, bit) for bit in chip_bits] + [few_sums, few_far]
-    first_line += [few_here] if len(chip_bits) + 3 < chips else []
-    second_line = [lambda event: (), lambda event: (far_sum,), norm_step]
-    second_line += [functools.partial(sum_step, bit) for bit in reversed([1] + chip_bits)]
-    second_line += [functools.partial(sum_query, bit) for bit in query_bits]
-    attention_grads = ring_scatter(attention_in, first_line, second_line)
+    few_step(chip_bits[0], attention_sent)
+    few_step(chip_bits[1], travelling[-1])
+    attention_total = y_sum(attention_in, pin(attention_far, travelling[-1]))
+    for bit in chip_bits[2:]:
+        few_step(bit, attention_total)
+    attention_rows = line_scatter(attention_total)
+    few_sums(travelling[-1])
+    few_far(owned["few"][1])
+    norm_step(far_sum)
+    for bit in reversed([1] + chip_bits):
+        sum_step(bit, sums["small"])
+    for bit in query_bits:
+        sum_query(bit, sums["small"])
+    attention_rows = pin(attention_rows, *owned["few"][2:], sums["small"])
+    attention_grads = cores(other_pairs(attention_rows))
     few_owned = owned["few"]
     gene_owned = to_owner(*cores(other_pairs(gene_total)))
     grad_tokens, vector_sums = sums["tokens"], sums["small"]

time: 626 us -> 647 us (1.034)
  waiting for transfers between devices: 170 us -> 206 us
  starting transfers between devices: 89.9 us -> 63.8 us
    ppermute x45 -> x46, waiting for transfers between devices: 31.2 us -> 84.1 us  [dp_swap(): return lax.ppermute(value, 'dp', [(i, i ^ bit) for i in range(n_dp)])]
    ppermute x14 -> x0, waiting for transfers between devices: 29.7 us -> none  [the longest x7 29.5 us: ring_scatter(): high = lax.ppermute(high, 'dp', behind)]
    ppermute x14 -> x0, starting transfers between devices: 14.5 us -> none  [the longest x7 11.2 us: ring_scatter(): high = lax.ppermute(high, 'dp', behind)]
    ppermute x26, waiting for transfers between devices: 83.6 us -> 95.9 us  [query_swap(): return lax.ppermute(value, 'query', [(i, i ^ bit) for i in range(n_query)])]
    ppermute x45 -> x46, starting transfers between devices: 23.3 us -> 15.4 us  [dp_swap(): return lax.ppermute(value, 'dp', [(i, i ^ bit) for i in range(n_dp)])]
    convert_element_type x7 -> x0, other arithmetic: 6.64 us -> none  [ring_scatter(): high = (high.astype(F32) + piece(1 + step, 1).astype(F32)).astype(BF16)]
    unnamed x262 -> x280, local copies, waits for them, and re-layouts: 39.8 us -> 40.5 us
  transfers between devices with their start and end apart: 105 -> 93, of which waited for: 52 -> 44; matrix products, arithmetic and copies ran while one was open for 42% -> 42% of each run, Pallas kernels for 7% -> 7%
where the time goes in v3:
time: 647 us; the launch traced here: 640 us
  waiting for transfers between devices  206 us (32%)
  other arithmetic  108 us (17%)
  matrix products  104 us (16%)
  local copies, waits for them, and re-layouts  94.6 us (15%)
  starting transfers between devices  63.8 us (10%)
  Pallas kernels  48.4 us (7%)
  between operations  16.3 us (3%)
    ppermute x26, waiting for transfers between devices, query_swap(): return lax.ppermute(value, 'query', [(i, i ^ bit) for i in range(n_query)])  95.9 us
    ppermute x46, waiting for transfers between devices, dp_swap(): return lax.ppermute(value, 'dp', [(i, i ^ bit) for i in range(n_dp)])  84.1 us
    dot_general x7, matrix products, product(): return jnp.dot(left, right, preferred_element_type=F32)  42.9 us
    unnamed x280, local copies, waits for them, and re-layouts  40.5 us
    dot_general x10, matrix products, row_product(): lax.dot_general(left, right, (((0,), (0,)), ((), ())), preferred_element_...  37.1 us
    ppermute x26, starting transfers between devices, query_swap(): return lax.ppermute(value, 'query', [(i, i ^ bit) for i in range(n_query)])  32.3 us
    dot_general x8, matrix products, times_transpose(): lax.dot_general(left, right, (((1,), (1,)), ((), ())), preferred_element_...  23.6 us
    ppermute x7, waiting for transfers between devices, ring_step(): held.append(lax.ppermute(low, 'dp', ahead))  16 us
  transfers between devices with their start and end apart: 93, of which 44 were waited for; matrix products, arithmetic and copies ran while one was open for 42% of the time, Pallas kernels for 7%

profile of v3, /device:TPU:0, one launch (start us, length us, event | category | flops | bytes accessed | tf_op | source)
XLA Modules:
  0.0 640.0 jit_solution(12662935820556374775)
XLA Ops:
  15.6 5.6 collective-permute-done.1.refs_2_
  22.6 5.5 collective-permute-done.3.refs_1_
  64.4 4.6 collective-permute-done.15.refs_2_
  74.9 4.3 collective-permute-done.16.refs_14_
  106.7 5.6 shard_map.265
  117.3 3.2 shard_map.266
  123.2 4.1 fusion.28.projected_ref
  128.0 4.7 shard_map.267
  140.0 3.6 fusion.137
  143.6 4.7 shard_map.268
  150.4 3.3 fusion.138
  173.5 7.4 %collective-permute-done.26 = bf16[1,128,1280]{2,1,0:T(8,128)(2,1)S(1)} collective-permute-done((bf16[1,128,1280]{2,1,0:T(8,128)(2,1)S(1)}, bf16[1,128,1280]{2,1,0:T(8,128)(2,1)S(1)}, u32[]{:S(2)}, u32[]{:S(2)}) %collective-permute-start.26) | collective-permute-done | bytes 327712 | tf_op jit(solution)/shard_map/ppermute | solution.py:522
  183.6 6.3 collective-permute-done.24
  195.7 3.1 shard_map.270
  203.9 5.8 collective-permute-done.27
  212.4 3.3 pad_maximum_fusion
  215.8 3.0 maximum_maximum_fusion
  218.8 10.3 %multiply_convert_fusion.1 = (bf16[1024,1280]{1,0:T(8,128)(2,1)}, f32[1024,1280]{1,0:T(8,128)}) fusion(f32[1280]{0:T(1024)S(1)} %copy-done.120, bf16[1024,1280]{1,0:T(8,128)(2,1)} %bitcast.486, bf16[1280,1280]{1,0:T(8,128)(2,1)} %all-gather.4.cloned.1.call-done), kind=kOutput, calls=%fused_computation.22 | convolution fusion | flops 3368550400 | bytes 13767680 | tf_op jit(solution)/shard_map/dot_general | solution.py:17
  229.1 8.6 %fusion.139 = f32[1024,1280]{1,0:T(8,128)} fusion(bf16[1024,1280]{1,0:T(8,128)(2,1)} %get-tuple-element.147, bf16[1280,1280]{1,0:T(8,128)(2,1)} %all-gather.6.cloned.1.call-done), kind=kOutput, calls=%fused_computation.397 | convolution fusion | flops 3355443200 | bytes 11141120 | tf_op jit(solution)/shard_map/dot_general | solution.py:17
  240.9 6.3 convolution_convert_fusion.1
  251.3 6.8 %convert_reduce_fusion.1 = (f32[1280]{0:T(1024)}, bf16[1024,1280]{1,0:T(8,128)(2,1)S(1)}) fusion(f32[1024,1280]{1,0:T(8,128)S(1)} %bitcast.502, bf16[1024,1280]{1,0:T(8,128)(2,1)S(1)} %bitcast.485, bf16[1280,1280]{1,0:T(8,128)(2,1)S(1)} %copy-done.65), kind=kOutput, calls=%fused_computation.21 | convolution fusion | flops 3384277760 | bytes 13767680 | tf_op jit(solution)/shard_map/dot_general | solution.py:25
  259.5 4.3 convolution_convert_fusion
  273.0 6.3 fusion.140
  297.2 18.4 %collective-permute-done.80 = bf16[4,24,1280]{2,1,0:T(8,128)(2,1)} collective-permute-done((bf16[4,24,1280]{2,1,0:T(8,128)(2,1)S(1)}, bf16[4,24,1280]{2,1,0:T(8,128)(2,1)}, u32[]{:S(2)}, u32[]{:S(2)}) %collective-permute-start.80) | collective-permute-done | bytes 245792 | tf_op jit(solution)/shard_map/ppermute | solution.py:516
  324.5 3.0 fusion.15
  327.8 10.6 %collective-permute-done.46 = bf16[2,128,1280]{2,1,0:T(8,128)(2,1)} collective-permute-done((bf16[2,128,1280]{2,1,0:T(8,128)(2,1)}, bf16[2,128,1280]{2,1,0:T(8,128)(2,1)}, u32[]{:S(2)}, u32[]{:S(2)}) %collective-permute-start.46) | collective-permute-done | bytes 655392 | tf_op jit(solution)/shard_map/ppermute | solution.py:522
  340.2 3.1 multiply_reduce_fusion.2
  349.4 10.5 %fusion.1 = f32[1984,1280]{1,0:T(8,128)S(1)} fusion(bf16[1984,1280]{1,0:T(8,128)(2,1)} %copy-done.1, f32[1280]{0:T(1024)S(1)} %copy-done.119, f32[2,2,1280]{2,1,0:T(2,128)S(1)} %copy.135, f32[2,2,1280]{2,1,0:T(2,128)S(1)} %copy.134, pred[1984]{0:T(1024)(128)(4,1)S(1)} %copy-done.127, bf16[1280,2560]{1,0:T(8,128)(2,1)} %all-gather.8.cloned.1.call-done), kind=kOutput, calls=%fused_computation.2 | convolution fusion | flops 6508789760 | bytes 18561984 | tf_op jit(solution)/shard_map/dot_general | solution.py:17
  360.0 3.8 copy-done.40
  366.7 3.6 fusion.12
  379.3 8.1 %convert_reduce_fusion = (f32[1280]{0:T(1024)S(1)}, bf16[1984,1280]{1,0:T(8,128)(2,1)S(1)}, f32[1280]{0:T(1024)S(1)}) fusion(f32[1984,1280]{1,0:T(8,128)} %copy-done.40, f32[1280]{0:T(1024)S(1)} %copy-done.96, f32[1984]{0:T(1024)S(1)} %mul.476), kind=kLoop, calls=%fused_computation.4 | loop fusion | flops 38090240 | bytes 15260416 | tf_op jit(solution)/shard_map/reduce_sum | solution.py:749
  399.6 11.7 %convolution_convert_fusion.2 = bf16[1280,1280]{1,0:T(8,128)(2,1)} fusion(bf16[1984,1280]{1,0:T(8,128)(2,1)} %copy-done.1, bf16[1984,1280]{1,0:T(8,128)(2,1)} %copy-done.42), kind=kOutput, calls=%fused_computation.11 | convolution fusion | flops 6502809600 | bytes 13434880 | tf_op jit(solution)/shard_map/dot_general | solution.py:21
  411.9 3.0 fusion.141
  429.1 3.0 pad_maximum_fusion.1
  442.9 10.1 %shard_map.275 = bf16[1024,960]{1,0:T(8,128)(2,1)} custom-call(bf16[1024,960]{1,0:T(8,128)(2,1)} %fusion.28.projected_ref, bf16[1024,320]{1,0:T(8,128)(2,1)} %convolution_convert_fusion.5.grad_mixed_ref, bf16[8,1,320]{2,1,0:T(2,128)(2,1)} %copy.152.first_ref), custom_call_target="tpu_custom_call" | custom-call | flops 419430400 | bytes 4915200 | tf_op jit(solution)/shard_map/pallas_call | solution.py:128
  458.3 5.9 convolution_convert_fusion.3
  464.3 3.1 copy.153.qkv_ref
  485.6 32.3 %collective-permute-done.69 = bf16[1,24,1280]{2,1,0:T(8,128)(2,1)S(1)} collective-permute-done((bf16[1,24,1280]{2,1,0:T(8,128)(2,1)S(1)}, bf16[1,24,1280]{2,1,0:T(8,128)(2,1)S(1)}, u32[]{:S(2)}, u32[]{:S(2)}) %collective-permute-start.69) | collective-permute-done | bytes 61472 | tf_op jit(solution)/shard_map/ppermute | solution.py:516
  518.0 3.5 fusion.128
  524.5 3.0 fusion.11
  531.8 10.5 %collective-permute-done.81 = bf16[4,24,1280]{2,1,0:T(8,128)(2,1)} collective-permute-done((bf16[4,24,1280]{2,1,0:T(8,128)(2,1)S(1)}, bf16[4,24,1280]{2,1,0:T(8,128)(2,1)}, u32[]{:S(2)}, u32[]{:S(2)}) %collective-permute-start.81) | collective-permute-done | bytes 245792 | tf_op jit(solution)/shard_map/ppermute | solution.py:516
  547.8 3.3 fusion.20
  555.7 5.4 collective-permute-done.71
  561.3 4.3 collective-permute-done.72
  565.8 3.6 collective-permute-done.73
  575.8 25.7 %collective-permute-done.83 = bf16[2,3,80,1280]{3,2,1,0:T(8,128)(2,1)S(1)} collective-permute-done((bf16[2,3,80,1280]{3,2,1,0:T(8,128)(2,1)S(1)}, bf16[2,3,80,1280]{3,2,1,0:T(8,128)(2,1)S(1)}, u32[]{:S(2)}, u32[]{:S(2)}) %collective-permute-start.83) | collective-permute-done | bytes 1228832 | tf_op jit(solution)/shard_map/ppermute | solution.py:522
  609.6 10.2 %collective-permute-done.85 = bf16[2,80,1280]{2,1,0:T(8,128)(2,1)S(1)} collective-permute-done((bf16[2,80,1280]{2,1,0:T(8,128)(2,1)S(1)}, bf16[2,80,1280]{2,1,0:T(8,128)(2,1)S(1)}, u32[]{:S(2)}, u32[]{:S(2)}) %collective-permute-start.85) | collective-permute-done | bytes 409632 | tf_op jit(solution)/shard_map/ppermute | solution.py:522
  621.7 9.3 %collective-permute-done.77 = bf16[2,80,1280]{2,1,0:T(8,128)(2,1)S(1)} collective-permute-done((bf16[2,80,1280]{2,1,0:T(8,128)(2,1)S(1)}, bf16[2,80,1280]{2,1,0:T(8,128)(2,1)S(1)}, u32[]{:S(2)}, u32[]{:S(2)}) %collective-permute-start.77) | collective-permute-done | bytes 409632 | tf_op jit(solution)/shard_map/ppermute | solution.py:522
  (702 shorter events, 293.9 us)
Async XLA Ops:
  7.2 211.6 %all-gather.4.cloned.1.call-start = ((), (), s32[]{:S(2)}) async-start(), calls=%async_computation.4 | async-start | bytes 3686400 | tf_op jit(solution)/shard_map/all_gather | solution.py:585
  10.0 18.1 %collective-permute-start.3 = (bf16[2,128,1280]{2,1,0:T(8,128)(2,1)}, bf16[2,128,1280]{2,1,0:T(8,128)(2,1)S(1)}, u32[]{:S(2)}, u32[]{:S(2)}) collective-permute-start(bf16[2,128,1280]{2,1,0:T(8,128)(2,1)} %bitcast.465), channel_id=1, source_target_pairs={{0,1},{1,0},{2,3},{3,2},{4,5},{5,4},{6,7},{7,6},{8,9},{9,8},{10,11... | collective-permute-start | bytes 1966088 | tf_op jit(solution)/shard_map/ppermute | solution.py:522
  31.5 17.9 %collective-permute-start.10 = (bf16[2,128,1280]{2,1,0:T(8,128)(2,1)}, bf16[2,128,1280]{2,1,0:T(8,128)(2,1)S(1)}, u32[]{:S(2)}, u32[]{:S(2)}) collective-permute-start(bf16[2,128,1280]{2,1,0:T(8,128)(2,1)} %bitcast.482), channel_id=1, source_target_pairs={{0,1},{1,0},{2,3},{3,2},{4,5},{5,4},{6,7},{7,6},{8,9},{9,8},{10,11... | collective-permute-start | bytes 1966088 | tf_op jit(solution)/shard_map/ppermute | solution.py:522
  41.2 27.8 %collective-permute-start.15 = (bf16[384,1280]{1,0:T(8,128)(2,1)S(1)}, bf16[384,1280]{1,0:T(8,128)(2,1)}, u32[]{:S(2)}, u32[]{:S(2)}) collective-permute-start(bf16[384,1280]{1,0:T(8,128)(2,1)S(1)} %get-tuple-element.133.refs_0_), channel_id=1, source_target_pairs={{0,1},{1,0},{2,3},{3,2},{4,5},{5,4},{6,7},{7,6},{8,9},{9,8},{10,11... | collective-permute-start | bytes 2949128 | tf_op jit(solution)/shard_map/ppermute | solution.py:522
  79.6 149.5 %all-gather.6.cloned.1.call-start = ((), (), s32[]{:S(2)}) async-start(), calls=%async_computation.5 | async-start | bytes 3686400 | tf_op jit(solution)/shard_map/all_gather | solution.py:585
  83.2 263.6 %all-gather.8.cloned.1.call-start = ((), (), s32[]{:S(2)}) async-start(), calls=%async_computation.6 | async-start | bytes 7372800 | tf_op jit(solution)/shard_map/all_gather | solution.py:585
  83.4 33.9 %collective-permute-start.18 = (bf16[2,128,1280]{2,1,0:T(8,128)(2,1)S(1)}, bf16[2,128,1280]{2,1,0:T(8,128)(2,1)}, u32[]{:S(2)}, u32[]{:S(2)}) collective-permute-start(bf16[2,128,1280]{2,1,0:T(8,128)(2,1)S(1)} %bitcast.466), channel_id=1, source_target_pairs={{0,2},{2,0},{4,6},{6,4},{8,10},{10,8},{12,14},{14,12},{16,18},{18,... | collective-permute-start | bytes 1966088 | tf_op jit(solution)/shard_map/ppermute | solution.py:516
  95.8 32.2 %collective-permute-start.20 = (bf16[384,1280]{1,0:T(8,128)(2,1)S(1)}, bf16[384,1280]{1,0:T(8,128)(2,1)}, u32[]{:S(2)}, u32[]{:S(2)}) collective-permute-start(bf16[384,1280]{1,0:T(8,128)(2,1)S(1)} %get-tuple-element.134.refs_1_), channel_id=1, source_target_pairs={{0,1},{1,0},{2,3},{3,2},{4,5},{5,4},{6,7},{7,6},{8,9},{9,8},{10,11... | collective-permute-start | bytes 2949128 | tf_op jit(solution)/shard_map/ppermute | solution.py:522
  97.3 20.0 %collective-permute-start.19 = (bf16[2,128,1280]{2,1,0:T(8,128)(2,1)}, bf16[2,128,1280]{2,1,0:T(8,128)(2,1)}, u32[]{:S(2)}, u32[]{:S(2)}) collective-permute-start(bf16[2,128,1280]{2,1,0:T(8,128)(2,1)} %copy-done.9), channel_id=1, source_target_pairs={{0,2},{2,0},{4,6},{6,4},{8,10},{10,8},{12,14},{14,12},{16,18},{18,... | collective-permute-start | bytes 1966088 | tf_op jit(solution)/shard_map/ppermute | solution.py:516
  122.7 13.5 %collective-permute-start.22 = (bf16[2,320,320]{2,1,0:T(8,128)(2,1)}, bf16[2,320,320]{2,1,0:T(8,128)(2,1)}, u32[]{:S(2)}, u32[]{:S(2)}) collective-permute-start(bf16[2,320,320]{2,1,0:T(8,128)(2,1)} %pad_maximum_fusion.12), channel_id=1, source_target_pairs={{0,1},{1,0},{2,3},{3,2},{4,5},{5,4},{6,7},{7,6},{8,9},{9,8},{10,11... | collective-permute-start | bytes 1228808 | tf_op jit(solution)/shard_map/ppermute | solution.py:522
  135.2 412.5 %reduce-scatter.7.cloned.1.call-start = ((), (), s32[]{:S(2)}) async-start(), calls=%async_computation.8 | async-start | bytes 2048000 | tf_op jit(solution)/shard_map/reduce_scatter | solution.py:601
  158.2 13.0 %collective-permute-start.23 = (bf16[1,2,128,1280]{3,2,1,0:T(8,128)(2,1)}, bf16[1,2,128,1280]{3,2,1,0:T(8,128)(2,1)}, u32[]{:S(2)}, u32[]{:S(2)}) collective-permute-start(bf16[1,2,128,1280]{3,2,1,0:T(8,128)(2,1)} %slice.1067), channel_id=1, source_target_pairs={{0,2},{2,0},{4,6},{6,4},{8,10},{10,8},{12,14},{14,12},{16,18},{18,... | collective-permute-start | bytes 1966088 | tf_op jit(solution)/shard_map/ppermute | solution.py:516
  160.9 31.5 %collective-permute-start.34 = (bf16[384,1280]{1,0:T(8,128)(2,1)S(1)}, bf16[384,1280]{1,0:T(8,128)(2,1)}, u32[]{:S(2)}, u32[]{:S(2)}) collective-permute-start(bf16[384,1280]{1,0:T(8,128)(2,1)S(1)} %get-tuple-element.133.refs_0_), channel_id=1, source_target_pairs={{0,2},{2,0},{4,6},{6,4},{8,10},{10,8},{12,14},{14,12},{16,18},{18,... | collective-permute-start | bytes 2949128 | tf_op jit(solution)/shard_map/ppermute | solution.py:516
  163.4 31.0 %collective-permute-start.35 = (bf16[384,1280]{1,0:T(8,128)(2,1)S(1)}, bf16[384,1280]{1,0:T(8,128)(2,1)}, u32[]{:S(2)}, u32[]{:S(2)}) collective-permute-start(bf16[384,1280]{1,0:T(8,128)(2,1)S(1)} %get-tuple-element.134.refs_1_), channel_id=1, source_target_pairs={{0,2},{2,0},{4,6},{6,4},{8,10},{10,8},{12,14},{14,12},{16,18},{18,... | collective-permute-start | bytes 2949128 | tf_op jit(solution)/shard_map/ppermute | solution.py:516
  164.1 31.5 %collective-permute-start.36 = (bf16[384,1280]{1,0:T(8,128)(2,1)}, bf16[384,1280]{1,0:T(8,128)(2,1)}, u32[]{:S(2)}, u32[]{:S(2)}) collective-permute-start(bf16[384,1280]{1,0:T(8,128)(2,1)} %collective-permute-done.15.refs_2_), channel_id=1, source_target_pairs={{0,2},{2,0},{4,6},{6,4},{8,10},{10,8},{12,14},{14,12},{16,18},{18,... | collective-permute-start | bytes 2949128 | tf_op jit(solution)/shard_map/ppermute | solution.py:516
  169.3 26.3 %collective-permute-start.37 = (bf16[384,1280]{1,0:T(8,128)(2,1)}, bf16[384,1280]{1,0:T(8,128)(2,1)S(1)}, u32[]{:S(2)}, u32[]{:S(2)}) collective-permute-start(bf16[384,1280]{1,0:T(8,128)(2,1)} %collective-permute-done.20.refs_3_), channel_id=1, source_target_pairs={{0,2},{2,0},{4,6},{6,4},{8,10},{10,8},{12,14},{14,12},{16,18},{18,... | collective-permute-start | bytes 2949128 | tf_op jit(solution)/shard_map/ppermute | solution.py:516
  171.2 9.8 %collective-permute-start.26 = (bf16[1,128,1280]{2,1,0:T(8,128)(2,1)S(1)}, bf16[1,128,1280]{2,1,0:T(8,128)(2,1)S(1)}, u32[]{:S(2)}, u32[]{:S(2)}) collective-permute-start(bf16[1,128,1280]{2,1,0:T(8,128)(2,1)S(1)} %fusion.62), channel_id=1, source_target_pairs={{0,1},{1,0},{2,3},{3,2},{4,5},{5,4},{6,7},{7,6},{8,9},{9,8},{10,11... | collective-permute-start | bytes 983048 | tf_op jit(solution)/shard_map/ppermute | solution.py:522
  189.9 22.5 %collective-permute-start.44 = (bf16[2,2,128,1280]{3,2,1,0:T(8,128)(2,1)}, bf16[2,2,128,1280]{3,2,1,0:T(8,128)(2,1)}, u32[]{:S(2)}, u32[]{:S(2)}) collective-permute-start(bf16[2,2,128,1280]{3,2,1,0:T(8,128)(2,1)} %pad_maximum_fusion.3), channel_id=1, source_target_pairs={{0,2},{2,0},{4,6},{6,4},{8,10},{10,8},{12,14},{14,12},{16,18},{18,... | collective-permute-start | bytes 3932168 | tf_op jit(solution)/shard_map/ppermute | solution.py:516
  192.4 10.6 %collective-permute-start.29 = (bf16[1,128,1280]{2,1,0:T(8,128)(2,1)S(1)}, bf16[1,128,1280]{2,1,0:T(8,128)(2,1)S(1)}, u32[]{:S(2)}, u32[]{:S(2)}) collective-permute-start(bf16[1,128,1280]{2,1,0:T(8,128)(2,1)S(1)} %fusion.68), channel_id=1, source_target_pairs={{0,1},{1,0},{2,3},{3,2},{4,5},{5,4},{6,7},{7,6},{8,9},{9,8},{10,11... | collective-permute-start | bytes 983048 | tf_op jit(solution)/shard_map/ppermute | solution.py:522
  194.4 15.2 %collective-permute-start.27 = (bf16[1,128,1280]{2,1,0:T(8,128)(2,1)S(1)}, bf16[1,128,1280]{2,1,0:T(8,128)(2,1)S(1)}, u32[]{:S(2)}, u32[]{:S(2)}) collective-permute-start(bf16[1,128,1280]{2,1,0:T(8,128)(2,1)S(1)} %get-tuple-element.333), channel_id=1, source_target_pairs={{0,1},{1,0},{2,3},{3,2},{4,5},{5,4},{6,7},{7,6},{8,9},{9,8},{10,11... | collective-permute-start | bytes 983048 | tf_op jit(solution)/shard_map/ppermute | solution.py:522
  203.9 11.9 %collective-permute-start.30 = (bf16[1,2,128,1280]{3,2,1,0:T(8,128)(2,1)}, bf16[1,2,128,1280]{3,2,1,0:T(8,128)(2,1)}, u32[]{:S(2)}, u32[]{:S(2)}) collective-permute-start(bf16[1,2,128,1280]{3,2,1,0:T(8,128)(2,1)} %pad_maximum_fusion.10), channel_id=1, source_target_pairs={{0,2},{2,0},{4,6},{6,4},{8,10},{10,8},{12,14},{14,12},{16,18},{18,... | collective-permute-start | bytes 1966088 | tf_op jit(solution)/shard_map/ppermute | solution.py:516
  240.3 17.8 %collective-permute-start.42 = (bf16[2,2,1,1280]{3,0,2,1:T(2,128)(2,1)S(1)}, bf16[2,2,1,1280]{3,0,2,1:T(2,128)(2,1)S(1)}, u32[]{:S(2)}, u32[]{:S(2)}) collective-permute-start(bf16[2,2,1,1280]{3,0,2,1:T(2,128)(2,1)S(1)} %copy.300), channel_id=1, source_target_pairs={{0,2},{2,0},{4,6},{6,4},{8,10},{10,8},{12,14},{14,12},{16,18},{18,... | collective-permute-start | bytes 30728 | tf_op jit(solution)/shard_map/ppermute | solution.py:516
  271.6 9.0 %collective-permute-start.78 = (bf16[1,24,1280]{2,1,0:T(8,128)(2,1)S(1)}, bf16[1,24,1280]{2,1,0:T(8,128)(2,1)S(1)}, u32[]{:S(2)}, u32[]{:S(2)}) collective-permute-start(bf16[1,24,1280]{2,1,0:T(8,128)(2,1)S(1)} %maximum_bitcast_fusion.1), channel_id=1, source_target_pairs={{0,4},{2,6},{4,0},{6,2},{8,12},{10,14},{12,8},{14,10},{16,20},{18,... | collective-permute-start | bytes 184328 | tf_op jit(solution)/shard_map/ppermute | solution.py:516
  280.6 37.3 %collective-permute-start.45 = (bf16[2,2,128,1280]{3,2,0,1:T(8,128)(2,1)}, bf16[2,2,128,1280]{3,2,0,1:T(8,128)(2,1)}, u32[]{:S(2)}, u32[]{:S(2)}) collective-permute-start(bf16[2,2,128,1280]{3,2,0,1:T(8,128)(2,1)} %copy.297), channel_id=1, source_target_pairs={{0,2},{2,0},{4,6},{6,4},{8,10},{10,8},{12,14},{14,12},{16,18},{18,... | collective-permute-start | bytes 3932168 | tf_op jit(solution)/shard_map/ppermute | solution.py:516
  283.2 41.3 %collective-permute-start.47 = (bf16[640,1280]{1,0:T(8,128)(2,1)}, bf16[640,1280]{1,0:T(8,128)(2,1)}, u32[]{:S(2)}, u32[]{:S(2)}) collective-permute-start(bf16[640,1280]{1,0:T(8,128)(2,1)} %bitcast.53), channel_id=1, source_target_pairs={{0,4},{2,6},{4,0},{6,2},{8,12},{10,14},{12,8},{14,10},{16,20},{18,... | collective-permute-start | bytes 4915208 | tf_op jit(solution)/shard_map/ppermute | solution.py:516
  285.3 36.8 %collective-permute-start.40 = (bf16[2,2,128,1280]{3,2,0,1:T(8,128)(2,1)}, bf16[2,2,128,1280]{3,2,0,1:T(8,128)(2,1)}, u32[]{:S(2)}, u32[]{:S(2)}) collective-permute-start(bf16[2,2,128,1280]{3,2,0,1:T(8,128)(2,1)} %copy.298), channel_id=1, source_target_pairs={{0,2},{2,0},{4,6},{6,4},{8,10},{10,8},{12,14},{14,12},{16,18},{18,... | collective-permute-start | bytes 3932168 | tf_op jit(solution)/shard_map/ppermute | solution.py:516
  288.0 27.6 %collective-permute-start.80 = (bf16[4,24,1280]{2,1,0:T(8,128)(2,1)S(1)}, bf16[4,24,1280]{2,1,0:T(8,128)(2,1)}, u32[]{:S(2)}, u32[]{:S(2)}) collective-permute-start(bf16[4,24,1280]{2,1,0:T(8,128)(2,1)S(1)} %pad_maximum_fusion.20), channel_id=1, source_target_pairs={{0,16},{2,18},{4,20},{6,22},{8,24},{10,26},{12,28},{14,30},{16,0},... | collective-permute-start | bytes 737288 | tf_op jit(solution)/shard_map/ppermute | solution.py:516
  292.1 74.5 %collective-permute-start.51 = (bf16[640,1280]{1,0:T(8,128)(2,1)}, bf16[640,1280]{1,0:T(8,128)(2,1)}, u32[]{:S(2)}, u32[]{:S(2)}) collective-permute-start(bf16[640,1280]{1,0:T(8,128)(2,1)} %bitcast.55), channel_id=1, source_target_pairs={{0,4},{2,6},{4,0},{6,2},{8,12},{10,14},{12,8},{14,10},{16,20},{18,... | collective-permute-start | bytes 4915208 | tf_op jit(solution)/shard_map/ppermute | solution.py:516
  320.4 17.9 %collective-permute-start.46 = (bf16[2,128,1280]{2,1,0:T(8,128)(2,1)}, bf16[2,128,1280]{2,1,0:T(8,128)(2,1)}, u32[]{:S(2)}, u32[]{:S(2)}) collective-permute-start(bf16[2,128,1280]{2,1,0:T(8,128)(2,1)} %fusion.48), channel_id=1, source_target_pairs={{0,1},{1,0},{2,3},{3,2},{4,5},{5,4},{6,7},{7,6},{8,9},{9,8},{10,11... | collective-permute-start | bytes 1966088 | tf_op jit(solution)/shard_map/ppermute | solution.py:522
  324.2 49.5 %collective-permute-start.41 = (bf16[2,128,1280]{2,1,0:T(8,128)(2,1)}, bf16[2,128,1280]{2,1,0:T(8,128)(2,1)}, u32[]{:S(2)}, u32[]{:S(2)}) collective-permute-start(bf16[2,128,1280]{2,1,0:T(8,128)(2,1)} %fusion.47), channel_id=1, source_target_pairs={{0,1},{1,0},{2,3},{3,2},{4,5},{5,4},{6,7},{7,6},{8,9},{9,8},{10,11... | collective-permute-start | bytes 1966088 | tf_op jit(solution)/shard_map/ppermute | solution.py:522
  327.5 220.2 %reduce-scatter.9.cloned.1.call-start = ((), (), s32[]{:S(2)}) async-start(), calls=%async_computation.9 | async-start | bytes 2048000 | tf_op jit(solution)/shard_map/reduce_scatter | solution.py:601
  345.1 33.8 %collective-permute-start.60 = (bf16[2,128,1280]{2,1,0:T(8,128)(2,1)}, bf16[2,128,1280]{2,1,0:T(8,128)(2,1)}, u32[]{:S(2)}, u32[]{:S(2)}) collective-permute-start(bf16[2,128,1280]{2,1,0:T(8,128)(2,1)} %bitcast.65), channel_id=1, source_target_pairs={{0,1},{1,0},{2,3},{3,2},{4,5},{5,4},{6,7},{7,6},{8,9},{9,8},{10,11... | collective-permute-start | bytes 1966088 | tf_op jit(solution)/shard_map/ppermute | solution.py:522
  378.9 226.5 %reduce-scatter.11.cloned.1.call-start = ((), (), s32[]{:S(2)}) async-start(), calls=%async_computation.10 | async-start | bytes 3686400 | tf_op jit(solution)/shard_map/reduce_scatter | solution.py:588
  391.4 37.6 %collective-permute-start.61 = (bf16[2,2,128,1280]{3,2,1,0:T(8,128)(2,1)S(1)}, bf16[2,2,128,1280]{3,2,1,0:T(8,128)(2,1)S(1)}, u32[]{:S(2)}, u32[]{:S(2)}) collective-permute-start(bf16[2,2,128,1280]{3,2,1,0:T(8,128)(2,1)S(1)} %pad_maximum_fusion.5), channel_id=1, source_target_pairs={{0,2},{2,0},{4,6},{6,4},{8,10},{10,8},{12,14},{14,12},{16,18},{18,... | collective-permute-start | bytes 3932168 | tf_op jit(solution)/shard_map/ppermute | solution.py:516
  399.6 12.3 %collective-permute-start.57 = (bf16[2,2,1,1280]{3,0,2,1:T(2,128)(2,1)S(1)}, bf16[2,2,1,1280]{3,0,2,1:T(2,128)(2,1)S(1)}, u32[]{:S(2)}, u32[]{:S(2)}) collective-permute-start(bf16[2,2,1,1280]{3,0,2,1:T(2,128)(2,1)S(1)} %pad_maximum_fusion.28), channel_id=1, source_target_pairs={{0,2},{2,0},{4,6},{6,4},{8,10},{10,8},{12,14},{14,12},{16,18},{18,... | collective-permute-start | bytes 30728 | tf_op jit(solution)/shard_map/ppermute | solution.py:516
  411.4 197.1 %reduce-scatter.5.cloned.1.call-start = ((), (), s32[]{:S(2)}) async-start(), calls=%async_computation.7 | async-start | bytes 2048000 | tf_op jit(solution)/shard_map/reduce_scatter | solution.py:601
  439.1 14.0 %collective-permute-start.64 = (bf16[2,320,320]{2,1,0:T(8,128)(2,1)}, bf16[2,320,320]{2,1,0:T(8,128)(2,1)}, u32[]{:S(2)}, u32[]{:S(2)}) collective-permute-start(bf16[2,320,320]{2,1,0:T(8,128)(2,1)} %pad_maximum_fusion.13), channel_id=1, source_target_pairs={{0,2},{2,0},{4,6},{6,4},{8,10},{10,8},{12,14},{14,12},{16,18},{18,... | collective-permute-start | bytes 1228808 | tf_op jit(solution)/shard_map/ppermute | solution.py:516
  456.7 13.5 %collective-permute-start.65 = (bf16[2,320,320]{2,1,0:T(8,128)(2,1)}, bf16[2,320,320]{2,1,0:T(8,128)(2,1)}, u32[]{:S(2)}, u32[]{:S(2)}) collective-permute-start(bf16[2,320,320]{2,1,0:T(8,128)(2,1)} %pad_maximum_fusion.14), channel_id=1, source_target_pairs={{0,1},{1,0},{2,3},{3,2},{4,5},{5,4},{6,7},{7,6},{8,9},{9,8},{10,11... | collective-permute-start | bytes 1228808 | tf_op jit(solution)/shard_map/ppermute | solution.py:522
  475.2 49.3 %collective-permute-start.68 = (bf16[640,1280]{1,0:T(8,128)(2,1)}, bf16[640,1280]{1,0:T(8,128)(2,1)}, u32[]{:S(2)}, u32[]{:S(2)}) collective-permute-start(bf16[640,1280]{1,0:T(8,128)(2,1)} %bitcast.110), channel_id=1, source_target_pairs={{0,4},{2,6},{4,0},{6,2},{8,12},{10,14},{12,8},{14,10},{16,20},{18,... | collective-permute-start | bytes 4915208 | tf_op jit(solution)/shard_map/ppermute | solution.py:516
  482.3 40.7 %collective-permute-start.66 = (bf16[2,2,128,1280]{3,2,0,1:T(8,128)(2,1)S(1)}, bf16[2,2,128,1280]{3,2,0,1:T(8,128)(2,1)}, u32[]{:S(2)}, u32[]{:S(2)}) collective-permute-start(bf16[2,2,128,1280]{3,2,0,1:T(8,128)(2,1)S(1)} %copy.296), channel_id=1, source_target_pairs={{0,2},{2,0},{4,6},{6,4},{8,10},{10,8},{12,14},{14,12},{16,18},{18,... | collective-permute-start | bytes 3932168 | tf_op jit(solution)/shard_map/ppermute | solution.py:516
  482.3 35.6 %collective-permute-start.69 = (bf16[1,24,1280]{2,1,0:T(8,128)(2,1)S(1)}, bf16[1,24,1280]{2,1,0:T(8,128)(2,1)S(1)}, u32[]{:S(2)}, u32[]{:S(2)}) collective-permute-start(bf16[1,24,1280]{2,1,0:T(8,128)(2,1)S(1)} %copy-done.86), channel_id=1, source_target_pairs={{0,4},{2,6},{4,0},{6,2},{8,12},{10,14},{12,8},{14,10},{16,20},{18,... | collective-permute-start | bytes 184328 | tf_op jit(solution)/shard_map/ppermute | solution.py:516
  527.5 14.8 %collective-permute-start.81 = (bf16[4,24,1280]{2,1,0:T(8,128)(2,1)S(1)}, bf16[4,24,1280]{2,1,0:T(8,128)(2,1)}, u32[]{:S(2)}, u32[]{:S(2)}) collective-permute-start(bf16[4,24,1280]{2,1,0:T(8,128)(2,1)S(1)} %pad_maximum_fusion.19), channel_id=1, source_target_pairs={{0,16},{2,18},{4,20},{6,22},{8,24},{10,26},{12,28},{14,30},{16,0},... | collective-permute-start | bytes 737288 | tf_op jit(solution)/shard_map/ppermute | solution.py:516
  530.2 20.9 %collective-permute-start.67 = (bf16[2,128,1280]{2,1,0:T(8,128)(2,1)}, bf16[2,128,1280]{2,1,0:T(8,128)(2,1)}, u32[]{:S(2)}, u32[]{:S(2)}) collective-permute-start(bf16[2,128,1280]{2,1,0:T(8,128)(2,1)} %fusion.49), channel_id=1, source_target_pairs={{0,1},{1,0},{2,3},{3,2},{4,5},{5,4},{6,7},{7,6},{8,9},{9,8},{10,11... | collective-permute-start | bytes 1966088 | tf_op jit(solution)/shard_map/ppermute | solution.py:522
  561.2 11.3 %collective-permute-start.82 = (bf16[3,80,1280]{2,1,0:T(8,128)(2,1)S(1)}, bf16[3,80,1280]{2,1,0:T(8,128)(2,1)S(1)}, u32[]{:S(2)}, u32[]{:S(2)}) collective-permute-start(bf16[3,80,1280]{2,1,0:T(8,128)(2,1)S(1)} %get-tuple-element.288), channel_id=1, source_target_pairs={{0,2},{2,0},{4,6},{6,4},{8,10},{10,8},{12,14},{14,12},{16,18},{18,... | collective-permute-start | bytes 1843208 | tf_op jit(solution)/shard_map/ppermute | solution.py:516
  572.6 28.9 %collective-permute-start.83 = (bf16[2,3,80,1280]{3,2,1,0:T(8,128)(2,1)S(1)}, bf16[2,3,80,1280]{3,2,1,0:T(8,128)(2,1)S(1)}, u32[]{:S(2)}, u32[]{:S(2)}) collective-permute-start(bf16[2,3,80,1280]{3,2,1,0:T(8,128)(2,1)S(1)} %pad_maximum_fusion.6), channel_id=1, source_target_pairs={{0,1},{1,0},{2,3},{3,2},{4,5},{5,4},{6,7},{7,6},{8,9},{9,8},{10,11... | collective-permute-start | bytes 3686408 | tf_op jit(solution)/shard_map/ppermute | solution.py:522
  608.0 11.8 %collective-permute-start.85 = (bf16[2,80,1280]{2,1,0:T(8,128)(2,1)S(1)}, bf16[2,80,1280]{2,1,0:T(8,128)(2,1)S(1)}, u32[]{:S(2)}, u32[]{:S(2)}) collective-permute-start(bf16[2,80,1280]{2,1,0:T(8,128)(2,1)S(1)} %pad_maximum_fusion.18), channel_id=1, source_target_pairs={{0,1},{1,0},{2,3},{3,2},{4,5},{5,4},{6,7},{7,6},{8,9},{9,8},{10,11... | collective-permute-start | bytes 1228808 | tf_op jit(solution)/shard_map/ppermute | solution.py:522
  609.5 10.4 %collective-permute-start.76 = (bf16[80,1280]{1,0:T(8,128)(2,1)S(1)}, bf16[80,1280]{1,0:T(8,128)(2,1)S(1)}, u32[]{:S(2)}, u32[]{:S(2)}) collective-permute-start(bf16[80,1280]{1,0:T(8,128)(2,1)S(1)} %get-tuple-element.312), channel_id=1, source_target_pairs={{0,2},{2,0},{4,6},{6,4},{8,10},{10,8},{12,14},{14,12},{16,18},{18,... | collective-permute-start | bytes 614408 | tf_op jit(solution)/shard_map/ppermute | solution.py:516
  619.9 11.0 %collective-permute-start.77 = (bf16[2,80,1280]{2,1,0:T(8,128)(2,1)S(1)}, bf16[2,80,1280]{2,1,0:T(8,128)(2,1)S(1)}, u32[]{:S(2)}, u32[]{:S(2)}) collective-permute-start(bf16[2,80,1280]{2,1,0:T(8,128)(2,1)S(1)} %pad_maximum_fusion.17), channel_id=1, source_target_pairs={{0,1},{1,0},{2,3},{3,2},{4,5},{5,4},{6,7},{7,6},{8,9},{9,8},{10,11... | collective-permute-start | bytes 1228808 | tf_op jit(solution)/shard_map/ppermute | solution.py:522
  (180 other events, 1045.9 us)
Sparse Core Ops, SparseCore 0:
  79.7 60.0 all-gather.3
  141.9 60.6 all-gather.5
  205.4 113.7 all-gather.7
  327.7 34.5 reduce-scatter.6
  379.0 34.6 reduce-scatter.8
  417.2 78.9 reduce-scatter.10
  531.9 36.5 reduce-scatter.4
